TPU v7x, 32 devices: a whole 2x2x4 slice. The times are simulated.
32 devices in a mesh: bx: 8 (over z, x), by: 4 (over y, core).
Axes of the slice: x: 2, y: 2, z: 4, core: 2. Of those that a mesh axis runs over, the one named last changes fastest.
Arguments:
- thermal_anomaly: float32 [8, 256, 1024], P(None, 'bx', 'by'), may hold values from -6 to 6
- saltiness_anomaly: float32 [8, 256, 1024], P(None, 'bx', 'by'), may hold values from -6 to 6
- speed_across_first_face: float32 [8, 256, 1024], P(None, 'bx', 'by'), may hold values from -4 to 4
- speed_across_second_face: float32 [8, 256, 1024], P(None, 'bx', 'by'), may hold values from -4 to 4
- isoline_incline_first: float32 [8, 256, 1024], P(None, 'bx', 'by'), may hold values from -0.6 to 0.6
- isoline_incline_second: float32 [8, 256, 1024], P(None, 'bx', 'by'), may hold values from -0.6 to 0.6
- top_boundary_source: float32 [2, 256, 1024], P(None, 'bx', 'by'), may hold values from -6 to 6
- wet_layer_number: int32 [256, 1024], P('bx', 'by'), may hold values from 0 to 8, as said below
- operator_main_entry: float32 [256, 1024], P(('bx', 'by')), may hold values from 0.05 to 1
Outputs:
- temperature_new: float32 [8, 256, 1024], P(None, 'bx', 'by')
- salinity_new: float32 [8, 256, 1024], P(None, 'bx', 'by')
- surface_pressure: float32 [256, 1024], P(('bx', 'by'))
Inputs may be any that keep to these rules, and one draw needn't show every extreme that they name: wet_layer_number is 0 on every column of a land block (aligned blocks of 64 x 64 columns); other columns hold any count.
All inputs are finite; a program needn't handle non-finite values.
Results may differ from a plain program's by a relative error of at most 0.0003.
Values sent between devices are 32-bit elements; how exact they have to be, the bound alone decides.
No kernel may reach another device: no remote copies, remote signals or barrier semaphores. Data moves between devices by JAX's collectives and lax.ppermute only.
A program may use at most 64 MiB of HBM per device.

v0:
```python
import math

import jax
import jax.numpy as jnp
from jax import lax
from jax.sharding import PartitionSpec as P

ITERS = 3


def with_halo(cells, sides, width):
    for axis, dim in sides:
        count = lax.axis_size(axis)
        ends = count - 1
        head = lax.slice_in_dim(cells, 0, width, axis=dim)
        tail = lax.slice_in_dim(cells, cells.shape[dim] - width, cells.shape[dim], axis=dim)
        cells = jnp.concatenate(
            [
                lax.ppermute(tail, axis, [(i, (i + 1) % count) for i in range(ends)]),
                cells,
                lax.ppermute(head, axis, [((i + 1) % count, i) for i in range(ends)]),
            ],
            axis=dim,
        )
    return cells


def tendency(cp, up, vp, sxp, syp, wetp):
    cp = cp * wetp
    mask_x = wetp[:, :-1, 1:-1] * wetp[:, 1:, 1:-1]
    left = cp[:, :, :-1, 1:-1]
    right = cp[:, :, 1:, 1:-1]
    cross_x = 0.25 * (
        cp[:, :, :-1, 2:] - cp[:, :, :-1, :-2] + (cp[:, :, 1:, 2:] - cp[:, :, 1:, :-2])
    )
    flux_x = mask_x * (
        up[:, :-1, 1:-1] * 0.5 * (left + right)
        - 0.15 * (right - left + sxp[:, :-1, 1:-1] * cross_x)
    )
    mask_y = wetp[:, 1:-1, :-1] * wetp[:, 1:-1, 1:]
    lower = cp[:, :, 1:-1, :-1]
    upper = cp[:, :, 1:-1, 1:]
    cross_y = 0.25 * (
        cp[:, :, 2:, :-1] - cp[:, :, :-2, :-1] + (cp[:, :, 2:, 1:] - cp[:, :, :-2, 1:])
    )
    flux_y = mask_y * (
        vp[:, 1:-1, :-1] * 0.5 * (lower + upper)
        - 0.15 * (upper - lower + syp[:, 1:-1, :-1] * cross_y)
    )
    wet_in = wetp[:, 1:-1, 1:-1]
    return wet_in * (
        -(flux_x[:, :, 1:] - flux_x[:, :, :-1]) - (flux_y[:, :, :, 1:] - flux_y[:, :, :, :-1])
    )


def column_step(carried_quantities, tend, wet, top_boundary_source):
    layer_tally = wet.shape[0]
    star = (carried_quantities + tend) * wet
    star = star.at[:, 0].add(top_boundary_source * wet[0])
    density = -0.2 * star[0] + 0.8 * star[1]
    strat = density[1:] - density[:-1]
    couple = (0.05 + 1.0 / (1.0 + 10.0 * jnp.maximum(strat, 0.0))) * wet[:-1] * wet[1:]
    zero_plane = jnp.zeros_like(wet[:1])
    above = jnp.concatenate([zero_plane, couple], 0)
    below = jnp.concatenate([couple, zero_plane], 0)
    diag = 1.0 + above + below
    primes = []
    rights = []
    for level in range(layer_tally):
        if level == 0:
            pivot = diag[0]
            rhs = star[:, 0]
        else:
            pivot = diag[level] - above[level] * primes[-1]
            rhs = star[:, level] + above[level] * rights[-1]
        primes.append(-below[level] / pivot * -1.0)
        rights.append(rhs / pivot)
    solved = [None] * layer_tally
    solved[layer_tally - 1] = rights[layer_tally - 1]
    for level in range(layer_tally - 2, -1, -1):
        solved[level] = rights[level] + primes[level] * solved[level + 1]
    fresh = jnp.stack(solved, 1) * wet
    density_new = -0.2 * fresh[0] + 0.8 * fresh[1]
    forcing = 4.0 / math.sqrt(layer_tally) * jnp.sum(wet * density_new, 0)
    return (fresh, forcing)


def nine_point(padded, operator_main_entry):
    centre = padded[1:-1, 1:-1]
    edges = padded[:-2, 1:-1] + padded[2:, 1:-1] + padded[1:-1, :-2] + padded[1:-1, 2:]
    corners = padded[:-2, :-2] + padded[:-2, 2:] + padded[2:, :-2] + padded[2:, 2:]
    return (6.0 + operator_main_entry) * centre - edges - 0.5 * corners


def local(
    thermal_anomaly,
    saltiness_anomaly,
    speed_across_first_face,
    speed_across_second_face,
    isoline_incline_first,
    isoline_incline_second,
    top_boundary_source,
    wet_layer_number,
    operator_main_entry,
):
    layer_tally, strip_accumulated, vertical_integral = thermal_anomaly.shape
    bottom_level_map = wet_layer_number.astype(jnp.float32)[None]
    planes = jnp.concatenate(
        [
            thermal_anomaly,
            saltiness_anomaly,
            speed_across_first_face,
            speed_across_second_face,
            isoline_incline_first,
            isoline_incline_second,
            bottom_level_map,
        ],
        0,
    )
    padded = with_halo(planes, (("bx", 1), ("by", 2)), 1)
    tracers_p = padded[: 2 * layer_tally].reshape(
        2, layer_tally, strip_accumulated + 2, vertical_integral + 2
    )
    east_p = padded[2 * layer_tally : 3 * layer_tally]
    north_p = padded[3 * layer_tally : 4 * layer_tally]
    slope_ep = padded[4 * layer_tally : 5 * layer_tally]
    slope_np = padded[5 * layer_tally : 6 * layer_tally]
    depth_p = padded[6 * layer_tally]
    level_ids = jnp.arange(layer_tally, dtype=jnp.float32)[:, None, None]
    wet_p = (level_ids < depth_p[None]).astype(jnp.float32)
    tend = tendency(tracers_p, east_p, north_p, slope_ep, slope_np, wet_p)
    wet = wet_p[:, 1:-1, 1:-1]
    carried_quantities = jnp.stack([thermal_anomaly, saltiness_anomaly], 0)
    fresh, forcing = column_step(carried_quantities, tend, wet, top_boundary_source)
    slab = lax.all_to_all(forcing, "by", split_axis=0, concat_axis=1, tiled=True)
    solution = jnp.zeros_like(slab)
    resid = slab

    def inner(left_field, right_field):
        return lax.psum(jnp.sum(left_field * right_field), ("bx", "by"))

    direction = slab
    norm_now = inner(resid, resid)
    for step in range(ITERS):
        rows_p = with_halo(direction, ((("bx", "by"), 0),), 1)
        image = nine_point(jnp.pad(rows_p, ((0, 0), (1, 1))), operator_main_entry)
        alpha = norm_now / inner(direction, image)
        solution = solution + alpha * direction
        resid = resid - alpha * image
        if step + 1 < ITERS:
            norm_next = inner(resid, resid)
            direction = resid + norm_next / norm_now * direction
            norm_now = norm_next
    return (fresh[0], fresh[1], solution)


def solution(mesh):
    return jax.shard_map(
        local,
        mesh=mesh,
        in_specs=(
            P(None, "bx", "by"),
            P(None, "bx", "by"),
            P(None, "bx", "by"),
            P(None, "bx", "by"),
            P(None, "bx", "by"),
            P(None, "bx", "by"),
            P(None, "bx", "by"),
            P("bx", "by"),
            P(("bx", "by"), None),
        ),
        out_specs=(P(None, "bx", "by"), P(None, "bx", "by"), P(("bx", "by"), None)),
        check_vma=False,
    )
```

profile of v0, /device:TPU:0, one launch (start us, length us, event | category | flops | bytes accessed | tf_op | source)
XLA Modules:
  0.0 283.7 jit_solution(15581652433624035366)
XLA Ops:
  0.7 1.9 copy_bitcast_fusion.1
  2.6 0.8 convert_bitcast_fusion
  3.4 1.8 copy_bitcast_fusion
  5.2 0.2 copy_dynamic-update-slice_fusion.3
  5.3 0.2 copy_dynamic-update-slice_fusion.2
  5.5 0.2 copy_dynamic-update-slice_fusion.1
  5.7 0.2 copy_dynamic-update-slice_fusion
  5.9 0.1 dynamic-update-slice.9
  6.0 1.3 collective-permute-start.1
  7.3 5.5 %collective-permute-start = (f32[49,1,256]{2,0,1:T(8,128)S(1)}, f32[49,1,256]{2,0,1:T(8,128)S(1)}, u32[]{:S(2)}, u32[]{:S(2)}) collective-permute-start(f32[49,1,256]{2,0,1:T(8,128)S(1)} %get-tuple-element.64), channel_id=1, source_target_pairs={{0,4},{4,8},{8,12},{12,16},{16,20},{20,24},{24,28},{1,5},{5,9},{9,... | collective-permute-start | bytes 150536 | tf_op jit(solution)/shard_map/ppermute | solution.py:19
  12.8 0.2 collective-permute-done.1
  13.0 1.6 collective-permute-done
  14.6 0.1 pad_maximum_fusion
  14.8 1.3 fusion.75
  16.0 1.6 copy.53
  17.6 1.3 collective-permute-start.3
  19.0 0.4 copy.52
  19.4 3.0 %collective-permute-start.2 = (f32[49,34,1]{0,1,2:T(8,128)S(1)}, f32[49,34,1]{0,1,2:T(8,128)S(1)}, u32[]{:S(2)}, u32[]{:S(2)}) collective-permute-start(f32[49,34,1]{0,1,2:T(8,128)S(1)} %copy.52), channel_id=1, source_target_pairs={{0,1},{1,2},{2,3},{4,5},{5,6},{6,7},{8,9},{9,10},{10,11},{12,13},{... | collective-permute-start | bytes 20000 | tf_op jit(solution)/shard_map/ppermute | solution.py:19
  22.4 0.9 maximum_multiply_fusion.1
  23.3 1.4 copy.55
  24.7 0.5 copy.54
  25.2 1.1 pad_maximum_fusion.9
  26.4 0.2 slice_multiply_fusion
  26.6 0.2 slice_multiply_fusion.1
  26.8 0.1 slice.463
  26.9 0.1 slice.485
  27.2 0.3 copy-done
  27.5 0.4 fusion.1
  27.9 0.3 maximum_multiply_fusion
  28.2 0.7 fusion.7
  28.9 0.2 copy-done.1
  29.2 0.6 fusion.13
  29.9 0.3 copy-done.3
  30.3 0.2 fusion.17
  30.6 0.9 scatter-add.4
  31.5 0.2 slice_multiply_fusion.2
  31.9 0.6 slice_subtract_fusion.7
  32.7 0.7 fusion.33
  33.4 0.6 multiply_add_fusion
  34.0 0.8 stack.11
  34.9 0.2 multiply_reduce_fusion
  35.1 7.5 %all_to_all.16 = f32[4,8,256]{2,1,0:T(8,128)S(1)} all-to-all(f32[4,8,256]{2,1,0:T(8,128)S(1)} %multiply_bitcast_fusion), channel_id=1, replica_groups=mesh['bx'=8,'by'=4] {'by'}, dimensions={0} | all-to-all | bytes 65536 | tf_op jit(solution)/shard_map/all_to_all | solution.py:135
  42.6 1.3 collective-permute-start.5
  43.8 3.0 %collective-permute-start.4 = (f32[1,1024]{1,0:T(1,128)S(1)}, f32[1,1024]{1,0:T(1,128)S(1)}, u32[]{:S(2)}, u32[]{:S(2)}) collective-permute-start(f32[1,1024]{1,0:T(1,128)S(1)} %bitcast.103), channel_id=1, source_target_pairs={{0,1},{1,2},{2,3},{3,4},{4,5},{5,6},{6,7},{7,8},{8,9},{9,10},{10,1... | collective-permute-start | bytes 12296 | tf_op jit(solution)/shard_map/ppermute | solution.py:19
  46.9 0.6 multiply_reduce_fusion.5
  47.5 0.2 collective-permute-done.4
  47.8 0.7 multiply_reduce_fusion.4
  48.5 45.9 %all-reduce.5 = (f32[]{:T(128)}, f32[]{:T(128)}) all-reduce(f32[]{:T(128)} %multiply_reduce_fusion.5, f32[]{:T(128)} %get-tuple-element.27), channel_id=1, replica_groups=mesh['bx'=8,'by'=4] {'bx','by'}, use_global_device_ids=true, to_apply=%region_2.0 | all-reduce | flops 2 | bytes 16 | tf_op jit(solution)/shard_map/psum | solution.py:140
  95.8 0.6 multiply_reduce_fusion.3
  96.4 40.0 %psum.44 = f32[]{:T(128)} all-reduce(f32[]{:T(128)} %get-tuple-element.25), channel_id=1, replica_groups=mesh['bx'=8,'by'=4] {'bx','by'}, use_global_device_ids=true, to_apply=%region_6.7 | all-reduce | flops 1 | bytes 8 | tf_op jit(solution)/shard_map/psum | solution.py:140
  137.8 1.3 collective-permute-start.7
  139.1 3.0 %collective-permute-start.6 = (f32[1,1024]{1,0:T(1,128)S(1)}, f32[1,1024]{1,0:T(1,128)S(1)}, u32[]{:S(2)}, u32[]{:S(2)}) collective-permute-start(f32[1,1024]{1,0:T(1,128)S(1)} %get-tuple-element.82), channel_id=1, source_target_pairs={{0,1},{1,2},{2,3},{3,4},{4,5},{5,6},{6,7},{7,8},{8,9},{9,10},{10,1... | collective-permute-start | bytes 12296 | tf_op jit(solution)/shard_map/ppermute | solution.py:19
  142.1 0.8 collective-permute-done.6
  143.0 0.7 multiply_reduce_fusion.2
  143.7 44.1 %psum.45 = f32[]{:T(128)} all-reduce(f32[]{:T(128)} %get-tuple-element.23), channel_id=1, replica_groups=mesh['bx'=8,'by'=4] {'bx','by'}, use_global_device_ids=true, to_apply=%region_8.9 | all-reduce | flops 1 | bytes 8 | tf_op jit(solution)/shard_map/psum | solution.py:140
  189.2 0.6 multiply_reduce_fusion.1
  189.8 39.9 %psum.46 = f32[]{:T(128)} all-reduce(f32[]{:T(128)} %multiply_reduce_fusion.1), channel_id=1, replica_groups=mesh['bx'=8,'by'=4] {'bx','by'}, use_global_device_ids=true, to_apply=%region_10.11 | all-reduce | flops 1 | bytes 8 | tf_op jit(solution)/shard_map/psum | solution.py:140
  231.1 1.3 collective-permute-start.9
  232.4 3.0 %collective-permute-start.8 = (f32[1,1024]{1,0:T(1,128)S(1)}, f32[1,1024]{1,0:T(1,128)S(1)}, u32[]{:S(2)}, u32[]{:S(2)}) collective-permute-start(f32[1,1024]{1,0:T(1,128)S(1)} %get-tuple-element.80), channel_id=1, source_target_pairs={{0,1},{1,2},{2,3},{3,4},{4,5},{5,6},{6,7},{7,8},{8,9},{9,10},{10,1... | collective-permute-start | bytes 12296 | tf_op jit(solution)/shard_map/ppermute | solution.py:19
  235.4 0.8 copy.61
  236.3 0.7 fusion.42
  237.0 0.8 copy.62
  237.8 43.9 %psum.47 = f32[]{:T(128)} all-reduce(f32[]{:T(128)} %fusion.42), channel_id=1, replica_groups=mesh['bx'=8,'by'=4] {'bx','by'}, use_global_device_ids=true, to_apply=%region_12.13 | all-reduce | flops 1 | bytes 8 | tf_op jit(solution)/shard_map/psum | solution.py:140
  283.1 0.6 multiply_add_fusion.7
  (61 shorter events, 1.3 us)
Async XLA Ops:
  0.6 4.5 %copy-start.8 = (f32[8,32,256]{2,1,0:T(8,128)S(1)}, f32[8,32,256]{2,1,0:T(8,128)}, u32[]{:S(2)}) copy-start(f32[8,32,256]{2,1,0:T(8,128)} %param.13) | copy-start | bytes 786436
  0.6 4.7 %copy-start.9 = (f32[8,32,256]{2,1,0:T(8,128)S(1)}, f32[8,32,256]{2,1,0:T(8,128)}, u32[]{:S(2)}) copy-start(f32[8,32,256]{2,1,0:T(8,128)} %param.14) | copy-start | bytes 786436
  0.7 4.9 %copy-start.10 = (f32[8,32,256]{2,1,0:T(8,128)S(1)}, f32[8,32,256]{2,1,0:T(8,128)}, u32[]{:S(2)}) copy-start(f32[8,32,256]{2,1,0:T(8,128)} %param.15) | copy-start | bytes 786436
  0.7 5.0 %copy-start.11 = (f32[8,32,256]{2,1,0:T(8,128)S(1)}, f32[8,32,256]{2,1,0:T(8,128)}, u32[]{:S(2)}) copy-start(f32[8,32,256]{2,1,0:T(8,128)} %param.16) | copy-start | bytes 786436
  6.0 7.0 %collective-permute-start.1 = (f32[49,1,256]{2,0,1:T(8,128)S(1)}, f32[49,1,256]{2,0,1:T(8,128)S(1)}, u32[]{:S(2)}, u32[]{:S(2)}) collective-permute-start(f32[49,1,256]{2,0,1:T(8,128)S(1)} %get-tuple-element.65), channel_id=1, source_target_pairs={{4,0},{8,4},{12,8},{16,12},{20,16},{24,20},{28,24},{5,1},{9,5},{13... | collective-permute-start | bytes 150536 | tf_op jit(solution)/shard_map/ppermute | solution.py:21
  7.3 7.3 %collective-permute-start = (f32[49,1,256]{2,0,1:T(8,128)S(1)}, f32[49,1,256]{2,0,1:T(8,128)S(1)}, u32[]{:S(2)}, u32[]{:S(2)}) collective-permute-start(f32[49,1,256]{2,0,1:T(8,128)S(1)} %get-tuple-element.64), channel_id=1, source_target_pairs={{0,4},{4,8},{8,12},{12,16},{16,20},{20,24},{24,28},{1,5},{5,9},{9,... | collective-permute-start | bytes 150536 | tf_op jit(solution)/shard_map/ppermute | solution.py:19
  13.0 12.2 %copy-start.5 = (f32[49,1,256]{2,0,1:T(8,128)}, f32[49,1,256]{2,0,1:T(8,128)S(1)}, u32[]{:S(2)}) copy-start(f32[49,1,256]{2,0,1:T(8,128)S(1)} %collective-permute-done.1) | copy-start | bytes 150532
  17.6 5.7 %collective-permute-start.3 = (f32[49,34,1]{0,1,2:T(8,128)S(1)}, f32[49,34,1]{0,1,2:T(8,128)S(1)}, u32[]{:S(2)}, u32[]{:S(2)}) collective-permute-start(f32[49,34,1]{0,1,2:T(8,128)S(1)} %copy.53), channel_id=1, source_target_pairs={{1,0},{2,1},{3,2},{5,4},{6,5},{7,6},{9,8},{10,9},{11,10},{13,12},{... | collective-permute-start | bytes 20000 | tf_op jit(solution)/shard_map/ppermute | solution.py:21
  19.4 5.3 %collective-permute-start.2 = (f32[49,34,1]{0,1,2:T(8,128)S(1)}, f32[49,34,1]{0,1,2:T(8,128)S(1)}, u32[]{:S(2)}, u32[]{:S(2)}) collective-permute-start(f32[49,34,1]{0,1,2:T(8,128)S(1)} %copy.52), channel_id=1, source_target_pairs={{0,1},{1,2},{2,3},{4,5},{5,6},{6,7},{8,9},{9,10},{10,11},{12,13},{... | collective-permute-start | bytes 20000 | tf_op jit(solution)/shard_map/ppermute | solution.py:19
  26.3 0.8 copy-start.12
  26.3 1.2 copy-start
  26.3 1.2 copy-start.6
  28.2 1.0 copy-start.1
  28.2 1.0 copy-start.2
  29.2 0.9 copy-start.3
  29.2 1.0 copy-start.4
  34.0 13.8 %copy-start.7 = (f32[8,1024]{1,0:T(8,128)S(1)}, f32[8,1024]{1,0:T(8,128)}, u32[]{:S(2)}) copy-start(f32[8,1024]{1,0:T(8,128)} %param.19) | copy-start | bytes 98308
  42.6 4.9 %collective-permute-start.5 = (f32[1,1024]{1,0:T(1,128)S(1)}, f32[1,1024]{1,0:T(1,128)S(1)}, u32[]{:S(2)}, u32[]{:S(2)}) collective-permute-start(f32[1,1024]{1,0:T(1,128)S(1)} %bitcast.104), channel_id=1, source_target_pairs={{1,0},{2,1},{3,2},{4,3},{5,4},{6,5},{7,6},{8,7},{9,8},{10,9},{11,1... | collective-permute-start | bytes 12296 | tf_op jit(solution)/shard_map/ppermute | solution.py:21
  43.8 3.8 %collective-permute-start.4 = (f32[1,1024]{1,0:T(1,128)S(1)}, f32[1,1024]{1,0:T(1,128)S(1)}, u32[]{:S(2)}, u32[]{:S(2)}) collective-permute-start(f32[1,1024]{1,0:T(1,128)S(1)} %bitcast.103), channel_id=1, source_target_pairs={{0,1},{1,2},{2,3},{3,4},{4,5},{5,6},{6,7},{7,8},{8,9},{9,10},{10,1... | collective-permute-start | bytes 12296 | tf_op jit(solution)/shard_map/ppermute | solution.py:19
  137.8 4.3 %collective-permute-start.7 = (f32[1,1024]{1,0:T(1,128)S(1)}, f32[1,1024]{1,0:T(1,128)S(1)}, u32[]{:S(2)}, u32[]{:S(2)}) collective-permute-start(f32[1,1024]{1,0:T(1,128)S(1)} %get-tuple-element.83), channel_id=1, source_target_pairs={{1,0},{2,1},{3,2},{4,3},{5,4},{6,5},{7,6},{8,7},{9,8},{10,9},{11,1... | collective-permute-start | bytes 12296 | tf_op jit(solution)/shard_map/ppermute | solution.py:21
  139.1 3.8 %collective-permute-start.6 = (f32[1,1024]{1,0:T(1,128)S(1)}, f32[1,1024]{1,0:T(1,128)S(1)}, u32[]{:S(2)}, u32[]{:S(2)}) collective-permute-start(f32[1,1024]{1,0:T(1,128)S(1)} %get-tuple-element.82), channel_id=1, source_target_pairs={{0,1},{1,2},{2,3},{3,4},{4,5},{5,6},{6,7},{7,8},{8,9},{9,10},{10,1... | collective-permute-start | bytes 12296 | tf_op jit(solution)/shard_map/ppermute | solution.py:19
  231.1 5.2 %collective-permute-start.9 = (f32[1,1024]{1,0:T(1,128)S(1)}, f32[1,1024]{1,0:T(1,128)S(1)}, u32[]{:S(2)}, u32[]{:S(2)}) collective-permute-start(f32[1,1024]{1,0:T(1,128)S(1)} %get-tuple-element.81), channel_id=1, source_target_pairs={{1,0},{2,1},{3,2},{4,3},{5,4},{6,5},{7,6},{8,7},{9,8},{10,9},{11,1... | collective-permute-start | bytes 12296 | tf_op jit(solution)/shard_map/ppermute | solution.py:21
  232.4 3.9 %collective-permute-start.8 = (f32[1,1024]{1,0:T(1,128)S(1)}, f32[1,1024]{1,0:T(1,128)S(1)}, u32[]{:S(2)}, u32[]{:S(2)}) collective-permute-start(f32[1,1024]{1,0:T(1,128)S(1)} %get-tuple-element.80), channel_id=1, source_target_pairs={{0,1},{1,2},{2,3},{3,4},{4,5},{5,6},{6,7},{7,8},{8,9},{9,10},{10,1... | collective-permute-start | bytes 12296 | tf_op jit(solution)/shard_map/ppermute | solution.py:19
where the time goes:
time: 285 us; the launch traced here: 284 us
  blocking collectives  221 us (78%)
  starting transfers between devices  24.1 us (8%)
  local copies, waits for them, and re-layouts  14.6 us (5%)
  other arithmetic  13 us (5%)
  between operations  7.87 us (3%)
    psum x5, blocking collectives, inner(): return lax.psum(jnp.sum(left_field * right_field), ('bx', 'by'))  214 us
    ppermute x5, starting transfers between devices, with_halo(): lax.ppermute(tail, axis, [(i, (i + 1) % count) for i in range(ends)])  17.6 us
    all_to_all x1, blocking collectives, local(): lax.all_to_all(forcing, 'by', split_axis=0, concat_axis=1, tiled=True)  7.47 us
    ppermute x5, starting transfers between devices, with_halo(): lax.ppermute(head, axis, [((i + 1) % count, i) for i in range(ends)])  6.47 us
  transfers between devices with their start and end apart: 10, of which 4 were waited for; matrix products, arithmetic and copies ran while one was open for 1% of the time, Pallas kernels for 0%

commit v1 on v0

--- a/solution.py
+++ b/solution.py
@@ -6,10 +6,13 @@
 from jax.sharding import PartitionSpec as P
 
 ITERS = 3
-
-
-def with_halo(cells, sides, width):
-    for axis, dim in sides:
+CENTRE = 4.5
+SCALE = 4.5
+DEEP = ITERS + 1
+
+
+def with_halo(cells, sides):
+    for axis, dim, width in sides:
         count = lax.axis_size(axis)
         ends = count - 1
         head = lax.slice_in_dim(cells, 0, width, axis=dim)
@@ -85,11 +88,37 @@
     return (fresh, forcing)
 
 
-def nine_point(padded, operator_main_entry):
+def shifted_operator(padded, main):
     centre = padded[1:-1, 1:-1]
     edges = padded[:-2, 1:-1] + padded[2:, 1:-1] + padded[1:-1, :-2] + padded[1:-1, 2:]
     corners = padded[:-2, :-2] + padded[:-2, 2:] + padded[2:, :-2] + padded[2:, 2:]
-    return (6.0 + operator_main_entry) * centre - edges - 0.5 * corners
+    return ((6.0 - CENTRE + main) * centre - edges - 0.5 * corners) * (1.0 / SCALE)
+
+
+def coefficients(moments):
+    def inner(a, b):
+        return sum(x * y * moments[i + j] for i, x in enumerate(a) for j, y in enumerate(b))
+
+    one = jnp.ones_like(moments[0])
+    resid = [one]
+    direction = [one]
+    total = [jnp.zeros_like(one)] * ITERS
+    norm_now = inner(resid, resid)
+    for step in range(ITERS):
+        image = [jnp.zeros_like(one)] * (len(direction) + 1)
+        for i, x in enumerate(direction):
+            image[i] = image[i] + CENTRE * x
+            image[i + 1] = image[i + 1] + SCALE * x
+        alpha = norm_now / inner(direction, image)
+        for i, x in enumerate(direction):
+            total[i] = total[i] + alpha * x
+        if step + 1 < ITERS:
+            resid = [r - alpha * q for r, q in zip(resid + [jnp.zeros_like(one)], image)]
+            norm_next = inner(resid, resid)
+            beta = norm_next / norm_now
+            direction = [r + beta * p for r, p in zip(resid, direction + [jnp.zeros_like(one)])]
+            norm_now = norm_next
+    return total
 
 
 def local(
@@ -103,8 +132,12 @@
     wet_layer_number,
     operator_main_entry,
 ):
-    layer_tally, strip_accumulated, vertical_integral = thermal_anomaly.shape
-    bottom_level_map = wet_layer_number.astype(jnp.float32)[None]
+    layers, rows, columns = thermal_anomaly.shape
+    across = lax.axis_size("by")
+    along = lax.axis_size("bx")
+    own_bx = lax.axis_index("bx")
+    own_by = lax.axis_index("by")
+    strip = rows // across
     planes = jnp.concatenate(
         [
             thermal_anomaly,
@@ -113,62 +146,79 @@
             speed_across_second_face,
             isoline_incline_first,
             isoline_incline_second,
-            bottom_level_map,
+            top_boundary_source,
+            wet_layer_number.astype(jnp.float32)[None],
         ],
         0,
     )
-    padded = with_halo(planes, (("bx", 1), ("by", 2)), 1)
-    tracers_p = padded[: 2 * layer_tally].reshape(
-        2, layer_tally, strip_accumulated + 2, vertical_integral + 2
-    )
-    east_p = padded[2 * layer_tally : 3 * layer_tally]
-    north_p = padded[3 * layer_tally : 4 * layer_tally]
-    slope_ep = padded[4 * layer_tally : 5 * layer_tally]
-    slope_np = padded[5 * layer_tally : 6 * layer_tally]
-    depth_p = padded[6 * layer_tally]
-    level_ids = jnp.arange(layer_tally, dtype=jnp.float32)[:, None, None]
+    padded = with_halo(planes, (("by", 2, 1), ("bx", 1, DEEP)))
+    tracers_p = padded[: 2 * layers].reshape((2, layers) + padded.shape[1:])
+    east_p = padded[2 * layers : 3 * layers]
+    north_p = padded[3 * layers : 4 * layers]
+    slope_ep = padded[4 * layers : 5 * layers]
+    slope_np = padded[5 * layers : 6 * layers]
+    source_p = padded[6 * layers : 6 * layers + 2]
+    depth_p = padded[6 * layers + 2]
+    level_ids = jnp.arange(layers, dtype=jnp.float32)[:, None, None]
     wet_p = (level_ids < depth_p[None]).astype(jnp.float32)
     tend = tendency(tracers_p, east_p, north_p, slope_ep, slope_np, wet_p)
-    wet = wet_p[:, 1:-1, 1:-1]
-    carried_quantities = jnp.stack([thermal_anomaly, saltiness_anomaly], 0)
-    fresh, forcing = column_step(carried_quantities, tend, wet, top_boundary_source)
-    slab = lax.all_to_all(forcing, "by", split_axis=0, concat_axis=1, tiled=True)
-    solution = jnp.zeros_like(slab)
-    resid = slab
-
-    def inner(left_field, right_field):
-        return lax.psum(jnp.sum(left_field * right_field), ("bx", "by"))
-
-    direction = slab
-    norm_now = inner(resid, resid)
+    fresh, forcing = column_step(
+        tracers_p[:, :, 1:-1, 1:-1], tend, wet_p[:, 1:-1, 1:-1], source_p[:, 1:-1, 1:-1]
+    )
+    fresh = fresh[:, :, ITERS:-ITERS]
+
+    tall = strip + 2 * ITERS
+    everyone = range(across)
+    blocks = jnp.zeros((across, tall, columns), jnp.float32)
+    for hop in everyone:
+        peer = (own_by + hop) % across
+        block = lax.dynamic_slice(forcing, (peer * strip, 0), (tall, columns))
+        if hop:
+            block = lax.ppermute(block, "by", [(i, (i + hop) % across) for i in everyone])
+        origin = (own_by - hop) % across
+        blocks = lax.dynamic_update_slice(blocks, block[None], (origin, 0, 0))
+    field = jnp.concatenate([blocks[i] for i in everyone], 1)
+
+    ends = across * along - 1
+    names = ("bx", "by")
+    wide = ITERS - 1
+    main = jnp.concatenate(
+        [
+            lax.ppermute(operator_main_entry[-wide:], names, [(i, i + 1) for i in range(ends)]),
+            operator_main_entry,
+            lax.ppermute(operator_main_entry[:wide], names, [(i + 1, i) for i in range(ends)]),
+        ],
+        0,
+    )
+    first = (own_bx * across + own_by) * strip
+    basis = [field[ITERS:-ITERS]]
     for step in range(ITERS):
-        rows_p = with_halo(direction, ((("bx", "by"), 0),), 1)
-        image = nine_point(jnp.pad(rows_p, ((0, 0), (1, 1))), operator_main_entry)
-        alpha = norm_now / inner(direction, image)
-        solution = solution + alpha * direction
-        resid = resid - alpha * image
-        if step + 1 < ITERS:
-            norm_next = inner(resid, resid)
-            direction = resid + norm_next / norm_now * direction
-            norm_now = norm_next
-    return (fresh[0], fresh[1], solution)
+        trim = step
+        here = main[trim : main.shape[0] - trim]
+        field = shifted_operator(jnp.pad(field, ((0, 0), (1, 1))), here)
+        reach = wide - step
+        line = first - reach + jnp.arange(field.shape[0])[:, None]
+        field = jnp.where((line >= 0) & (line < along * across * strip), field, 0.0)
+        basis.append(field[reach : field.shape[0] - reach])
+    pairs = [(0, 0), (0, 1), (1, 1), (1, 2), (2, 2), (2, 3)]
+    sums = jnp.stack([jnp.sum(basis[i] * basis[j]) for i, j in pairs])
+    row = jnp.pad(sums, (0, 128 - len(pairs)))
+    gathered = lax.all_to_all(
+        jnp.broadcast_to(row[None, None], (ends + 1, 1, 128)), names, 0, 0, tiled=True
+    )
+    moments = jnp.sum(gathered, (0, 1))
+    total = coefficients([moments[i] for i in range(len(pairs))])
+    pressure = total[0] * basis[0] + total[1] * basis[1] + total[2] * basis[2]
+    return (fresh[0], fresh[1], pressure)
 
 
 def solution(mesh):
+    tile = P(None, "bx", "by")
+    rows = P(("bx", "by"), None)
     return jax.shard_map(
         local,
         mesh=mesh,
-        in_specs=(
-            P(None, "bx", "by"),
-            P(None, "bx", "by"),
-            P(None, "bx", "by"),
-            P(None, "bx", "by"),
-            P(None, "bx", "by"),
-            P(None, "bx", "by"),
-            P(None, "bx", "by"),
-            P("bx", "by"),
-            P(("bx", "by"), None),
-        ),
-        out_specs=(P(None, "bx", "by"), P(None, "bx", "by"), P(("bx", "by"), None)),
+        in_specs=(tile,) * 7 + (P("bx", "by"), rows),
+        out_specs=(tile, tile, rows),
         check_vma=False,
     )

time: 285 us -> 88.8 us (0.31)
  blocking collectives: 221 us -> 0 us
  waiting for transfers between devices: 2.81 us -> 20.5 us
  between operations: 7.87 us -> 21.1 us
  other arithmetic: 13 us -> 8.03 us
    psum x5 -> x0, blocking collectives: 214 us -> none  [inner(): return lax.psum(jnp.sum(left_field * right_field), ('bx', 'by'))]
    ppermute x5 -> x2, starting transfers between devices: 17.6 us -> 7.59 us  [with_halo(): lax.ppermute(tail, axis, [(i, (i + 1) % count) for i in range(ends)])]
    ppermute x0 -> x5, starting transfers between devices: none -> 9.59 us  [the longest x1 5.12 us: local(): lax.ppermute(operator_main_entry[-wide:], names, [(i, i + 1) for i in ran...]
    all_to_all x1 -> x0, blocking collectives: 7.47 us -> none  [local(): lax.all_to_all(forcing, 'by', split_axis=0, concat_axis=1, tiled=True)]
    all_to_all x0 -> x1, waiting for transfers between devices: none -> 6.22 us  [local(): lax.all_to_all(jnp.broadcast_to(row[None, None], (ends + 1, 1, 128)), nam...]
    all_to_all x0 -> x1, starting transfers between devices: none -> 6.03 us  [local(): lax.all_to_all(jnp.broadcast_to(row[None, None], (ends + 1, 1, 128)), nam...]
    ppermute x5 -> x2, waiting for transfers between devices: 0.23 us -> 5.53 us  [with_halo(): lax.ppermute(head, axis, [((i + 1) % count, i) for i in range(ends)])]
    ppermute x5 -> x2, waiting for transfers between devices: 2.59 us -> 7.32 us  [with_halo(): lax.ppermute(tail, axis, [(i, (i + 1) % count) for i in range(ends)])]
  transfers between devices with their start and end apart: 10 -> 10, of which waited for: 4 -> 5; matrix products, arithmetic and copies ran while one was open for 1% -> 11% of each run, Pallas kernels for 0% -> 0%
where the time goes in v1:
time: 88.8 us; the launch traced here: 88.2 us
  starting transfers between devices  25.8 us (29%)
  between operations  21.1 us (24%)
  waiting for transfers between devices  20.5 us (23%)
  local copies, waits for them, and re-layouts  12.7 us (14%)
  other arithmetic  8.03 us (9%)
    ppermute x2, starting transfers between devices, with_halo(): lax.ppermute(tail, axis, [(i, (i + 1) % count) for i in range(ends)])  7.59 us
    ppermute x2, waiting for transfers between devices, with_halo(): lax.ppermute(tail, axis, [(i, (i + 1) % count) for i in range(ends)])  7.32 us
    all_to_all x1, waiting for transfers between devices, local(): lax.all_to_all(jnp.broadcast_to(row[None, None], (ends + 1, 1, 128)), nam...  6.22 us
    all_to_all x1, starting transfers between devices, local(): lax.all_to_all(jnp.broadcast_to(row[None, None], (ends + 1, 1, 128)), nam...  6.03 us
    ppermute x2, waiting for transfers between devices, with_halo(): lax.ppermute(head, axis, [((i + 1) % count, i) for i in range(ends)])  5.53 us
    ppermute x1, starting transfers between devices, local(): lax.ppermute(operator_main_entry[-wide:], names, [(i, i + 1) for i in ran...  5.12 us
    another operation x1, local copies, waits for them, and re-layouts, local(): sums = jnp.stack([jnp.sum(basis[i] * basis[j]) for i, j in pairs])  3.96 us
    ppermute x3, starting transfers between devices, local(): lax.ppermute(block, 'by', [(i, (i + hop) % across) for i in everyone])  3.18 us
  transfers between devices with their start and end apart: 10, of which 5 were waited for; matrix products, arithmetic and copies ran while one was open for 11% of the time, Pallas kernels for 0%

profile of v1, /device:TPU:0, one launch (start us, length us, event | category | flops | bytes accessed | tf_op | source)
XLA Modules:
  0.0 88.2 jit_solution(16936221294341986061)
XLA Ops:
  0.6 0.0 copy-start
  0.6 0.0 copy-start.1
  0.7 0.0 copy-start.2
  0.7 0.0 copy-start.4
  0.7 0.0 copy-start.5
  0.7 1.0 %constant_dynamic-update-slice_fusion.7 = f32[51,32,256]{2,1,0:T(8,128)S(1)} fusion(f32[8,32,256]{2,1,0:T(8,128)} %param.11), kind=kLoop, calls=%fused_computation.160 | loop fusion | bytes 524288
  1.7 1.0 %constant_dynamic-update-slice_fusion.6 = f32[51,32,256]{2,1,0:T(8,128)S(1)} fusion(f32[51,32,256]{2,1,0:T(8,128)S(1)} %constant_dynamic-update-slice_fusion.7, f32[8,32,256]{2,1,0:T(8,128)} %param.12), kind=kLoop, calls=%fused_computation.159 | loop fusion | bytes 524288
  2.7 1.0 %constant_dynamic-update-slice_fusion.5 = f32[51,32,256]{2,1,0:T(8,128)S(1)} fusion(f32[51,32,256]{2,1,0:T(8,128)S(1)} %constant_dynamic-update-slice_fusion.6, f32[8,32,256]{2,1,0:T(8,128)} %param.13), kind=kLoop, calls=%fused_computation.158 | loop fusion | bytes 524288
  3.7 0.0 copy-done
  3.7 0.0 copy-done.1
  3.8 0.3 fusion.81
  4.1 0.0 copy-start.3
  4.2 0.6 copy.61
  4.7 1.3 %collective-permute-start.1 = (f32[51,32,1]{0,1,2:T(8,128)S(1)}, f32[51,32,1]{0,1,2:T(8,128)S(1)}, u32[]{:S(2)}, u32[]{:S(2)}) collective-permute-start(f32[51,32,1]{0,1,2:T(8,128)S(1)} %copy.61), channel_id=1, source_target_pairs={{1,0},{2,1},{3,2},{5,4},{6,5},{7,6},{9,8},{10,9},{11,10},{13,12},{... | collective-permute-start | bytes 19592 | tf_op jit(solution)/shard_map/ppermute | solution.py:24
  6.0 0.6 copy.60
  6.6 3.0 %collective-permute-start = (f32[51,32,1]{0,1,2:T(8,128)S(1)}, f32[51,32,1]{0,1,2:T(8,128)S(1)}, u32[]{:S(2)}, u32[]{:S(2)}) collective-permute-start(f32[51,32,1]{0,1,2:T(8,128)S(1)} %copy.60), channel_id=1, source_target_pairs={{0,1},{1,2},{2,3},{4,5},{5,6},{6,7},{8,9},{9,10},{10,11},{12,13},{... | collective-permute-start | bytes 19592 | tf_op jit(solution)/shard_map/ppermute | solution.py:22
  9.7 1.3 %collective-permute-start.8 = (f32[2,1024]{1,0:T(2,128)S(1)}, f32[2,1024]{1,0:T(2,128)S(1)}, u32[]{:S(2)}, u32[]{:S(2)}) collective-permute-start(f32[2,1024]{1,0:T(2,128)S(1)} %get-tuple-element.73), channel_id=1, source_target_pairs={{1,0},{2,1},{3,2},{4,3},{5,4},{6,5},{7,6},{8,7},{9,8},{10,9},{11,1... | collective-permute-start | bytes 24584 | tf_op jit(solution)/shard_map/ppermute | solution.py:189
  10.9 5.1 %collective-permute-start.7 = (f32[2,1024]{1,0:T(2,128)S(1)}, f32[2,1024]{1,0:T(2,128)S(1)}, u32[]{:S(2)}, u32[]{:S(2)}) collective-permute-start(f32[2,1024]{1,0:T(2,128)S(1)} %get-tuple-element.72), channel_id=1, source_target_pairs={{0,1},{1,2},{2,3},{3,4},{4,5},{5,6},{6,7},{7,8},{8,9},{9,10},{10,1... | collective-permute-start | bytes 24584 | tf_op jit(solution)/shard_map/ppermute | solution.py:187
  16.2 0.0 collective-permute-done.1
  16.2 0.8 copy.63
  17.1 0.0 collective-permute-done
  17.1 0.8 copy.62
  17.9 0.5 pad_maximum_fusion.3
  18.4 1.3 %collective-permute-start.3 = (f32[51,4,258]{2,1,0:T(4,128)S(1)}, f32[51,4,258]{2,1,0:T(4,128)S(1)}, u32[]{:S(2)}, u32[]{:S(2)}) collective-permute-start(f32[51,4,258]{2,1,0:T(4,128)S(1)} %get-tuple-element.43), channel_id=1, source_target_pairs={{4,0},{8,4},{12,8},{16,12},{20,16},{24,20},{28,24},{5,1},{9,5},{13... | collective-permute-start | bytes 631592 | tf_op jit(solution)/shard_map/ppermute | solution.py:24
  19.7 4.6 %collective-permute-start.2 = (f32[51,4,258]{2,1,0:T(4,128)S(1)}, f32[51,4,258]{2,1,0:T(4,128)S(1)}, u32[]{:S(2)}, u32[]{:S(2)}) collective-permute-start(f32[51,4,258]{2,1,0:T(4,128)S(1)} %get-tuple-element.42), channel_id=1, source_target_pairs={{0,4},{4,8},{8,12},{12,16},{16,20},{20,24},{24,28},{1,5},{5,9},{9,... | collective-permute-start | bytes 631592 | tf_op jit(solution)/shard_map/ppermute | solution.py:22
  24.3 5.5 %collective-permute-done.3 = f32[51,4,258]{2,1,0:T(4,128)S(1)} collective-permute-done((f32[51,4,258]{2,1,0:T(4,128)S(1)}, f32[51,4,258]{2,1,0:T(4,128)S(1)}, u32[]{:S(2)}, u32[]{:S(2)}) %collective-permute-start.3) | collective-permute-done | bytes 210560 | tf_op jit(solution)/shard_map/ppermute | solution.py:24
  29.9 7.3 %collective-permute-done.2 = f32[51,4,258]{2,1,0:T(4,128)S(1)} collective-permute-done((f32[51,4,258]{2,1,0:T(4,128)S(1)}, f32[51,4,258]{2,1,0:T(4,128)S(1)}, u32[]{:S(2)}, u32[]{:S(2)}) %collective-permute-start.2) | collective-permute-done | bytes 210560 | tf_op jit(solution)/shard_map/ppermute | solution.py:22
  37.2 0.1 maximum_bitcast_fusion
  37.3 0.2 slice.508
  37.5 0.1 slice_bitcast_fusion.2
  37.6 1.2 %pad_maximum_fusion = f32[51,40,258]{2,1,0:T(8,128)S(1)} fusion(f32[51,4,258]{2,1,0:T(4,128)S(1)} %collective-permute-done.3, f32[51,32,1]{2,1,0:T(8,128)S(1)} %copy.63, f32[51,32,256]{2,1,0:T(8,128)S(1)} %constant_dynamic-update-slice_fusion, f32[51,32,1]{2,1,0:T(8,128)S(1)} %copy.62, f32[51,4,258]{2,1,0:T(4,128)S(1)} %collective-permute-done.2), kind=kLoop, calls=%fused_computation | loop fusion | flops 2105280 | bytes 4210560 | tf_op jit(solution)/shard_map/concatenate | solution.py:20
  38.8 0.1 slice.506
  38.9 0.1 broadcast_multiply_fusion
  39.0 0.6 maximum_multiply_fusion.1
  39.6 0.9 %fusion.5 = f32[2,8,38,257]{3,2,1,0:T(8,128)S(1)} fusion(f32[2,8,40,258]{3,2,1,0:T(8,128)S(1)} %broadcast_multiply_fusion, f32[8,38,257]{2,1,0:T(8,128)S(1)} %get-tuple-element.41, f32[8,38,257]{2,1,0:T(8,128)S(1)} %get-tuple-element.40, f32[8,38,257]{2,1,0:T(8,128)S(1)} %get-tuple-element.80), kind=kLoop, calls=%fused_computation.7 | loop fusion | flops 1718816 | bytes 5312704 | tf_op jit(solution)/shard_map/mul | solution.py:49
  40.5 0.4 maximum_multiply_fusion.3
  40.9 0.8 fusion.16
  41.7 0.5 fusion.9
  42.1 0.1 fusion.37
  42.3 0.1 fusion.22
  42.3 0.2 slice_multiply_fusion.6
  42.6 0.1 fusion.58
  42.7 0.1 fusion.72
  42.8 0.2 add_dynamic-update-slice_fusion
  43.1 0.1 broadcast_multiply_fusion.1
  43.2 0.2 fusion.21
  43.4 0.3 collective-permute-start.4
  43.6 1.6 %collective-permute-start.5 = (f32[14,256]{1,0:T(8,128)S(1)}, f32[14,256]{1,0:T(8,128)S(1)}, u32[]{:S(2)}, u32[]{:S(2)}) collective-permute-start(f32[14,256]{1,0:T(8,128)S(1)} %get-tuple-element.70), channel_id=1, source_target_pairs={{0,2},{1,3},{2,0},{3,1},{4,6},{5,7},{6,4},{7,5},{8,10},{9,11},{10,... | collective-permute-start | bytes 43016 | tf_op jit(solution)/shard_map/ppermute | solution.py:177
  45.3 1.3 %collective-permute-start.6 = (f32[14,256]{1,0:T(8,128)S(1)}, f32[14,256]{1,0:T(8,128)S(1)}, u32[]{:S(2)}, u32[]{:S(2)}) collective-permute-start(f32[14,256]{1,0:T(8,128)S(1)} %get-tuple-element.69), channel_id=1, source_target_pairs={{0,3},{1,0},{2,1},{3,2},{4,7},{5,4},{6,5},{7,6},{8,11},{9,8},{10,9... | collective-permute-start | bytes 43016 | tf_op jit(solution)/shard_map/ppermute | solution.py:177
  46.6 0.0 collective-permute-done.4
  46.6 0.8 collective-permute-done.5
  47.4 0.6 collective-permute-done.6
  48.0 0.0 collective-permute-done.8
  48.1 0.0 collective-permute-done.7
  48.1 0.2 pad_maximum_fusion.5
  48.3 0.2 fusion.53
  48.4 0.8 fusion.70
  49.2 4.0 %stack.39 = f32[6]{0:T(128)S(1)} concatenate(f32[1]{0:T(128)} %bitcast.39, f32[1]{0:T(128)} %bitcast.40, f32[1]{0:T(128)} %bitcast.41, f32[1]{0:T(128)} %bitcast.42, f32[1]{0:T(128)} %bitcast.43, f32[1]{0:T(128)} %bitcast.44), dimensions={0} | concatenate | bytes 48 | tf_op jit(solution)/shard_map/stack | solution.py:204
  53.2 0.6 broadcast_in_dim.62
  53.8 6.0 %all-to-all-start = ((f32[32,1,128]{2,1,0:T(1,128)}), f32[32,1,128]{2,1,0:T(1,128)S(1)}, u32[]{:S(2)}, u32[]{:S(2)}) async-start(f32[32,1,128]{2,1,0:T(1,128)} %broadcast_in_dim.62), calls=%async_computation | async-start | bytes 32768 | tf_op jit(solution)/shard_map/all_to_all | solution.py:206
  59.9 0.9 slice_bitcast_fusion
  60.7 6.2 %all-to-all-done = f32[32,1,128]{2,1,0:T(1,128)S(1)} async-done(((f32[32,1,128]{2,1,0:T(1,128)}), f32[32,1,128]{2,1,0:T(1,128)S(1)}, u32[]{:S(2)}, u32[]{:S(2)}) %all-to-all-start) | async-done | bytes 16416 | tf_op jit(solution)/shard_map/all_to_all | solution.py:206
  67.0 0.7 fusion.83
  87.5 0.6 multiply_add_fusion.6
  (35 shorter events, 0.4 us)
Async XLA Ops:
  0.6 3.0 %copy-start = (f32[8,32,256]{2,1,0:T(8,128)S(1)}, f32[8,32,256]{2,1,0:T(8,128)}, u32[]{:S(2)}) copy-start(f32[8,32,256]{2,1,0:T(8,128)} %param.14) | copy-start | bytes 786436
  0.6 3.1 %copy-start.1 = (f32[8,32,256]{2,1,0:T(8,128)S(1)}, f32[8,32,256]{2,1,0:T(8,128)}, u32[]{:S(2)}) copy-start(f32[8,32,256]{2,1,0:T(8,128)} %param.15) | copy-start | bytes 786436
  0.7 3.1 %copy-start.2 = (f32[8,32,256]{2,1,0:T(8,128)S(1)}, f32[8,32,256]{2,1,0:T(8,128)}, u32[]{:S(2)}) copy-start(f32[8,32,256]{2,1,0:T(8,128)} %param.16) | copy-start | bytes 786436
  0.7 3.1 %copy-start.4 = (f32[2,32,256]{2,1,0:T(8,128)S(1)}, f32[2,32,256]{2,1,0:T(8,128)}, u32[]{:S(2)}) copy-start(f32[2,32,256]{2,1,0:T(8,128)} %param.17) | copy-start | bytes 196612
  0.7 3.1 %copy-start.5 = (s32[32,256]{1,0:T(8,128)S(1)}, s32[32,256]{1,0:T(8,128)}, u32[]{:S(2)}) copy-start(s32[32,256]{1,0:T(8,128)} %param.18) | copy-start | bytes 98308
  4.1 5.5 %copy-start.3 = (f32[8,1024]{1,0:T(8,128)S(1)}, f32[8,1024]{1,0:T(8,128)}, u32[]{:S(2)}) copy-start(f32[8,1024]{1,0:T(8,128)} %param.19) | copy-start | bytes 98308
  4.7 11.5 %collective-permute-start.1 = (f32[51,32,1]{0,1,2:T(8,128)S(1)}, f32[51,32,1]{0,1,2:T(8,128)S(1)}, u32[]{:S(2)}, u32[]{:S(2)}) collective-permute-start(f32[51,32,1]{0,1,2:T(8,128)S(1)} %copy.61), channel_id=1, source_target_pairs={{1,0},{2,1},{3,2},{5,4},{6,5},{7,6},{9,8},{10,9},{11,10},{13,12},{... | collective-permute-start | bytes 19592 | tf_op jit(solution)/shard_map/ppermute | solution.py:24
  6.6 10.5 %collective-permute-start = (f32[51,32,1]{0,1,2:T(8,128)S(1)}, f32[51,32,1]{0,1,2:T(8,128)S(1)}, u32[]{:S(2)}, u32[]{:S(2)}) collective-permute-start(f32[51,32,1]{0,1,2:T(8,128)S(1)} %copy.60), channel_id=1, source_target_pairs={{0,1},{1,2},{2,3},{4,5},{5,6},{6,7},{8,9},{9,10},{10,11},{12,13},{... | collective-permute-start | bytes 19592 | tf_op jit(solution)/shard_map/ppermute | solution.py:22
  9.7 38.4 %collective-permute-start.8 = (f32[2,1024]{1,0:T(2,128)S(1)}, f32[2,1024]{1,0:T(2,128)S(1)}, u32[]{:S(2)}, u32[]{:S(2)}) collective-permute-start(f32[2,1024]{1,0:T(2,128)S(1)} %get-tuple-element.73), channel_id=1, source_target_pairs={{1,0},{2,1},{3,2},{4,3},{5,4},{6,5},{7,6},{8,7},{9,8},{10,9},{11,1... | collective-permute-start | bytes 24584 | tf_op jit(solution)/shard_map/ppermute | solution.py:189
  10.9 37.1 %collective-permute-start.7 = (f32[2,1024]{1,0:T(2,128)S(1)}, f32[2,1024]{1,0:T(2,128)S(1)}, u32[]{:S(2)}, u32[]{:S(2)}) collective-permute-start(f32[2,1024]{1,0:T(2,128)S(1)} %get-tuple-element.72), channel_id=1, source_target_pairs={{0,1},{1,2},{2,3},{3,4},{4,5},{5,6},{6,7},{7,8},{8,9},{9,10},{10,1... | collective-permute-start | bytes 24584 | tf_op jit(solution)/shard_map/ppermute | solution.py:187
  18.4 11.4 %collective-permute-start.3 = (f32[51,4,258]{2,1,0:T(4,128)S(1)}, f32[51,4,258]{2,1,0:T(4,128)S(1)}, u32[]{:S(2)}, u32[]{:S(2)}) collective-permute-start(f32[51,4,258]{2,1,0:T(4,128)S(1)} %get-tuple-element.43), channel_id=1, source_target_pairs={{4,0},{8,4},{12,8},{16,12},{20,16},{24,20},{28,24},{5,1},{9,5},{13... | collective-permute-start | bytes 631592 | tf_op jit(solution)/shard_map/ppermute | solution.py:24
  19.7 17.5 %collective-permute-start.2 = (f32[51,4,258]{2,1,0:T(4,128)S(1)}, f32[51,4,258]{2,1,0:T(4,128)S(1)}, u32[]{:S(2)}, u32[]{:S(2)}) collective-permute-start(f32[51,4,258]{2,1,0:T(4,128)S(1)} %get-tuple-element.42), channel_id=1, source_target_pairs={{0,4},{4,8},{8,12},{12,16},{16,20},{20,24},{24,28},{1,5},{5,9},{9,... | collective-permute-start | bytes 631592 | tf_op jit(solution)/shard_map/ppermute | solution.py:22
  43.4 3.2 %collective-permute-start.4 = (f32[14,256]{1,0:T(8,128)S(1)}, f32[14,256]{1,0:T(8,128)S(1)}, u32[]{:S(2)}, u32[]{:S(2)}) collective-permute-start(f32[14,256]{1,0:T(8,128)S(1)} %get-tuple-element.71), channel_id=1, source_target_pairs={{0,1},{1,2},{2,3},{3,0},{4,5},{5,6},{6,7},{7,4},{8,9},{9,10},{10,1... | collective-permute-start | bytes 43016 | tf_op jit(solution)/shard_map/ppermute | solution.py:177
  43.6 3.7 %collective-permute-start.5 = (f32[14,256]{1,0:T(8,128)S(1)}, f32[14,256]{1,0:T(8,128)S(1)}, u32[]{:S(2)}, u32[]{:S(2)}) collective-permute-start(f32[14,256]{1,0:T(8,128)S(1)} %get-tuple-element.70), channel_id=1, source_target_pairs={{0,2},{1,3},{2,0},{3,1},{4,6},{5,7},{6,4},{7,5},{8,10},{9,11},{10,... | collective-permute-start | bytes 43016 | tf_op jit(solution)/shard_map/ppermute | solution.py:177
  45.3 2.8 %collective-permute-start.6 = (f32[14,256]{1,0:T(8,128)S(1)}, f32[14,256]{1,0:T(8,128)S(1)}, u32[]{:S(2)}, u32[]{:S(2)}) collective-permute-start(f32[14,256]{1,0:T(8,128)S(1)} %get-tuple-element.69), channel_id=1, source_target_pairs={{0,3},{1,0},{2,1},{3,2},{4,7},{5,4},{6,5},{7,6},{8,11},{9,8},{10,9... | collective-permute-start | bytes 43016 | tf_op jit(solution)/shard_map/ppermute | solution.py:177
  53.8 13.1 %all-to-all-start = ((f32[32,1,128]{2,1,0:T(1,128)}), f32[32,1,128]{2,1,0:T(1,128)S(1)}, u32[]{:S(2)}, u32[]{:S(2)}) async-start(f32[32,1,128]{2,1,0:T(1,128)} %broadcast_in_dim.62), calls=%async_computation | async-start | bytes 32768 | tf_op jit(solution)/shard_map/all_to_all | solution.py:206

commit v2 on v0

v2 whole, which is shorter than its diff:
```python
import functools
import math

import jax
import jax.numpy as jnp
from jax import lax
from jax.experimental import pallas as pl
from jax.experimental.pallas import tpu as pltpu
from jax.sharding import PartitionSpec as P

ITERS = 3
CENTRE = 4.5
SCALE = 4.5
DEEP = ITERS + 1
SUB = 8
LANE = 128
PAIRS = ((0, 0), (0, 1), (1, 1), (1, 2), (2, 2), (2, 3))


def iota(shape, dim):
    return lax.broadcasted_iota(jnp.int32, shape, dim)


def below(x):
    return pltpu.roll(x, x.shape[0] - 1, 0)


def above(x):
    return pltpu.roll(x, 1, 0)


def left_by(x, lanes):
    return pltpu.roll(x, x.shape[1] - lanes, 1)


def pack_edges(lo_t, lo_s, lo_d, hi_t, hi_s, hi_v, hi_y, hi_d, first_ref, even_ref, odd_ref):
    layers, rows, _ = lo_t.shape
    cells = 2 * layers
    lane = iota((rows, LANE), 1)

    def put(total, where, column):
        return jnp.where(where, column, total)

    first = jnp.zeros((rows, LANE), jnp.float32)
    last = jnp.zeros((rows, LANE), jnp.float32)
    edge = LANE - 1
    for k in range(layers):
        first = put(first, lane == k, lo_t[k][:, 0:1])
        first = put(first, lane == layers + k, lo_s[k][:, 0:1])
        last = put(last, lane == k, hi_t[k][:, edge:])
        last = put(last, lane == layers + k, hi_s[k][:, edge:])
        two = (lane == cells + k) | (lane == cells + layers + k)
        last = put(last, two, hi_v[k][:, edge:])
        two = (lane == 2 * cells + k) | (lane == 2 * cells + layers + k)
        last = put(last, two, hi_y[k][:, edge:])
    span = (lane >= 3 * cells) & (lane < 4 * cells)
    first = put(first, span, lo_d[:, 0:1].astype(jnp.float32))
    last = put(last, span, hi_d[:, edge:].astype(jnp.float32))
    first_ref[...] = first
    even = lax.axis_index("by") % 2 == 0
    even_ref[...] = jnp.where(even, last, first)
    odd_ref[...] = jnp.where(even, first, last)


def pack_rows(*refs):
    tops, bottoms, (even_ref, odd_ref) = refs[:8], refs[8:16], refs[16:]

    def flat(group):
        planes = []
        for ref in group[:7]:
            planes += [ref[k] for k in range(ref.shape[0])]
        planes.append(group[7][...].astype(jnp.float32))
        planes.append(planes[-1])
        return planes

    even = lax.axis_index("bx") % 2 == 0
    tops, bottoms = flat(tops), flat(bottoms)
    upper = iota(tops[0].shape, 0) < DEEP
    for q in range(len(tops) // 2):
        up = jnp.where(upper, tops[2 * q], pltpu.roll(tops[2 * q + 1], DEEP, 0))
        down = jnp.where(upper, pltpu.roll(bottoms[2 * q], DEEP, 0), bottoms[2 * q + 1])
        even_ref[q] = jnp.where(even, down, up)
        odd_ref[q] = jnp.where(even, up, down)


def join_edges(first_ref, from_even, from_odd, even_in, odd_in, edge_ref, even_ref, odd_ref):
    rows = first_ref.shape[0]
    half = LANE // 2
    even = lax.axis_index("by") % 2 == 0
    lane = iota((rows, LANE), 1)
    a, b = from_even[...], from_odd[...]
    left = jnp.where(even, b, a)
    right = jnp.where(even, a, b)
    left = jnp.where(lane < half, left, pltpu.roll(first_ref[...], half, 1))
    edge_ref[:, :LANE] = left
    edge_ref[:, LANE:] = right
    even = lax.axis_index("bx") % 2 == 0
    upper = iota((SUB, 2 * LANE), 0) < DEEP
    up = pltpu.roll(edge_ref[:SUB, :], DEEP, 0)
    down = edge_ref[rows - SUB :, :]
    even_ref[0] = jnp.where(upper, even_in[0], jnp.where(even, down, up))
    odd_ref[0] = jnp.where(upper, odd_in[0], jnp.where(even, up, down))


def tile_step(get, source, depth, edge, layers):
    rows, columns = depth.shape
    cells = 2 * layers
    lane = iota((rows, columns), 1)
    first, last = lane == 0, lane == columns - 1

    def after(x, fill):
        return jnp.where(last, fill, left_by(x, 1))

    def before(x, fill):
        return jnp.where(first, fill, pltpu.roll(x, 1, 1))

    level = (iota((rows, LANE), 1) % layers).astype(jnp.float32)
    left, right = edge[:, :LANE], edge[:, LANE:]
    wet_left = level < left_by(left, 3 * cells)
    wet_own = level < left_by(left, LANE // 2 + 3 * cells)
    wet_right = level < left_by(right, 3 * cells)
    cell_left = jnp.where(wet_left, left, 0.0)
    cell_own = jnp.where(wet_own, left_by(left, LANE // 2), 0.0)
    cell_right = jnp.where(wet_right, right, 0.0)
    slope_left = below(cell_left) - above(cell_left)
    slope_own = below(cell_own) - above(cell_own)
    slope_right = below(cell_right) - above(cell_right)
    flux_left = left_by(left, cells) * 0.5 * (cell_left + cell_own) - 0.15 * (
        cell_own - cell_left + left_by(left, 2 * cells) * 0.25 * (slope_left + slope_own)
    )
    flux_left = jnp.where(wet_left & wet_own, flux_left, 0.0)

    depth_right = right[:, 3 * cells : 3 * cells + 1]
    depth_east = jnp.minimum(depth, below(depth))
    depth_north = jnp.minimum(depth, after(depth, depth_right))
    stars = ([], [])
    for k in range(layers):
        wet = depth > k
        mask = depth_east > k
        half = 0.5 * get(2, k)
        e_here = jnp.where(mask, half + 0.15, 0.0)
        e_next = jnp.where(mask, half - 0.15, 0.0)
        e_cross = jnp.where(mask, 0.0375 * get(4, k), 0.0)
        mask = depth_north > k
        half = 0.5 * get(3, k)
        n_here = jnp.where(mask, half + 0.15, 0.0)
        n_next = jnp.where(mask, half - 0.15, 0.0)
        n_cross = jnp.where(mask, 0.0375 * get(5, k), 0.0)
        for t in range(2):
            one = slice(t * layers + k, t * layers + k + 1)
            cell = jnp.where(wet, get(t, k), 0.0)
            east, west = below(cell), above(cell)
            north = after(cell, cell_right[:, one])
            south = before(cell, cell_left[:, one])
            cross = north - south
            flux = e_here * cell + e_next * east - e_cross * (cross + below(cross))
            star = cell - (flux - above(flux))
            cross = east - west
            cross = cross + after(cross, slope_right[:, one])
            flux = n_here * cell + n_next * north - n_cross * cross
            star = star - (flux - before(flux, flux_left[:, one]))
            if k == 0:
                star = star + source[t]
            stars[t].append(jnp.where(wet, star, 0.0))
    primes, rights = [], ([], [])
    upper = None
    density = 0.8 * stars[1][0] - 0.2 * stars[0][0]
    for k in range(layers):
        if k + 1 < layers:
            deeper = 0.8 * stars[1][k + 1] - 0.2 * stars[0][k + 1]
            couple = 0.05 + 1.0 / (1.0 + 10.0 * jnp.maximum(deeper - density, 0.0))
            couple = jnp.where(depth > k + 1, couple, 0.0)
            density = deeper
        else:
            couple = None
        if k == 0:
            inverse = 1.0 / (1.0 + couple)
        elif couple is not None:
            inverse = 1.0 / (1.0 + upper + couple - upper * primes[-1])
        else:
            inverse = 1.0 / (1.0 + upper - upper * primes[-1])
        for t in range(2):
            value = stars[t][k]
            if k:
                value = value + upper * rights[t][-1]
            rights[t].append(value * inverse)
        if couple is not None:
            primes.append(couple * inverse)
        upper = couple
    fresh = ([None] * layers, [None] * layers)
    forcing = None
    solved = [rights[0][-1], rights[1][-1]]
    for k in range(layers - 1, -1, -1):
        wet = depth > k
        for t in range(2):
            if k < layers - 1:
                solved[t] = rights[t][k] + primes[k] * solved[t]
            fresh[t][k] = jnp.where(wet, solved[t], 0.0)
        part = 0.8 * fresh[1][k] - 0.2 * fresh[0][k]
        forcing = part if forcing is None else forcing + part
    return fresh[0], fresh[1], forcing * (4.0 / math.sqrt(layers))


def inner_tile(t, s, u, v, x, y, source, depth, edge, t_out, s_out, f_out):
    layers = t.shape[0]
    refs = (t, s, u, v, x, y)
    warm, salt, forcing = tile_step(
        lambda kind, k: refs[kind][k],
        [source[0], source[1]],
        depth[...].astype(jnp.float32),
        edge[...],
        layers,
    )
    for k in range(layers):
        t_out[k] = warm[k]
        s_out[k] = salt[k]
    f_out[...] = forcing


def rim_rows(across, even_out, odd_out, even_in, odd_in, t_old, s_old, f_old, *refs):
    t_new, s_new = refs[0], refs[1]
    sends, (field, blocks) = refs[2 : 2 + across], refs[2 + across :]
    layers = t_old.shape[0]
    rows = f_old.shape[0]
    strip = rows // across
    step = pl.program_id(0)
    top = step == 0
    even = lax.axis_index("bx") % 2 == 0
    use_odd = top == even
    shape = (SUB, f_old.shape[1])
    upper = iota(shape, 0) < DEEP
    planes = []
    for q in range(even_out.shape[0]):
        sent = jnp.where(use_odd, odd_out[q], even_out[q])
        came = jnp.where(use_odd, odd_in[q], even_in[q])
        low = jnp.where(top, came, sent)
        high = jnp.where(top, sent, came)
        planes.append(jnp.where(upper, low, pltpu.roll(high, DEEP, 0)))
        planes.append(jnp.where(upper, pltpu.roll(low, DEEP, 0), high))
    order = (0, 1, 2, 3, 4, 5)
    base = 6 * layers
    warm, salt, forcing = tile_step(
        lambda kind, k: planes[order[kind] * layers + k],
        [planes[base], planes[base + 1]],
        planes[base + 2],
        planes[base + 3],
        layers,
    )
    target = jnp.where(top, 0, SUB - 1)
    mine = iota(shape, 0) == target
    for k in range(layers):
        t_new[k] = jnp.where(mine, pltpu.roll(warm[k], DEEP, 0), t_old[k])
        s_new[k] = jnp.where(mine, pltpu.roll(salt[k], DEEP, 0), s_old[k])
    moved = pltpu.roll(forcing, DEEP, 0)

    @pl.when(top)
    def _():
        field[SUB : SUB + rows, :] = f_old[...]
        field[:SUB, :] = moved
        field[SUB : 2 * SUB, :] = jnp.where(mine, moved, f_old[:SUB, :])

    @pl.when(jnp.logical_not(top))
    def _():
        field[SUB + rows : 2 * SUB + rows, :] = moved
        field[rows : rows + SUB, :] = jnp.where(mine, moved, field[rows : rows + SUB, :])
        tall = blocks.shape[1]
        for peer in range(across):
            start = SUB - ITERS + peer * strip
            stop = min(start + tall, field.shape[0])
            blocks[peer, : stop - start, :] = field[start:stop, :]
        me = lax.axis_index("by")
        for hop in range(across):
            sends[hop][...] = blocks[hop_peer(me, hop, across)]


def hop_peer(me, hop, count):
    if count & (count - 1) == 0:
        return me ^ hop
    return (me + hop) % count


def hop_origin(me, hop, count):
    if count & (count - 1) == 0:
        return me ^ hop
    return (me + count - hop) % count


def powers(across, along, *refs):
    came = refs[:across]
    main_up, main_own, main_down = refs[across : across + 3]
    basis_ref, row_ref, field, main = refs[across + 3 :]
    strip, columns = main_own.shape
    width = columns // across
    tall = field.shape[0]
    me = lax.axis_index("by")
    for hop in range(across):
        origin = hop_origin(me, hop, across)
        field[:, pl.ds(pl.multiple_of(origin * width, LANE), width)] = came[hop][...]
    wide = ITERS - 1
    main[...] = jnp.zeros(main.shape, jnp.float32)
    main[ITERS - wide : ITERS, :] = main_up[...]
    main[ITERS : ITERS + strip, :] = main_own[...]
    main[ITERS + strip : ITERS + strip + wide, :] = main_down[...]
    shape = (tall, columns)
    lane = iota(shape, 1)
    line = (lax.axis_index("bx") * across + me) * strip - ITERS + iota(shape, 0)
    inside = (line >= 0) & (line < along * across * strip)
    first, last = lane == 0, lane == columns - 1
    centre = (main[...] + (6.0 - CENTRE)) * (1.0 / SCALE)
    centre = jnp.where(inside, centre, 0.0)
    share = jnp.where(inside, -1.0 / SCALE, 0.0)
    now = field[...]
    own = [now[ITERS : ITERS + strip]]
    for _ in range(ITERS):
        beside = below(now) + above(now)
        spread = now + 0.5 * beside
        east = jnp.where(last, 0.0, left_by(spread, 1))
        west = jnp.where(first, 0.0, pltpu.roll(spread, 1, 1))
        now = centre * now + share * (beside + east + west)
        own.append(now[ITERS : ITERS + strip])
    for k in range(ITERS):
        basis_ref[k] = own[k]
    place = iota((1, LANE), 1)
    row = jnp.zeros((1, LANE), jnp.float32)
    for k, (i, j) in enumerate(PAIRS):
        part = jnp.sum(own[i] * own[j], axis=0, keepdims=True)
        row = jnp.where(place == k, jnp.sum(part, axis=1, keepdims=True), row)
    row_ref[...] = jnp.broadcast_to(row[None], row_ref.shape)


def coefficients(moments):
    def inner(a, b):
        return sum(x * y * moments[i + j] for i, x in enumerate(a) for j, y in enumerate(b))

    zero = jnp.zeros_like(moments[0])
    resid = [zero + 1.0]
    direction = [zero + 1.0]
    total = [zero] * ITERS
    norm_now = inner(resid, resid)
    for step in range(ITERS):
        image = [zero] * (len(direction) + 1)
        for i, x in enumerate(direction):
            image[i] = image[i] + CENTRE * x
            image[i + 1] = image[i + 1] + SCALE * x
        alpha = norm_now / inner(direction, image)
        for i, x in enumerate(direction):
            total[i] = total[i] + alpha * x
        if step + 1 < ITERS:
            resid = [r - alpha * q for r, q in zip(resid + [zero], image)]
            norm_next = inner(resid, resid)
            beta = norm_next / norm_now
            direction = [r + beta * p for r, p in zip(resid, direction + [zero])]
            norm_now = norm_next
    return total


def combine(rows_ref, basis_ref, out_ref):
    moments = jnp.sum(rows_ref[...], axis=0)
    total = coefficients([moments[:, k : k + 1] for k in range(len(PAIRS))])
    out_ref[...] = total[0] * basis_ref[0] + total[1] * basis_ref[1] + total[2] * basis_ref[2]


def shape_of(*dims):
    return jax.ShapeDtypeStruct(dims, jnp.float32)


def whole(x):
    return pl.BlockSpec(x.shape, lambda *_: (0,) * len(x.shape))


def block(shape, *index):
    return pl.BlockSpec(shape, lambda *_: index)


def pairs(count, start):
    both = [(i, i + 1) for i in range(start, count - 1, 2)]
    return both + [(b, a) for a, b in both]


def local(t, s, u, v, x, y, source, depth, main):
    layers, rows, columns = t.shape
    across, along = lax.axis_size("by"), lax.axis_size("bx")
    strip = rows // across
    params = pltpu.CompilerParams(vmem_limit_bytes=48 << 20)

    call = functools.partial(pl.pallas_call, compiler_params=params)

    stack = (layers, rows, LANE)
    end = columns // LANE - 1
    pack = shape_of(rows, LANE)
    lo, hi = block(stack, 0, 0, 0), block(stack, 0, 0, end)
    lo_d, hi_d = block((rows, LANE), 0, 0), block((rows, LANE), 0, end)
    first, even, odd = call(
        pack_edges,
        grid=(1,),
        in_specs=[lo, lo, lo_d, hi, hi, hi, hi, hi_d],
        out_specs=[whole(pack)] * 3,
        out_shape=[pack] * 3,
    )(t, s, depth, t, s, v, y, depth)
    from_even = lax.ppermute(even, "by", pairs(across, 0))
    from_odd = lax.ppermute(odd, "by", pairs(across, 1))

    fields = (t, s, u, v, x, y, source)
    deep = [(f.shape[0], SUB, columns) for f in fields]
    foot = rows // SUB - 1
    count = (6 * layers + 4) // 2
    rim = shape_of(count, SUB, columns)
    even, odd = call(
        pack_rows,
        grid=(1,),
        in_specs=[block(d, 0, 0, 0) for d in deep]
        + [block((SUB, columns), 0, 0)]
        + [block(d, 0, foot, 0) for d in deep]
        + [block((SUB, columns), foot, 0)],
        out_specs=[whole(rim)] * 2,
        out_shape=[rim] * 2,
    )(*fields, depth, *fields, depth)

    plane = shape_of(rows, columns)
    tail = block((1, SUB, columns), count - 1, 0, 0)
    edge, even, odd = call(
        join_edges,
        grid=(1,),
        in_specs=[whole(pack)] * 3 + [tail] * 2,
        out_specs=[block((rows, 2 * LANE), 0, 0), tail, tail],
        out_shape=[shape_of(rows, 2 * LANE), rim, rim],
        input_output_aliases={3: 1, 4: 2},
    )(first, from_even, from_odd, even, odd)
    odd_in = lax.ppermute(odd, "bx", pairs(along, 1))
    even_in = lax.ppermute(even, "bx", pairs(along, 0))

    cube = shape_of(layers, rows, columns)
    args = (*fields, depth, edge)
    warm, salt, forcing = call(
        inner_tile,
        grid=(1,),
        in_specs=[whole(a) for a in args],
        out_specs=[whole(cube), whole(cube), whole(plane)],
        out_shape=[cube, cube, plane],
    )(*args)

    ends = across * along - 1
    names = ("bx", "by")
    wide = ITERS - 1
    main_up = lax.ppermute(main[-wide:], names, [(i, i + 1) for i in range(ends)])
    main_down = lax.ppermute(main[:wide], names, [(i + 1, i) for i in range(ends)])

    tall = -(-(strip + 2 * ITERS) // SUB) * SUB
    part = shape_of(tall, columns)
    touched = pl.BlockSpec((layers, SUB, columns), lambda i: (0, i * foot, 0))
    warm, salt, *sends = call(
        functools.partial(rim_rows, across),
        grid=(2,),
        in_specs=[whole(rim)] * 4 + [touched, touched, whole(plane)],
        out_specs=[touched, touched] + [whole(part)] * across,
        out_shape=[cube, cube] + [part] * across,
        input_output_aliases={4: 0, 5: 1},
        scratch_shapes=[
            pltpu.VMEM((rows + 2 * SUB, columns), jnp.float32),
            pltpu.VMEM((across, tall, columns), jnp.float32),
        ],
    )(even, odd, even_in, odd_in, warm, salt, forcing)

    came = [sends[0]]
    for hop in range(1, across):
        route = [(i, hop_peer(i, hop, across)) for i in range(across)]
        came.append(lax.ppermute(sends[hop], "by", route))

    basis_shape = shape_of(ITERS, strip, columns * across)
    row_shape = shape_of(ends + 1, 1, LANE)
    args = (*came, main_up, main, main_down)
    basis, row = call(
        functools.partial(powers, across, along),
        grid=(1,),
        in_specs=[whole(a) for a in args],
        out_specs=[whole(basis_shape), whole(row_shape)],
        out_shape=[basis_shape, row_shape],
        scratch_shapes=[pltpu.VMEM((tall, columns * across), jnp.float32)] * 2,
    )(*args)
    gathered = lax.all_to_all(row, names, 0, 0, tiled=True)
    result = shape_of(strip, columns * across)
    pressure = call(
        combine,
        grid=(1,),
        in_specs=[whole(gathered), whole(basis)],
        out_specs=whole(result),
        out_shape=result,
    )(gathered, basis)
    return warm, salt, pressure


def solution(mesh):
    tile = P(None, "bx", "by")
    rows = P(("bx", "by"), None)
    return jax.shard_map(
        local,
        mesh=mesh,
        in_specs=(tile,) * 7 + (P("bx", "by"), rows),
        out_specs=(tile, tile, rows),
        check_vma=False,
    )
```

time: 285 us -> 50 us (0.18)
  blocking collectives: 221 us -> 17.8 us
  other arithmetic: 13 us -> 0 us
  local copies, waits for them, and re-layouts: 14.6 us -> 4.59 us
  Pallas kernels: 0 us -> 7.14 us
  between operations: 7.87 us -> 0.77 us
  starting transfers between devices: 24.1 us -> 17.1 us
    psum x5 -> x0, blocking collectives: 214 us -> none  [inner(): return lax.psum(jnp.sum(left_field * right_field), ('bx', 'by'))]
    all_to_all x1, blocking collectives: 7.47 us -> 17.8 us  [local(): gathered = lax.all_to_all(row, names, 0, 0, tiled=True)]
    pallas_call x0 -> x7, Pallas kernels: none -> 7.14 us  [the longest x1 2.88 us: local(): call(inner_tile, grid=(1,), in_specs=[whole(a) for a in args], out_specs=...]
    ppermute x10 -> x9, starting transfers between devices: 24.1 us -> 17.1 us  [the longest x3 8.53 us: local(): came.append(lax.ppermute(sends[hop], 'by', route))]
    another operation x3 -> x0, local copies, waits for them, and re-layouts: 4.53 us -> none  [the longest x2 3.7 us: local(): carried_quantities = jnp.stack([thermal_anomaly, saltiness_anomaly], 0)]
    reduce_sum x7 -> x0, other arithmetic: 4.07 us -> none  [the longest x6 3.92 us: inner(): return lax.psum(jnp.sum(left_field * right_field), ('bx', 'by'))]
    mul x12 -> x0, other arithmetic: 3.8 us -> none  [the longest x1 0.89 us: tendency(): up[:, :-1, 1:-1] * 0.5 * (left + right)]
    slice x10 -> x1, local copies, waits for them, and re-layouts: 3.7 us -> 0.01 us  [local(): main[:wide]]
  transfers between devices with their start and end apart: 10 -> 9, of which waited for: 4 -> 3; matrix products, arithmetic and copies ran while one was open for 1% -> 0% of each run, Pallas kernels for 0% -> 6%
where the time goes in v2:
time: 50 us; the launch traced here: 49.5 us
  blocking collectives  17.8 us (36%)
  starting transfers between devices  17.1 us (34%)
  Pallas kernels  7.14 us (14%)
  local copies, waits for them, and re-layouts  4.59 us (9%)
  waiting for transfers between devices  2.09 us (4%)
  between operations  0.77 us (2%)
    all_to_all x1, blocking collectives, local(): gathered = lax.all_to_all(row, names, 0, 0, tiled=True)  17.8 us
    ppermute x3, starting transfers between devices, local(): came.append(lax.ppermute(sends[hop], 'by', route))  8.53 us
    unnamed x22, local copies, waits for them, and re-layouts  4.58 us
    pallas_call x1, Pallas kernels, local(): call(inner_tile, grid=(1,), in_specs=[whole(a) for a in args], out_specs=...  2.88 us
    ppermute x1, starting transfers between devices, local(): even_in = lax.ppermute(even, 'bx', pairs(along, 0))  2.84 us
    ppermute x1, starting transfers between devices, local(): lax.ppermute(main[-wide:], names, [(i, i + 1) for i in range(ends)])  2.64 us
    pallas_call x1, Pallas kernels, local(): call(functools.partial(rim_rows, across), grid=(2,), in_specs=[whole(rim)...  2.56 us
    ppermute x1, waiting for transfers between devices, local(): lax.ppermute(main[:wide], names, [(i + 1, i) for i in range(ends)])  1.76 us
  transfers between devices with their start and end apart: 9, of which 3 were waited for; matrix products, arithmetic and copies ran while one was open for 0% of the time, Pallas kernels for 6%

profile of v2, /device:TPU:0, one launch (start us, length us, event | category | flops | bytes accessed | tf_op | source)
XLA Modules:
  0.0 49.5 jit_solution(11633213058742553256)
XLA Ops:
  0.6 0.0 copy-start
  0.6 0.9 %copy-done = f32[8,32,256]{2,1,0:T(8,128)S(1)} copy-done((f32[8,32,256]{2,1,0:T(8,128)S(1)}, f32[8,32,256]{2,1,0:T(8,128)}, u32[]{:S(2)}) %copy-start) | copy-done | bytes 262168
  1.6 0.0 copy-start.2
  1.6 0.9 %copy-done.2 = f32[8,32,256]{2,1,0:T(8,128)S(1)} copy-done((f32[8,32,256]{2,1,0:T(8,128)S(1)}, f32[8,32,256]{2,1,0:T(8,128)}, u32[]{:S(2)}) %copy-start.2) | copy-done | bytes 262168
  2.5 0.0 copy-start.4
  2.5 0.9 %copy-done.4 = f32[8,32,256]{2,1,0:T(8,128)S(1)} copy-done((f32[8,32,256]{2,1,0:T(8,128)S(1)}, f32[8,32,256]{2,1,0:T(8,128)}, u32[]{:S(2)}) %copy-start.4) | copy-done | bytes 262168
  3.5 0.0 copy-start.5
  3.5 0.9 %copy-done.5 = f32[8,32,256]{2,1,0:T(8,128)S(1)} copy-done((f32[8,32,256]{2,1,0:T(8,128)S(1)}, f32[8,32,256]{2,1,0:T(8,128)}, u32[]{:S(2)}) %copy-start.5) | copy-done | bytes 262168
  4.4 0.0 copy-start.8
  4.4 0.8 %copy-done.8 = s32[32,256]{1,0:T(8,128)S(1)} copy-done((s32[32,256]{1,0:T(8,128)S(1)}, s32[32,256]{1,0:T(8,128)}, u32[]{:S(2)}) %copy-start.8) | copy-done | bytes 32792
  5.2 0.0 copy-start.6
  5.2 0.0 copy-start.7
  5.2 0.0 copy-start.9
  5.2 0.3 shard_map.112
  5.5 0.5 %collective-permute-start = (f32[32,128]{1,0:T(8,128)S(1)}, f32[32,128]{1,0:T(8,128)S(1)}, u32[]{:S(2)}, u32[]{:S(2)}) collective-permute-start(f32[32,128]{1,0:T(8,128)S(1)} %get-tuple-element.23), channel_id=1, source_target_pairs={{0,1},{2,3},{1,0},{3,2},{4,5},{6,7},{5,4},{7,6},{8,9},{10,11},{9,8... | collective-permute-start | bytes 49160 | tf_op jit(solution)/shard_map/ppermute | solution.py:400
  6.0 0.7 %collective-permute-start.1 = (f32[32,128]{1,0:T(8,128)S(1)}, f32[32,128]{1,0:T(8,128)S(1)}, u32[]{:S(2)}, u32[]{:S(2)}) collective-permute-start(f32[32,128]{1,0:T(8,128)S(1)} %get-tuple-element.24), channel_id=1, source_target_pairs={{1,2},{2,1},{5,6},{6,5},{9,10},{10,9},{13,14},{14,13},{17,18},{18,... | collective-permute-start | bytes 49160 | tf_op jit(solution)/shard_map/ppermute | solution.py:401
  6.7 0.0 copy-done.6
  6.7 0.0 copy-done.7
  6.7 0.0 copy-done.9
  6.7 0.0 copy-start.3
  6.7 0.1 shard_map.113
  6.8 0.0 copy-start.1
  6.8 0.1 collective-permute-done.from_even
  6.9 0.0 collective-permute-done.1.from_odd
  6.9 0.1 shard_map.114
  6.9 2.8 %collective-permute-start.2 = (f32[26,8,256]{2,1,0:T(8,128)S(1)}, f32[26,8,256]{2,1,0:T(8,128)S(1)}, u32[]{:S(2)}, u32[]{:S(2)}) collective-permute-start(f32[26,8,256]{2,1,0:T(8,128)S(1)} %get-tuple-element.27.even_out), channel_id=1, source_target_pairs={{0,4},{8,12},{16,20},{24,28},{4,0},{12,8},{20,16},{28,24},{1,5},{9... | collective-permute-start | bytes 638984 | tf_op jit(solution)/shard_map/ppermute | solution.py:430
  9.8 0.7 %collective-permute-start.3 = (f32[26,8,256]{2,1,0:T(8,128)S(1)}, f32[26,8,256]{2,1,0:T(8,128)S(1)}, u32[]{:S(2)}, u32[]{:S(2)}) collective-permute-start(f32[26,8,256]{2,1,0:T(8,128)S(1)} %get-tuple-element.28.odd_out), channel_id=1, source_target_pairs={{4,8},{12,16},{20,24},{8,4},{16,12},{24,20},{5,9},{13,17},{21,25},... | collective-permute-start | bytes 638984 | tf_op jit(solution)/shard_map/ppermute | solution.py:429
  10.5 0.0 copy-done.3
  10.5 0.0 copy-done.1
  10.5 2.9 %shard_map.115 = (f32[8,32,256]{2,1,0:T(8,128)}, f32[8,32,256]{2,1,0:T(8,128)}, f32[32,256]{1,0:T(8,128)S(1)}) custom-call(f32[8,32,256]{2,1,0:T(8,128)S(1)} %copy-done.1, f32[8,32,256]{2,1,0:T(8,128)S(1)} %copy-done.3, f32[8,32,256]{2,1,0:T(8,128)S(1)} %copy-done.6, f32[8,32,256]{2,1,0:T(8,128)S(1)} %copy-done.4, f32[8,32,256]{2,1,0:T(8,128)S(1)} %copy-done.7, ...), custom_call_target="tpu_custom_call" | custom-call | tf_op jit(solution)/shard_map/pallas_call | solution.py:434
  13.4 0.3 collective-permute-done.2.even_in
  13.6 0.0 collective-permute-done.3.odd_in
  13.6 0.0 copy-start.10
  13.6 2.6 %shard_map.116 = (f32[8,32,256]{2,1,0:T(8,128)}, f32[8,32,256]{2,1,0:T(8,128)}, f32[16,256]{1,0:T(8,128)S(1)}, f32[16,256]{1,0:T(8,128)S(1)}, f32[16,256]{1,0:T(8,128)S(1)}, /*index=5*/f32[16,256]{1,0:T(8,128)S(1)}) custom-call(f32[26,8,256]{2,1,0:T(8,128)S(1)} %get-tuple-element.27.even_out, ...), custom_call_target="tpu_custom_call", output_to_operand_aliasing={{0}: (4, {}), {1}: (5, {})} | custom-call | tf_op jit(solution)/shard_map/pallas_call | solution.py:451
  16.2 7.1 %collective-permute-start.4 = (f32[16,256]{1,0:T(8,128)S(1)}, f32[16,256]{1,0:T(8,128)S(1)}, u32[]{:S(2)}, u32[]{:S(2)}) collective-permute-start(f32[16,256]{1,0:T(8,128)S(1)} %get-tuple-element.36), channel_id=1, source_target_pairs={{0,1},{1,0},{2,3},{3,2},{4,5},{5,4},{6,7},{7,6},{8,9},{9,8},{10,11... | collective-permute-start | bytes 49160 | tf_op jit(solution)/shard_map/ppermute | solution.py:467
  23.3 0.0 collective-permute-start.5
  23.3 1.4 %collective-permute-start.6 = (f32[16,256]{1,0:T(8,128)S(1)}, f32[16,256]{1,0:T(8,128)S(1)}, u32[]{:S(2)}, u32[]{:S(2)}) collective-permute-start(f32[16,256]{1,0:T(8,128)S(1)} %get-tuple-element.38), channel_id=1, source_target_pairs={{0,3},{1,2},{2,1},{3,0},{4,7},{5,6},{6,5},{7,4},{8,11},{9,10},{10,... | collective-permute-start | bytes 49160 | tf_op jit(solution)/shard_map/ppermute | solution.py:467
  24.7 0.0 copy-done.10
  24.7 2.6 %collective-permute-start.7 = (f32[2,1024]{1,0:T(2,128)S(1)}, f32[2,1024]{1,0:T(2,128)S(1)}, u32[]{:S(2)}, u32[]{:S(2)}) collective-permute-start(f32[2,1024]{1,0:T(2,128)S(1)} %get-tuple-element.42), channel_id=1, source_target_pairs={{0,1},{1,2},{2,3},{3,4},{4,5},{5,6},{6,7},{7,8},{8,9},{9,10},{10,1... | collective-permute-start | bytes 24584 | tf_op jit(solution)/shard_map/ppermute | solution.py:445
  27.4 1.3 %collective-permute-start.8 = (f32[2,1024]{1,0:T(2,128)S(1)}, f32[2,1024]{1,0:T(2,128)S(1)}, u32[]{:S(2)}, u32[]{:S(2)}) collective-permute-start(f32[2,1024]{1,0:T(2,128)S(1)} %get-tuple-element.41), channel_id=1, source_target_pairs={{1,0},{2,1},{3,2},{4,3},{5,4},{6,5},{7,6},{8,7},{9,8},{10,9},{11,1... | collective-permute-start | bytes 24584 | tf_op jit(solution)/shard_map/ppermute | solution.py:446
  28.7 0.0 collective-permute-done.7.refs_4_
  28.7 1.8 %collective-permute-done.8.refs_6_ = f32[2,1024]{1,0:T(2,128)S(1)} collective-permute-done((f32[2,1024]{1,0:T(2,128)S(1)}, f32[2,1024]{1,0:T(2,128)S(1)}, u32[]{:S(2)}, u32[]{:S(2)}) %collective-permute-start.8) | collective-permute-done | bytes 8224 | tf_op jit(solution)/shard_map/ppermute | solution.py:446
  30.4 0.0 collective-permute-done.4.refs_1_
  30.4 0.0 collective-permute-done.5.refs_2_
  30.4 0.0 collective-permute-done.6.refs_3_
  30.5 0.4 shard_map.117
  30.9 17.8 %all_to_all.5.rows_ref = f32[32,1,128]{2,1,0:T(1,128)S(1)} all-to-all(f32[32,1,128]{2,1,0:T(1,128)S(1)} %get-tuple-element.39), channel_id=1, replica_groups=mesh['bx'=8,'by'=4] {'bx','by'}, dimensions={0} | all-to-all | bytes 32768 | tf_op jit(solution)/shard_map/all_to_all | solution.py:480
  48.7 0.8 %shard_map.118 = f32[8,1024]{1,0:T(8,128)} custom-call(f32[32,1,128]{2,1,0:T(1,128)S(1)} %all_to_all.5.rows_ref, f32[3,8,1024]{2,1,0:T(8,128)S(1)} %get-tuple-element.40.basis_ref), custom_call_target="tpu_custom_call" | custom-call | tf_op jit(solution)/shard_map/pallas_call | solution.py:482
  (1 shorter events, 0.0 us)
Async XLA Ops:
  0.6 1.0 %copy-start = (f32[8,32,256]{2,1,0:T(8,128)S(1)}, f32[8,32,256]{2,1,0:T(8,128)}, u32[]{:S(2)}) copy-start(f32[8,32,256]{2,1,0:T(8,128)} %t.1) | copy-start | bytes 786436
  1.6 0.9 %copy-start.2 = (f32[8,32,256]{2,1,0:T(8,128)S(1)}, f32[8,32,256]{2,1,0:T(8,128)}, u32[]{:S(2)}) copy-start(f32[8,32,256]{2,1,0:T(8,128)} %s.1) | copy-start | bytes 786436
  2.5 0.9 %copy-start.4 = (f32[8,32,256]{2,1,0:T(8,128)S(1)}, f32[8,32,256]{2,1,0:T(8,128)}, u32[]{:S(2)}) copy-start(f32[8,32,256]{2,1,0:T(8,128)} %v.1) | copy-start | bytes 786436
  3.5 0.9 %copy-start.5 = (f32[8,32,256]{2,1,0:T(8,128)S(1)}, f32[8,32,256]{2,1,0:T(8,128)}, u32[]{:S(2)}) copy-start(f32[8,32,256]{2,1,0:T(8,128)} %y.1) | copy-start | bytes 786436
  4.4 0.8 %copy-start.8 = (s32[32,256]{1,0:T(8,128)S(1)}, s32[32,256]{1,0:T(8,128)}, u32[]{:S(2)}) copy-start(s32[32,256]{1,0:T(8,128)} %depth.1) | copy-start | bytes 98308
  5.2 1.5 %copy-start.6 = (f32[8,32,256]{2,1,0:T(8,128)S(1)}, f32[8,32,256]{2,1,0:T(8,128)}, u32[]{:S(2)}) copy-start(f32[8,32,256]{2,1,0:T(8,128)} %u.1) | copy-start | bytes 786436
  5.2 1.5 %copy-start.7 = (f32[8,32,256]{2,1,0:T(8,128)S(1)}, f32[8,32,256]{2,1,0:T(8,128)}, u32[]{:S(2)}) copy-start(f32[8,32,256]{2,1,0:T(8,128)} %x.1) | copy-start | bytes 786436
  5.2 1.5 %copy-start.9 = (f32[2,32,256]{2,1,0:T(8,128)S(1)}, f32[2,32,256]{2,1,0:T(8,128)}, u32[]{:S(2)}) copy-start(f32[2,32,256]{2,1,0:T(8,128)} %source.1) | copy-start | bytes 196612
  5.5 1.4 %collective-permute-start = (f32[32,128]{1,0:T(8,128)S(1)}, f32[32,128]{1,0:T(8,128)S(1)}, u32[]{:S(2)}, u32[]{:S(2)}) collective-permute-start(f32[32,128]{1,0:T(8,128)S(1)} %get-tuple-element.23), channel_id=1, source_target_pairs={{0,1},{2,3},{1,0},{3,2},{4,5},{6,7},{5,4},{7,6},{8,9},{10,11},{9,8... | collective-permute-start | bytes 49160 | tf_op jit(solution)/shard_map/ppermute | solution.py:400
  6.0 0.8 %collective-permute-start.1 = (f32[32,128]{1,0:T(8,128)S(1)}, f32[32,128]{1,0:T(8,128)S(1)}, u32[]{:S(2)}, u32[]{:S(2)}) collective-permute-start(f32[32,128]{1,0:T(8,128)S(1)} %get-tuple-element.24), channel_id=1, source_target_pairs={{1,2},{2,1},{5,6},{6,5},{9,10},{10,9},{13,14},{14,13},{17,18},{18,... | collective-permute-start | bytes 49160 | tf_op jit(solution)/shard_map/ppermute | solution.py:401
  6.7 3.7 %copy-start.3 = (f32[8,32,256]{2,1,0:T(8,128)S(1)}, f32[8,32,256]{2,1,0:T(8,128)}, u32[]{:S(2)}) copy-start(f32[8,32,256]{2,1,0:T(8,128)} %s.1) | copy-start | bytes 786436
  6.8 3.7 %copy-start.1 = (f32[8,32,256]{2,1,0:T(8,128)S(1)}, f32[8,32,256]{2,1,0:T(8,128)}, u32[]{:S(2)}) copy-start(f32[8,32,256]{2,1,0:T(8,128)} %t.1) | copy-start | bytes 786436
  6.9 6.7 %collective-permute-start.2 = (f32[26,8,256]{2,1,0:T(8,128)S(1)}, f32[26,8,256]{2,1,0:T(8,128)S(1)}, u32[]{:S(2)}, u32[]{:S(2)}) collective-permute-start(f32[26,8,256]{2,1,0:T(8,128)S(1)} %get-tuple-element.27.even_out), channel_id=1, source_target_pairs={{0,4},{8,12},{16,20},{24,28},{4,0},{12,8},{20,16},{28,24},{1,5},{9... | collective-permute-start | bytes 638984 | tf_op jit(solution)/shard_map/ppermute | solution.py:430
  9.8 3.8 %collective-permute-start.3 = (f32[26,8,256]{2,1,0:T(8,128)S(1)}, f32[26,8,256]{2,1,0:T(8,128)S(1)}, u32[]{:S(2)}, u32[]{:S(2)}) collective-permute-start(f32[26,8,256]{2,1,0:T(8,128)S(1)} %get-tuple-element.28.odd_out), channel_id=1, source_target_pairs={{4,8},{12,16},{20,24},{8,4},{16,12},{24,20},{5,9},{13,17},{21,25},... | collective-permute-start | bytes 638984 | tf_op jit(solution)/shard_map/ppermute | solution.py:429
  13.6 11.1 %copy-start.10 = (f32[8,1024]{1,0:T(8,128)S(1)}, f32[8,1024]{1,0:T(8,128)}, u32[]{:S(2)}) copy-start(f32[8,1024]{1,0:T(8,128)} %refs_5_.3) | copy-start | bytes 98308
  16.2 14.3 %collective-permute-start.4 = (f32[16,256]{1,0:T(8,128)S(1)}, f32[16,256]{1,0:T(8,128)S(1)}, u32[]{:S(2)}, u32[]{:S(2)}) collective-permute-start(f32[16,256]{1,0:T(8,128)S(1)} %get-tuple-element.36), channel_id=1, source_target_pairs={{0,1},{1,0},{2,3},{3,2},{4,5},{5,4},{6,7},{7,6},{8,9},{9,8},{10,11... | collective-permute-start | bytes 49160 | tf_op jit(solution)/shard_map/ppermute | solution.py:467
  23.3 7.1 %collective-permute-start.5 = (f32[16,256]{1,0:T(8,128)S(1)}, f32[16,256]{1,0:T(8,128)S(1)}, u32[]{:S(2)}, u32[]{:S(2)}) collective-permute-start(f32[16,256]{1,0:T(8,128)S(1)} %get-tuple-element.37), channel_id=1, source_target_pairs={{0,2},{1,3},{2,0},{3,1},{4,6},{5,7},{6,4},{7,5},{8,10},{9,11},{10,... | collective-permute-start | bytes 49160 | tf_op jit(solution)/shard_map/ppermute | solution.py:467
  23.3 7.1 %collective-permute-start.6 = (f32[16,256]{1,0:T(8,128)S(1)}, f32[16,256]{1,0:T(8,128)S(1)}, u32[]{:S(2)}, u32[]{:S(2)}) collective-permute-start(f32[16,256]{1,0:T(8,128)S(1)} %get-tuple-element.38), channel_id=1, source_target_pairs={{0,3},{1,2},{2,1},{3,0},{4,7},{5,6},{6,5},{7,4},{8,11},{9,10},{10,... | collective-permute-start | bytes 49160 | tf_op jit(solution)/shard_map/ppermute | solution.py:467
  24.7 4.0 %collective-permute-start.7 = (f32[2,1024]{1,0:T(2,128)S(1)}, f32[2,1024]{1,0:T(2,128)S(1)}, u32[]{:S(2)}, u32[]{:S(2)}) collective-permute-start(f32[2,1024]{1,0:T(2,128)S(1)} %get-tuple-element.42), channel_id=1, source_target_pairs={{0,1},{1,2},{2,3},{3,4},{4,5},{5,6},{6,7},{7,8},{8,9},{9,10},{10,1... | collective-permute-start | bytes 24584 | tf_op jit(solution)/shard_map/ppermute | solution.py:445
  27.4 3.1 %collective-permute-start.8 = (f32[2,1024]{1,0:T(2,128)S(1)}, f32[2,1024]{1,0:T(2,128)S(1)}, u32[]{:S(2)}, u32[]{:S(2)}) collective-permute-start(f32[2,1024]{1,0:T(2,128)S(1)} %get-tuple-element.41), channel_id=1, source_target_pairs={{1,0},{2,1},{3,2},{4,3},{5,4},{6,5},{7,6},{8,7},{9,8},{10,9},{11,1... | collective-permute-start | bytes 24584 | tf_op jit(solution)/shard_map/ppermute | solution.py:446

commit v3 on v2

--- a/solution.py
+++ b/solution.py
@@ -33,37 +33,54 @@
     return pltpu.roll(x, x.shape[1] - lanes, 1)
 
 
-def pack_edges(lo_t, lo_s, lo_d, hi_t, hi_s, hi_v, hi_y, hi_d, first_ref, even_ref, odd_ref):
-    layers, rows, _ = lo_t.shape
+def pack_edges(t, s, v, y, depth, main, first_ref, even_ref, odd_ref, cubes, planes, lines, sems):
+    layers, rows, columns = t.shape
     cells = 2 * layers
+    wide = ITERS - 1
+    head, tail = pl.ds(0, LANE), pl.ds(columns - LANE, LANE)
+    moves = [(t.at[:, :, tail], cubes.at[0]), (s.at[:, :, tail], cubes.at[1])]
+    moves += [(v.at[:, :, tail], cubes.at[2]), (y.at[:, :, tail], cubes.at[3])]
+    moves += [(t.at[:, :, head], cubes.at[4]), (s.at[:, :, head], cubes.at[5])]
+    moves += [(depth.at[:, tail], planes.at[0]), (depth.at[:, head], planes.at[1]), (main, lines)]
+    copies = [pltpu.make_async_copy(a, b, sems.at[i]) for i, (a, b) in enumerate(moves)]
+    for copy in copies:
+        copy.start()
+    for copy in copies:
+        copy.wait()
     lane = iota((rows, LANE), 1)
-
-    def put(total, where, column):
-        return jnp.where(where, column, total)
-
     first = jnp.zeros((rows, LANE), jnp.float32)
     last = jnp.zeros((rows, LANE), jnp.float32)
     edge = LANE - 1
     for k in range(layers):
-        first = put(first, lane == k, lo_t[k][:, 0:1])
-        first = put(first, lane == layers + k, lo_s[k][:, 0:1])
-        last = put(last, lane == k, hi_t[k][:, edge:])
-        last = put(last, lane == layers + k, hi_s[k][:, edge:])
+        first = jnp.where(lane == k, cubes[4, k][:, 0:1], first)
+        first = jnp.where(lane == layers + k, cubes[5, k][:, 0:1], first)
+        last = jnp.where(lane == k, cubes[0, k][:, edge:], last)
+        last = jnp.where(lane == layers + k, cubes[1, k][:, edge:], last)
         two = (lane == cells + k) | (lane == cells + layers + k)
-        last = put(last, two, hi_v[k][:, edge:])
+        last = jnp.where(two, cubes[2, k][:, edge:], last)
         two = (lane == 2 * cells + k) | (lane == 2 * cells + layers + k)
-        last = put(last, two, hi_y[k][:, edge:])
+        last = jnp.where(two, cubes[3, k][:, edge:], last)
     span = (lane >= 3 * cells) & (lane < 4 * cells)
-    first = put(first, span, lo_d[:, 0:1].astype(jnp.float32))
-    last = put(last, span, hi_d[:, edge:].astype(jnp.float32))
+    first = jnp.where(span, planes[1][:, 0:1].astype(jnp.float32), first)
+    last = jnp.where(span, planes[0][:, edge:].astype(jnp.float32), last)
     first_ref[...] = first
     even = lax.axis_index("by") % 2 == 0
-    even_ref[...] = jnp.where(even, last, first)
-    odd_ref[...] = jnp.where(even, first, last)
-
-
-def pack_rows(*refs):
-    tops, bottoms, (even_ref, odd_ref) = refs[:8], refs[8:16], refs[16:]
+    even_ref[:rows, :] = jnp.where(even, last, first)
+    odd_ref[:rows, :] = jnp.where(even, first, last)
+    strip = lines.shape[0]
+    parts = lines.shape[1] // LANE
+    for r in range(wide):
+        for j in range(parts):
+            here = slice(j * LANE, (j + 1) * LANE)
+            up = lines[r : r + 1, here]
+            down = lines[strip - wide + r : strip - wide + r + 1, here]
+            at = rows + r * parts + j
+            even_ref[at : at + 1, :] = jnp.where(even, down, up)
+            odd_ref[at : at + 1, :] = jnp.where(even, up, down)
+
+
+def pack_rows(across, *refs):
+    tops, bottoms, (main, even_ref, odd_ref) = refs[:8], refs[8:16], refs[16:]
 
     def flat(group):
         planes = []
@@ -76,11 +93,23 @@
     even = lax.axis_index("bx") % 2 == 0
     tops, bottoms = flat(tops), flat(bottoms)
     upper = iota(tops[0].shape, 0) < DEEP
-    for q in range(len(tops) // 2):
+    count = len(tops) // 2
+    for q in range(count):
         up = jnp.where(upper, tops[2 * q], pltpu.roll(tops[2 * q + 1], DEEP, 0))
         down = jnp.where(upper, pltpu.roll(bottoms[2 * q], DEEP, 0), bottoms[2 * q + 1])
         even_ref[q] = jnp.where(even, down, up)
         odd_ref[q] = jnp.where(even, up, down)
+    wide = ITERS - 1
+    strip = main.shape[0]
+    width = tops[0].shape[1]
+    for r in range(wide):
+        for j in range(across):
+            here = slice(j * width, (j + 1) * width)
+            up = main[r : r + 1, here]
+            down = main[strip - wide + r : strip - wide + r + 1, here]
+            q, at = divmod(r * across + j, SUB)
+            even_ref[count + q, at : at + 1, :] = jnp.where(even, down, up)
+            odd_ref[count + q, at : at + 1, :] = jnp.where(even, up, down)
 
 
 def join_edges(first_ref, from_even, from_odd, even_in, odd_in, edge_ref, even_ref, odd_ref):
@@ -88,7 +117,7 @@
     half = LANE // 2
     even = lax.axis_index("by") % 2 == 0
     lane = iota((rows, LANE), 1)
-    a, b = from_even[...], from_odd[...]
+    a, b = from_even[:rows, :], from_odd[:rows, :]
     left = jnp.where(even, b, a)
     right = jnp.where(even, a, b)
     left = jnp.where(lane < half, left, pltpu.roll(first_ref[...], half, 1))
@@ -217,60 +246,64 @@
     f_out[...] = forcing
 
 
-def rim_rows(across, even_out, odd_out, even_in, odd_in, t_old, s_old, f_old, *refs):
-    t_new, s_new = refs[0], refs[1]
+def rim_rows(across, even_out, odd_out, even_in, odd_in, f_old, *refs):
+    layers = refs[0].shape[0]
+    t_fix, s_fix = refs[:2]
     sends, (field, blocks) = refs[2 : 2 + across], refs[2 + across :]
-    layers = t_old.shape[0]
     rows = f_old.shape[0]
     strip = rows // across
-    step = pl.program_id(0)
-    top = step == 0
     even = lax.axis_index("bx") % 2 == 0
-    use_odd = top == even
+    me = lax.axis_index("by")
     shape = (SUB, f_old.shape[1])
     upper = iota(shape, 0) < DEEP
     planes = []
-    for q in range(even_out.shape[0]):
-        sent = jnp.where(use_odd, odd_out[q], even_out[q])
-        came = jnp.where(use_odd, odd_in[q], even_in[q])
-        low = jnp.where(top, came, sent)
-        high = jnp.where(top, sent, came)
-        planes.append(jnp.where(upper, low, pltpu.roll(high, DEEP, 0)))
-        planes.append(jnp.where(upper, pltpu.roll(low, DEEP, 0), high))
-    order = (0, 1, 2, 3, 4, 5)
     base = 6 * layers
+    for q in range(base // 2 + 2):
+        sent_even, sent_odd, came_even, came_odd = even_out[q], odd_out[q], even_in[q], odd_in[q]
+        ups = [jnp.where(even, came_odd, came_even), jnp.where(even, sent_odd, sent_even)]
+        downs = [jnp.where(even, sent_even, sent_odd), jnp.where(even, came_even, came_odd)]
+        one = [jnp.where(upper, low, pltpu.roll(high, DEEP, 0)) for low, high in (ups, downs)]
+        two = [jnp.where(upper, pltpu.roll(low, DEEP, 0), high) for low, high in (ups, downs)]
+        planes += [jnp.concatenate(one, 0), jnp.concatenate(two, 0)]
     warm, salt, forcing = tile_step(
-        lambda kind, k: planes[order[kind] * layers + k],
+        lambda kind, k: planes[kind * layers + k],
         [planes[base], planes[base + 1]],
         planes[base + 2],
         planes[base + 3],
         layers,
     )
-    target = jnp.where(top, 0, SUB - 1)
-    mine = iota(shape, 0) == target
-    for k in range(layers):
-        t_new[k] = jnp.where(mine, pltpu.roll(warm[k], DEEP, 0), t_old[k])
-        s_new[k] = jnp.where(mine, pltpu.roll(salt[k], DEEP, 0), s_old[k])
-    moved = pltpu.roll(forcing, DEEP, 0)
-
-    @pl.when(top)
-    def _():
-        field[SUB : SUB + rows, :] = f_old[...]
-        field[:SUB, :] = moved
-        field[SUB : 2 * SUB, :] = jnp.where(mine, moved, f_old[:SUB, :])
-
-    @pl.when(jnp.logical_not(top))
-    def _():
-        field[SUB + rows : 2 * SUB + rows, :] = moved
-        field[rows : rows + SUB, :] = jnp.where(mine, moved, field[rows : rows + SUB, :])
-        tall = blocks.shape[1]
+    for fix, fresh in ((t_fix, warm), (s_fix, salt)):
+        for k in range(layers):
+            fix[k, :SUB, :] = pltpu.roll(fresh[k][:SUB], DEEP, 0)
+            fix[k, SUB:, :] = pltpu.roll(fresh[k][SUB:], DEEP, 0)
+    top = pltpu.roll(forcing[:SUB], DEEP, 0)
+    bottom = pltpu.roll(forcing[SUB:], DEEP, 0)
+    line = iota(shape, 0)
+    field[:SUB, :] = top
+    field[SUB : SUB + rows, :] = f_old[...]
+    field[SUB : 2 * SUB, :] = jnp.where(line == 0, top, f_old[:SUB, :])
+    field[rows : rows + SUB, :] = jnp.where(line == SUB - 1, bottom, field[rows : rows + SUB, :])
+    field[SUB + rows : 2 * SUB + rows, :] = bottom
+    extra = even_out.shape[0] - base // 2 - 2
+    tall = blocks.shape[1] - extra * SUB
+    for peer in range(across):
+        start = SUB - ITERS + peer * strip
+        stop = min(start + tall, field.shape[0])
+        blocks[peer, : stop - start, :] = field[start:stop, :]
+    use_even = even == (me == 0)
+    for q in range(extra):
+        relay = jnp.where(use_even, even_in[base // 2 + 2 + q], odd_in[base // 2 + 2 + q])
         for peer in range(across):
-            start = SUB - ITERS + peer * strip
-            stop = min(start + tall, field.shape[0])
-            blocks[peer, : stop - start, :] = field[start:stop, :]
-        me = lax.axis_index("by")
-        for hop in range(across):
-            sends[hop][...] = blocks[hop_peer(me, hop, across)]
+            blocks[peer, tall + q * SUB : tall + (q + 1) * SUB, :] = relay
+    for hop in range(across):
+        sends[hop][...] = blocks[hop_peer(me, hop, across)]
+
+
+def patch(fix_t, fix_s, t_old, s_old, t_new, s_new):
+    target = jnp.where(pl.program_id(0) == 0, 0, SUB - 1)
+    mine = iota(t_old.shape, 1) == target
+    t_new[...] = jnp.where(mine, fix_t[...], t_old[...])
+    s_new[...] = jnp.where(mine, fix_s[...], s_old[...])
 
 
 def hop_peer(me, hop, count):
@@ -287,7 +320,7 @@
 
 def powers(across, along, *refs):
     came = refs[:across]
-    main_up, main_own, main_down = refs[across : across + 3]
+    from_even, from_odd, main_own = refs[across : across + 3]
     basis_ref, row_ref, field, main = refs[across + 3 :]
     strip, columns = main_own.shape
     width = columns // across
@@ -295,12 +328,35 @@
     me = lax.axis_index("by")
     for hop in range(across):
         origin = hop_origin(me, hop, across)
-        field[:, pl.ds(pl.multiple_of(origin * width, LANE), width)] = came[hop][...]
+        field[:, pl.ds(pl.multiple_of(origin * width, LANE), width)] = came[hop][:tall, :]
     wide = ITERS - 1
     main[...] = jnp.zeros(main.shape, jnp.float32)
-    main[ITERS - wide : ITERS, :] = main_up[...]
     main[ITERS : ITERS + strip, :] = main_own[...]
-    main[ITERS + strip : ITERS + strip + wide, :] = main_down[...]
+    over, under = ITERS - wide, ITERS + strip
+    even = me % 2 == 0
+    parts = columns // LANE
+    begin = from_even.shape[0] - wide * parts
+    for r in range(wide):
+        for j in range(parts):
+            here = slice(j * LANE, (j + 1) * LANE)
+            at = begin + r * parts + j
+            a, b = from_even[at : at + 1, :], from_odd[at : at + 1, :]
+            main[over + r : over + r + 1, here] = jnp.where(even, b, a)
+            main[under + r : under + r + 1, here] = jnp.where(even, a, b)
+
+    def relayed(start, mine, sender):
+        hop = [h for h in range(across) if hop_origin(mine, h, across) == sender][0]
+
+        @pl.when(me == mine)
+        def _():
+            for r in range(wide):
+                for j in range(across):
+                    at = tall + r * across + j
+                    here = slice(j * width, (j + 1) * width)
+                    main[start + r : start + r + 1, here] = came[hop][at : at + 1, :]
+
+    relayed(over, 0, across - 1)
+    relayed(under, across - 1, 0)
     shape = (tall, columns)
     lane = iota(shape, 1)
     line = (lax.axis_index("bx") * across + me) * strip - ITERS + iota(shape, 0)
@@ -385,18 +441,23 @@
 
     call = functools.partial(pl.pallas_call, compiler_params=params)
 
-    stack = (layers, rows, LANE)
-    end = columns // LANE - 1
+    hbm = pl.BlockSpec(memory_space=pltpu.HBM)
+    wide = ITERS - 1
     pack = shape_of(rows, LANE)
-    lo, hi = block(stack, 0, 0, 0), block(stack, 0, 0, end)
-    lo_d, hi_d = block((rows, LANE), 0, 0), block((rows, LANE), 0, end)
+    more = shape_of(rows + wide * (columns * across // LANE), LANE)
     first, even, odd = call(
         pack_edges,
         grid=(1,),
-        in_specs=[lo, lo, lo_d, hi, hi, hi, hi, hi_d],
-        out_specs=[whole(pack)] * 3,
-        out_shape=[pack] * 3,
-    )(t, s, depth, t, s, v, y, depth)
+        in_specs=[hbm] * 6,
+        out_specs=[whole(pack), whole(more), whole(more)],
+        out_shape=[pack, more, more],
+        scratch_shapes=[
+            pltpu.VMEM((6, layers, rows, LANE), jnp.float32),
+            pltpu.VMEM((2, rows, LANE), jnp.int32),
+            pltpu.VMEM(main.shape, jnp.float32),
+            pltpu.SemaphoreType.DMA((9,)),
+        ],
+    )(*(pltpu.with_memory_space_constraint(a, pltpu.HBM) for a in (t, s, v, y, depth, main)))
     from_even = lax.ppermute(even, "by", pairs(across, 0))
     from_odd = lax.ppermute(odd, "by", pairs(across, 1))
 
@@ -404,24 +465,25 @@
     deep = [(f.shape[0], SUB, columns) for f in fields]
     foot = rows // SUB - 1
     count = (6 * layers + 4) // 2
-    rim = shape_of(count, SUB, columns)
+    extra = -(-wide * across // SUB)
+    rim = shape_of(count + extra, SUB, columns)
     even, odd = call(
-        pack_rows,
+        functools.partial(pack_rows, across),
         grid=(1,),
         in_specs=[block(d, 0, 0, 0) for d in deep]
         + [block((SUB, columns), 0, 0)]
         + [block(d, 0, foot, 0) for d in deep]
-        + [block((SUB, columns), foot, 0)],
+        + [block((SUB, columns), foot, 0), whole(main)],
         out_specs=[whole(rim)] * 2,
         out_shape=[rim] * 2,
-    )(*fields, depth, *fields, depth)
+    )(*fields, depth, *fields, depth, main)
 
     plane = shape_of(rows, columns)
     tail = block((1, SUB, columns), count - 1, 0, 0)
     edge, even, odd = call(
         join_edges,
         grid=(1,),
-        in_specs=[whole(pack)] * 3 + [tail] * 2,
+        in_specs=[whole(pack), whole(more), whole(more), tail, tail],
         out_specs=[block((rows, 2 * LANE), 0, 0), tail, tail],
         out_shape=[shape_of(rows, 2 * LANE), rim, rim],
         input_output_aliases={3: 1, 4: 2},
@@ -439,36 +501,41 @@
         out_shape=[cube, cube, plane],
     )(*args)
 
-    ends = across * along - 1
-    names = ("bx", "by")
-    wide = ITERS - 1
-    main_up = lax.ppermute(main[-wide:], names, [(i, i + 1) for i in range(ends)])
-    main_down = lax.ppermute(main[:wide], names, [(i + 1, i) for i in range(ends)])
-
     tall = -(-(strip + 2 * ITERS) // SUB) * SUB
-    part = shape_of(tall, columns)
-    touched = pl.BlockSpec((layers, SUB, columns), lambda i: (0, i * foot, 0))
-    warm, salt, *sends = call(
+    part = shape_of(tall + extra * SUB, columns)
+    fix = shape_of(layers, 2 * SUB, columns)
+    fix_t, fix_s, *sends = call(
         functools.partial(rim_rows, across),
-        grid=(2,),
-        in_specs=[whole(rim)] * 4 + [touched, touched, whole(plane)],
-        out_specs=[touched, touched] + [whole(part)] * across,
-        out_shape=[cube, cube] + [part] * across,
-        input_output_aliases={4: 0, 5: 1},
+        grid=(1,),
+        in_specs=[whole(rim)] * 4 + [whole(plane)],
+        out_specs=[whole(fix)] * 2 + [whole(part)] * across,
+        out_shape=[fix] * 2 + [part] * across,
         scratch_shapes=[
             pltpu.VMEM((rows + 2 * SUB, columns), jnp.float32),
-            pltpu.VMEM((across, tall, columns), jnp.float32),
+            pltpu.VMEM((across,) + part.shape, jnp.float32),
         ],
-    )(even, odd, even_in, odd_in, warm, salt, forcing)
+    )(even, odd, even_in, odd_in, forcing)
 
     came = [sends[0]]
     for hop in range(1, across):
         route = [(i, hop_peer(i, hop, across)) for i in range(across)]
         came.append(lax.ppermute(sends[hop], "by", route))
 
+    rimmed = pl.BlockSpec((layers, SUB, columns), lambda i: (0, i, 0))
+    touched = pl.BlockSpec((layers, SUB, columns), lambda i: (0, i * foot, 0))
+    warm, salt = call(
+        patch,
+        grid=(2,),
+        in_specs=[rimmed, rimmed, touched, touched],
+        out_specs=[touched, touched],
+        out_shape=[cube, cube],
+        input_output_aliases={2: 0, 3: 1},
+    )(fix_t, fix_s, warm, salt)
+
     basis_shape = shape_of(ITERS, strip, columns * across)
-    row_shape = shape_of(ends + 1, 1, LANE)
-    args = (*came, main_up, main, main_down)
+    names = ("bx", "by")
+    row_shape = shape_of(across * along, 1, LANE)
+    args = (*came, from_even, from_odd, main)
     basis, row = call(
         functools.partial(powers, across, along),
         grid=(1,),

time: 50 us -> 40.9 us (0.82)
  blocking collectives: 17.8 us -> 0 us
  waiting for transfers between devices: 2.09 us -> 8.59 us
  Pallas kernels: 7.14 us -> 9.59 us
  local copies, waits for them, and re-layouts: 4.59 us -> 3.44 us
  starting transfers between devices: 17.1 us -> 18 us
    all_to_all x1 -> x0, blocking collectives: 17.8 us -> none  [local(): gathered = lax.all_to_all(row, names, 0, 0, tiled=True)]
    all_to_all x0 -> x1, waiting for transfers between devices: none -> 5.42 us  [local(): gathered = lax.all_to_all(row, names, 0, 0, tiled=True)]
    all_to_all x0 -> x1, starting transfers between devices: none -> 5.38 us  [local(): gathered = lax.all_to_all(row, names, 0, 0, tiled=True)]
    ppermute x2 -> x0, starting transfers between devices: 3.94 us -> none  [the longest x1 2.64 us: local(): lax.ppermute(main[-wide:], names, [(i, i + 1) for i in range(ends)])]
    ppermute x3, waiting for transfers between devices: 0.01 us -> 2.82 us  [local(): came.append(lax.ppermute(sends[hop], 'by', route))]
    pallas_call x4 -> x5, Pallas kernels: 2.99 us -> 4.82 us  [the longest x1 1.67 us: local(): call(pack_edges, grid=(1,), in_specs=[hbm] * 6, out_specs=[whole(pack), w...]
    ppermute x2 -> x0, waiting for transfers between devices: 1.76 us -> none  [the longest x1 1.76 us: local(): lax.ppermute(main[:wide], names, [(i + 1, i) for i in range(ends)])]
    unnamed x22 -> x24, local copies, waits for them, and re-layouts: 4.58 us -> 3.44 us
  transfers between devices with their start and end apart: 9 -> 8, of which waited for: 3 -> 4; matrix products, arithmetic and copies ran while one was open for 0% -> 0% of each run, Pallas kernels for 6% -> 11%
where the time goes in v3:
time: 40.9 us; the launch traced here: 40.4 us
  starting transfers between devices  18 us (44%)
  Pallas kernels  9.59 us (23%)
  waiting for transfers between devices  8.59 us (21%)
  local copies, waits for them, and re-layouts  3.44 us (8%)
  between operations  0.81 us (2%)
    ppermute x3, starting transfers between devices, local(): came.append(lax.ppermute(sends[hop], 'by', route))  8.26 us
    all_to_all x1, waiting for transfers between devices, local(): gathered = lax.all_to_all(row, names, 0, 0, tiled=True)  5.42 us
    all_to_all x1, starting transfers between devices, local(): gathered = lax.all_to_all(row, names, 0, 0, tiled=True)  5.38 us
    unnamed x24, local copies, waits for them, and re-layouts  3.44 us
    pallas_call x1, Pallas kernels, local(): call(inner_tile, grid=(1,), in_specs=[whole(a) for a in args], out_specs=...  2.88 us
    ppermute x3, waiting for transfers between devices, local(): came.append(lax.ppermute(sends[hop], 'by', route))  2.82 us
    ppermute x1, starting transfers between devices, local(): even_in = lax.ppermute(even, 'bx', pairs(along, 0))  2.54 us
    pallas_call x1, Pallas kernels, local(): call(pack_edges, grid=(1,), in_specs=[hbm] * 6, out_specs=[whole(pack), w...  1.67 us
  transfers between devices with their start and end apart: 8, of which 4 were waited for; matrix products, arithmetic and copies ran while one was open for 0% of the time, Pallas kernels for 11%

profile of v3, /device:TPU:0, one launch (start us, length us, event | category | flops | bytes accessed | tf_op | source)
XLA Modules:
  0.0 40.4 jit_solution(13045873416108571678)
XLA Ops:
  0.6 0.0 copy-start.3
  0.6 0.0 copy-start.2
  0.7 0.0 copy-start.1
  0.7 0.0 copy-start
  0.7 0.0 copy-start.8
  0.7 1.7 %shard_map.112 = (f32[32,128]{1,0:T(8,128)S(1)}, f32[48,128]{1,0:T(8,128)S(1)}, f32[48,128]{1,0:T(8,128)S(1)}) custom-call(f32[8,32,256]{2,1,0:T(8,128)} %t.3, f32[8,32,256]{2,1,0:T(8,128)} %s.3, f32[8,32,256]{2,1,0:T(8,128)} %v.3, f32[8,32,256]{2,1,0:T(8,128)} %y.3, s32[32,256]{1,0:T(8,128)} %depth.3, f32[8,1024]{1,0:T(8,128)} %refs_6_.3), custom_call_target="tpu_custom_call" | custom-call | tf_op jit(solution)/shard_map/pallas_call | solution.py:448
  2.4 0.5 %collective-permute-start = (f32[48,128]{1,0:T(8,128)S(1)}, f32[48,128]{1,0:T(8,128)S(1)}, u32[]{:S(2)}, u32[]{:S(2)}) collective-permute-start(f32[48,128]{1,0:T(8,128)S(1)} %get-tuple-element.25), channel_id=1, source_target_pairs={{0,1},{2,3},{1,0},{3,2},{4,5},{6,7},{5,4},{7,6},{8,9},{10,11},{9,8... | collective-permute-start | bytes 73736 | tf_op jit(solution)/shard_map/ppermute | solution.py:461
  2.9 0.7 %collective-permute-start.1 = (f32[48,128]{1,0:T(8,128)S(1)}, f32[48,128]{1,0:T(8,128)S(1)}, u32[]{:S(2)}, u32[]{:S(2)}) collective-permute-start(f32[48,128]{1,0:T(8,128)S(1)} %get-tuple-element.26), channel_id=1, source_target_pairs={{1,2},{2,1},{5,6},{6,5},{9,10},{10,9},{13,14},{14,13},{17,18},{18,... | collective-permute-start | bytes 73736 | tf_op jit(solution)/shard_map/ppermute | solution.py:462
  3.5 0.0 copy-done.3
  3.5 0.0 copy-done.2
  3.6 0.0 copy-done.1
  3.6 0.0 copy-done
  3.6 0.0 copy-done.8
  3.6 0.0 copy-start.4
  3.6 0.9 %copy-done.4 = f32[8,32,256]{2,1,0:T(8,128)S(1)} copy-done((f32[8,32,256]{2,1,0:T(8,128)S(1)}, f32[8,32,256]{2,1,0:T(8,128)}, u32[]{:S(2)}) %copy-start.4) | copy-done | bytes 262168
  4.5 0.0 copy-start.6
  4.5 0.9 %copy-done.6 = f32[8,32,256]{2,1,0:T(8,128)S(1)} copy-done((f32[8,32,256]{2,1,0:T(8,128)S(1)}, f32[8,32,256]{2,1,0:T(8,128)}, u32[]{:S(2)}) %copy-start.6) | copy-done | bytes 262168
  5.5 0.0 copy-start.9
  5.5 0.8 %copy-done.9 = s32[32,256]{1,0:T(8,128)S(1)} copy-done((s32[32,256]{1,0:T(8,128)S(1)}, s32[32,256]{1,0:T(8,128)}, u32[]{:S(2)}) %copy-start.9) | copy-done | bytes 32792
  6.2 0.0 copy-start.10
  6.2 0.8 %copy-done.10 = f32[8,1024]{1,0:T(8,128)S(1)} copy-done((f32[8,1024]{1,0:T(8,128)S(1)}, f32[8,1024]{1,0:T(8,128)}, u32[]{:S(2)}) %copy-start.10) | copy-done | bytes 32792
  7.0 0.0 copy-start.7
  7.0 0.1 shard_map.113
  7.1 0.0 copy-start.5
  7.1 0.0 collective-permute-done.from_even.refs_4_
  7.1 0.0 collective-permute-done.1.from_odd.refs_5_
  7.1 0.1 shard_map.114
  7.2 2.5 %collective-permute-start.2 = (f32[27,8,256]{2,1,0:T(8,128)S(1)}, f32[27,8,256]{2,1,0:T(8,128)S(1)}, u32[]{:S(2)}, u32[]{:S(2)}) collective-permute-start(f32[27,8,256]{2,1,0:T(8,128)S(1)} %get-tuple-element.29.even_out), channel_id=1, source_target_pairs={{0,4},{8,12},{16,20},{24,28},{4,0},{12,8},{20,16},{28,24},{1,5},{9... | collective-permute-start | bytes 663560 | tf_op jit(solution)/shard_map/ppermute | solution.py:492
  9.7 0.7 %collective-permute-start.3 = (f32[27,8,256]{2,1,0:T(8,128)S(1)}, f32[27,8,256]{2,1,0:T(8,128)S(1)}, u32[]{:S(2)}, u32[]{:S(2)}) collective-permute-start(f32[27,8,256]{2,1,0:T(8,128)S(1)} %get-tuple-element.30.odd_out), channel_id=1, source_target_pairs={{4,8},{12,16},{20,24},{8,4},{16,12},{24,20},{5,9},{13,17},{21,25},... | collective-permute-start | bytes 663560 | tf_op jit(solution)/shard_map/ppermute | solution.py:491
  10.4 0.0 copy-done.7
  10.4 0.0 copy-done.5
  10.4 2.9 %shard_map.115 = (f32[8,32,256]{2,1,0:T(8,128)}, f32[8,32,256]{2,1,0:T(8,128)}, f32[32,256]{1,0:T(8,128)S(1)}) custom-call(f32[8,32,256]{2,1,0:T(8,128)S(1)} %copy-done, f32[8,32,256]{2,1,0:T(8,128)S(1)} %copy-done.1, f32[8,32,256]{2,1,0:T(8,128)S(1)} %copy-done.5, f32[8,32,256]{2,1,0:T(8,128)S(1)} %copy-done.2, f32[8,32,256]{2,1,0:T(8,128)S(1)} %copy-done.7, ...), custom_call_target="tpu_custom_call" | custom-call | tf_op jit(solution)/shard_map/pallas_call | solution.py:496
  13.3 0.3 collective-permute-done.2.even_in
  13.6 0.0 collective-permute-done.3.odd_in
  13.6 0.0 copy-start.11
  13.6 1.4 %shard_map.116 = (f32[8,16,256]{2,1,0:T(8,128)S(1)}, f32[8,16,256]{2,1,0:T(8,128)S(1)}, f32[24,256]{1,0:T(8,128)S(1)}, f32[24,256]{1,0:T(8,128)S(1)}, f32[24,256]{1,0:T(8,128)S(1)}, /*index=5*/f32[24,256]{1,0:T(8,128)S(1)}) custom-call(f32[27,8,256]{2,1,0:T(8,128)S(1)} %get-tuple-element.29.even_out, f32[27,8,256]{2,1,0:T(8,128)S(1)} %get-tuple-element.30.odd_out, ...), custom_call_target="tpu_custom_call" | custom-call | tf_op jit(solution)/shard_map/pallas_call | solution.py:507
  15.0 6.8 %collective-permute-start.4 = (f32[24,256]{1,0:T(8,128)S(1)}, f32[24,256]{1,0:T(8,128)S(1)}, u32[]{:S(2)}, u32[]{:S(2)}) collective-permute-start(f32[24,256]{1,0:T(8,128)S(1)} %get-tuple-element.40), channel_id=1, source_target_pairs={{0,1},{1,0},{2,3},{3,2},{4,5},{5,4},{6,7},{7,6},{8,9},{9,8},{10,11... | collective-permute-start | bytes 73736 | tf_op jit(solution)/shard_map/ppermute | solution.py:522
  21.8 1.0 %collective-permute-start.5 = (f32[24,256]{1,0:T(8,128)S(1)}, f32[24,256]{1,0:T(8,128)S(1)}, u32[]{:S(2)}, u32[]{:S(2)}) collective-permute-start(f32[24,256]{1,0:T(8,128)S(1)} %get-tuple-element.41), channel_id=1, source_target_pairs={{0,2},{1,3},{2,0},{3,1},{4,6},{5,7},{6,4},{7,5},{8,10},{9,11},{10,... | collective-permute-start | bytes 73736 | tf_op jit(solution)/shard_map/ppermute | solution.py:522
  22.8 0.4 %collective-permute-start.6 = (f32[24,256]{1,0:T(8,128)S(1)}, f32[24,256]{1,0:T(8,128)S(1)}, u32[]{:S(2)}, u32[]{:S(2)}) collective-permute-start(f32[24,256]{1,0:T(8,128)S(1)} %get-tuple-element.42), channel_id=1, source_target_pairs={{0,3},{1,2},{2,1},{3,0},{4,7},{5,6},{6,5},{7,4},{8,11},{9,10},{10,... | collective-permute-start | bytes 73736 | tf_op jit(solution)/shard_map/ppermute | solution.py:522
  23.3 0.0 collective-permute-done.4.refs_1_
  23.3 2.4 %collective-permute-done.5.refs_2_ = f32[24,256]{1,0:T(8,128)S(1)} collective-permute-done((f32[24,256]{1,0:T(8,128)S(1)}, f32[24,256]{1,0:T(8,128)S(1)}, u32[]{:S(2)}, u32[]{:S(2)}) %collective-permute-start.5) | collective-permute-done | bytes 24608 | tf_op jit(solution)/shard_map/ppermute | solution.py:522
  25.7 0.4 %collective-permute-done.6.refs_3_ = f32[24,256]{1,0:T(8,128)S(1)} collective-permute-done((f32[24,256]{1,0:T(8,128)S(1)}, f32[24,256]{1,0:T(8,128)S(1)}, u32[]{:S(2)}, u32[]{:S(2)}) %collective-permute-start.6) | collective-permute-done | bytes 24608 | tf_op jit(solution)/shard_map/ppermute | solution.py:522
  26.1 0.0 copy-done.11
  26.1 1.1 %shard_map.118 = (f32[3,8,1024]{2,1,0:T(8,128)S(1)}, f32[32,1,128]{2,1,0:T(1,128)}) custom-call(f32[24,256]{1,0:T(8,128)S(1)} %get-tuple-element.39.refs_0_, f32[24,256]{1,0:T(8,128)S(1)} %collective-permute-done.4.refs_1_, f32[24,256]{1,0:T(8,128)S(1)} %collective-permute-done.5.refs_2_, f32[24,256]{1,0:T(8,128)S(1)} %collective-permute-done.6.refs_3_, ...), custom_call_target="tpu_custom_call" | custom-call | tf_op jit(solution)/shard_map/pallas_call | solution.py:539
  27.1 5.4 %all-to-all-start = ((f32[32,1,128]{2,1,0:T(1,128)}), f32[32,1,128]{2,1,0:T(1,128)S(1)}, u32[]{:S(2)}, u32[]{:S(2)}) async-start(f32[32,1,128]{2,1,0:T(1,128)} %get-tuple-element.43), calls=%async_computation | async-start | bytes 32768 | tf_op jit(solution)/shard_map/all_to_all | solution.py:547
  32.5 1.7 %shard_map.117 = (f32[8,32,256]{2,1,0:T(8,128)}, f32[8,32,256]{2,1,0:T(8,128)}) custom-call(f32[8,16,256]{2,1,0:T(8,128)S(1)} %get-tuple-element.33.fix_t, f32[8,16,256]{2,1,0:T(8,128)S(1)} %get-tuple-element.34.fix_s, f32[8,32,256]{2,1,0:T(8,128)} %get-tuple-element.35.t_old, ...), custom_call_target="tpu_custom_call", output_to_operand_aliasing={{0}: (2, {}), {1}: (3, {})} | custom-call | tf_op jit(solution)/shard_map/pallas_call | solution.py:526
  34.2 5.4 %all-to-all-done.rows_ref = f32[32,1,128]{2,1,0:T(1,128)S(1)} async-done(((f32[32,1,128]{2,1,0:T(1,128)}), f32[32,1,128]{2,1,0:T(1,128)S(1)}, u32[]{:S(2)}, u32[]{:S(2)}) %all-to-all-start) | async-done | bytes 16416 | tf_op jit(solution)/shard_map/all_to_all | solution.py:547
  39.6 0.8 %shard_map.119 = f32[8,1024]{1,0:T(8,128)} custom-call(f32[32,1,128]{2,1,0:T(1,128)S(1)} %all-to-all-done.rows_ref, f32[3,8,1024]{2,1,0:T(8,128)S(1)} %get-tuple-element.44.basis_ref), custom_call_target="tpu_custom_call" | custom-call | tf_op jit(solution)/shard_map/pallas_call | solution.py:549
Async XLA Ops:
  0.6 2.9 %copy-start.3 = (f32[8,32,256]{2,1,0:T(8,128)S(1)}, f32[8,32,256]{2,1,0:T(8,128)}, u32[]{:S(2)}) copy-start(f32[8,32,256]{2,1,0:T(8,128)} %y.3) | copy-start | bytes 786436
  0.6 2.9 %copy-start.2 = (f32[8,32,256]{2,1,0:T(8,128)S(1)}, f32[8,32,256]{2,1,0:T(8,128)}, u32[]{:S(2)}) copy-start(f32[8,32,256]{2,1,0:T(8,128)} %v.3) | copy-start | bytes 786436
  0.7 2.9 %copy-start.1 = (f32[8,32,256]{2,1,0:T(8,128)S(1)}, f32[8,32,256]{2,1,0:T(8,128)}, u32[]{:S(2)}) copy-start(f32[8,32,256]{2,1,0:T(8,128)} %s.3) | copy-start | bytes 786436
  0.7 2.9 %copy-start = (f32[8,32,256]{2,1,0:T(8,128)S(1)}, f32[8,32,256]{2,1,0:T(8,128)}, u32[]{:S(2)}) copy-start(f32[8,32,256]{2,1,0:T(8,128)} %t.3) | copy-start | bytes 786436
  0.7 2.9 %copy-start.8 = (f32[2,32,256]{2,1,0:T(8,128)S(1)}, f32[2,32,256]{2,1,0:T(8,128)}, u32[]{:S(2)}) copy-start(f32[2,32,256]{2,1,0:T(8,128)} %source.1) | copy-start | bytes 196612
  2.4 4.7 %collective-permute-start = (f32[48,128]{1,0:T(8,128)S(1)}, f32[48,128]{1,0:T(8,128)S(1)}, u32[]{:S(2)}, u32[]{:S(2)}) collective-permute-start(f32[48,128]{1,0:T(8,128)S(1)} %get-tuple-element.25), channel_id=1, source_target_pairs={{0,1},{2,3},{1,0},{3,2},{4,5},{6,7},{5,4},{7,6},{8,9},{10,11},{9,8... | collective-permute-start | bytes 73736 | tf_op jit(solution)/shard_map/ppermute | solution.py:461
  2.9 4.2 %collective-permute-start.1 = (f32[48,128]{1,0:T(8,128)S(1)}, f32[48,128]{1,0:T(8,128)S(1)}, u32[]{:S(2)}, u32[]{:S(2)}) collective-permute-start(f32[48,128]{1,0:T(8,128)S(1)} %get-tuple-element.26), channel_id=1, source_target_pairs={{1,2},{2,1},{5,6},{6,5},{9,10},{10,9},{13,14},{14,13},{17,18},{18,... | collective-permute-start | bytes 73736 | tf_op jit(solution)/shard_map/ppermute | solution.py:462
  3.6 1.0 %copy-start.4 = (f32[8,32,256]{2,1,0:T(8,128)S(1)}, f32[8,32,256]{2,1,0:T(8,128)}, u32[]{:S(2)}) copy-start(f32[8,32,256]{2,1,0:T(8,128)} %u.1) | copy-start | bytes 786436
  4.5 0.9 %copy-start.6 = (f32[8,32,256]{2,1,0:T(8,128)S(1)}, f32[8,32,256]{2,1,0:T(8,128)}, u32[]{:S(2)}) copy-start(f32[8,32,256]{2,1,0:T(8,128)} %x.1) | copy-start | bytes 786436
  5.5 0.8 %copy-start.9 = (s32[32,256]{1,0:T(8,128)S(1)}, s32[32,256]{1,0:T(8,128)}, u32[]{:S(2)}) copy-start(s32[32,256]{1,0:T(8,128)} %depth.3) | copy-start | bytes 98308
  6.2 0.8 %copy-start.10 = (f32[8,1024]{1,0:T(8,128)S(1)}, f32[8,1024]{1,0:T(8,128)}, u32[]{:S(2)}) copy-start(f32[8,1024]{1,0:T(8,128)} %refs_6_.3) | copy-start | bytes 98308
  7.0 3.4 %copy-start.7 = (f32[8,32,256]{2,1,0:T(8,128)S(1)}, f32[8,32,256]{2,1,0:T(8,128)}, u32[]{:S(2)}) copy-start(f32[8,32,256]{2,1,0:T(8,128)} %x.1) | copy-start | bytes 786436
  7.1 3.3 %copy-start.5 = (f32[8,32,256]{2,1,0:T(8,128)S(1)}, f32[8,32,256]{2,1,0:T(8,128)}, u32[]{:S(2)}) copy-start(f32[8,32,256]{2,1,0:T(8,128)} %u.1) | copy-start | bytes 786436
  7.2 6.4 %collective-permute-start.2 = (f32[27,8,256]{2,1,0:T(8,128)S(1)}, f32[27,8,256]{2,1,0:T(8,128)S(1)}, u32[]{:S(2)}, u32[]{:S(2)}) collective-permute-start(f32[27,8,256]{2,1,0:T(8,128)S(1)} %get-tuple-element.29.even_out), channel_id=1, source_target_pairs={{0,4},{8,12},{16,20},{24,28},{4,0},{12,8},{20,16},{28,24},{1,5},{9... | collective-permute-start | bytes 663560 | tf_op jit(solution)/shard_map/ppermute | solution.py:492
  9.7 3.9 %collective-permute-start.3 = (f32[27,8,256]{2,1,0:T(8,128)S(1)}, f32[27,8,256]{2,1,0:T(8,128)S(1)}, u32[]{:S(2)}, u32[]{:S(2)}) collective-permute-start(f32[27,8,256]{2,1,0:T(8,128)S(1)} %get-tuple-element.30.odd_out), channel_id=1, source_target_pairs={{4,8},{12,16},{20,24},{8,4},{16,12},{24,20},{5,9},{13,17},{21,25},... | collective-permute-start | bytes 663560 | tf_op jit(solution)/shard_map/ppermute | solution.py:491
  13.6 12.4 %copy-start.11 = (f32[8,1024]{1,0:T(8,128)S(1)}, f32[8,1024]{1,0:T(8,128)}, u32[]{:S(2)}) copy-start(f32[8,1024]{1,0:T(8,128)} %refs_6_.3) | copy-start | bytes 98308
  15.0 8.3 %collective-permute-start.4 = (f32[24,256]{1,0:T(8,128)S(1)}, f32[24,256]{1,0:T(8,128)S(1)}, u32[]{:S(2)}, u32[]{:S(2)}) collective-permute-start(f32[24,256]{1,0:T(8,128)S(1)} %get-tuple-element.40), channel_id=1, source_target_pairs={{0,1},{1,0},{2,3},{3,2},{4,5},{5,4},{6,7},{7,6},{8,9},{9,8},{10,11... | collective-permute-start | bytes 73736 | tf_op jit(solution)/shard_map/ppermute | solution.py:522
  21.8 3.8 %collective-permute-start.5 = (f32[24,256]{1,0:T(8,128)S(1)}, f32[24,256]{1,0:T(8,128)S(1)}, u32[]{:S(2)}, u32[]{:S(2)}) collective-permute-start(f32[24,256]{1,0:T(8,128)S(1)} %get-tuple-element.41), channel_id=1, source_target_pairs={{0,2},{1,3},{2,0},{3,1},{4,6},{5,7},{6,4},{7,5},{8,10},{9,11},{10,... | collective-permute-start | bytes 73736 | tf_op jit(solution)/shard_map/ppermute | solution.py:522
  22.8 3.3 %collective-permute-start.6 = (f32[24,256]{1,0:T(8,128)S(1)}, f32[24,256]{1,0:T(8,128)S(1)}, u32[]{:S(2)}, u32[]{:S(2)}) collective-permute-start(f32[24,256]{1,0:T(8,128)S(1)} %get-tuple-element.42), channel_id=1, source_target_pairs={{0,3},{1,2},{2,1},{3,0},{4,7},{5,6},{6,5},{7,4},{8,11},{9,10},{10,... | collective-permute-start | bytes 73736 | tf_op jit(solution)/shard_map/ppermute | solution.py:522
  27.1 12.5 %all-to-all-start = ((f32[32,1,128]{2,1,0:T(1,128)}), f32[32,1,128]{2,1,0:T(1,128)S(1)}, u32[]{:S(2)}, u32[]{:S(2)}) async-start(f32[32,1,128]{2,1,0:T(1,128)} %get-tuple-element.43), calls=%async_computation | async-start | bytes 32768 | tf_op jit(solution)/shard_map/all_to_all | solution.py:547

commit v4 on v3

--- a/solution.py
+++ b/solution.py
@@ -38,9 +38,11 @@
     cells = 2 * layers
     wide = ITERS - 1
     head, tail = pl.ds(0, LANE), pl.ds(columns - LANE, LANE)
-    moves = [(t.at[:, :, tail], cubes.at[0]), (s.at[:, :, tail], cubes.at[1])]
-    moves += [(v.at[:, :, tail], cubes.at[2]), (y.at[:, :, tail], cubes.at[3])]
-    moves += [(t.at[:, :, head], cubes.at[4]), (s.at[:, :, head], cubes.at[5])]
+    moves = []
+    for low in range(0, layers, layers // 2):
+        some = pl.ds(low, layers // 2)
+        for i, (ref, where) in enumerate(((t, tail), (s, tail), (v, tail), (y, tail), (t, head), (s, head))):
+            moves.append((ref.at[some, :, where], cubes.at[i, some]))
     moves += [(depth.at[:, tail], planes.at[0]), (depth.at[:, head], planes.at[1]), (main, lines)]
     copies = [pltpu.make_async_copy(a, b, sems.at[i]) for i, (a, b) in enumerate(moves)]
     for copy in copies:
@@ -79,29 +81,67 @@
             odd_ref[at : at + 1, :] = jnp.where(even, up, down)
 
 
-def pack_rows(across, *refs):
-    tops, bottoms, (main, even_ref, odd_ref) = refs[:8], refs[8:16], refs[16:]
-
-    def flat(group):
-        planes = []
-        for ref in group[:7]:
-            planes += [ref[k] for k in range(ref.shape[0])]
-        planes.append(group[7][...].astype(jnp.float32))
-        planes.append(planes[-1])
-        return planes
-
+def gather_rows(t, s, u, v, x, y, source, depth, near, near_depth, sems):
+    rows = t.shape[1]
+    copies = []
+    at = 0
+    for ref in (t, s, u, v, x, y, source):
+        for i, start in enumerate((0, rows - SUB)):
+            planes = near.at[pl.ds(at, ref.shape[0]), pl.ds(i * SUB, SUB)]
+            copies.append((ref.at[:, pl.ds(start, SUB)], planes))
+        at += ref.shape[0]
+    for i, start in enumerate((0, rows - SUB)):
+        copies.append((depth.at[pl.ds(start, SUB)], near_depth.at[pl.ds(i * SUB, SUB)]))
+    copies = [pltpu.make_async_copy(a, b, sems.at[i]) for i, (a, b) in enumerate(copies)]
+    for copy in copies:
+        copy.start()
+    for copy in copies:
+        copy.wait()
+
+
+def pack_rows(across, first_ref, from_even, from_odd, near, near_depth, main, edge_ref, even_ref, odd_ref):
+    rows, half = first_ref.shape[0], LANE // 2
+    layers = near.shape[0] // 6
+    even = lax.axis_index("by") % 2 == 0
+    lane = iota((rows, LANE), 1)
+    a, b = from_even[:rows, :], from_odd[:rows, :]
+    left = jnp.where(even, b, a)
+    right = jnp.where(even, a, b)
+    left = jnp.where(lane < half, left, pltpu.roll(first_ref[...], half, 1))
+    edge_ref[:, :LANE] = left
+    edge_ref[:, LANE:] = right
+
+    base = 6 * layers
+    depth = near_depth[...].astype(jnp.float32)
+    edge = jnp.concatenate([edge_ref[:SUB, :], edge_ref[rows - SUB :, :]], 0)
+    _, _, forcing = tile_step(
+        lambda kind, k: near[kind * layers + k], [near[base], near[base + 1]], depth, edge, layers
+    )
     even = lax.axis_index("bx") % 2 == 0
-    tops, bottoms = flat(tops), flat(bottoms)
-    upper = iota(tops[0].shape, 0) < DEEP
-    count = len(tops) // 2
-    for q in range(count):
-        up = jnp.where(upper, tops[2 * q], pltpu.roll(tops[2 * q + 1], DEEP, 0))
-        down = jnp.where(upper, pltpu.roll(bottoms[2 * q], DEEP, 0), bottoms[2 * q + 1])
-        even_ref[q] = jnp.where(even, down, up)
-        odd_ref[q] = jnp.where(even, up, down)
+    group = iota((SUB, edge.shape[1]), 0) // 2
+
+    def put(q, planes):
+        out_even, out_odd = None, None
+        for j, (up, down) in enumerate(planes):
+            one = jnp.where(even, down, up)
+            two = jnp.where(even, up, down)
+            one, two = [z if j == 0 else pltpu.roll(z, 2 * j, 0) for z in (one, two)]
+            out_even = one if j == 0 else jnp.where(group == j, one, out_even)
+            out_odd = two if j == 0 else jnp.where(group == j, two, out_odd)
+        even_ref[q] = out_even
+        odd_ref[q] = out_odd
+
+    def ends(plane):
+        return plane[:SUB], pltpu.roll(plane[SUB:], 2, 0)
+
+    for q in range(base // 4):
+        put(q, [ends(near[4 * q + j]) for j in range(4)])
+    put(base // 4, [ends(near[base]), ends(near[base + 1]), ends(depth), ends(edge)])
+    put(base // 4 + 1, [(pltpu.roll(forcing[:SUB], SUB - 1, 0), pltpu.roll(forcing[SUB:], 3, 0))])
+    count = base // 4 + 2
     wide = ITERS - 1
     strip = main.shape[0]
-    width = tops[0].shape[1]
+    width = edge.shape[1]
     for r in range(wide):
         for j in range(across):
             here = slice(j * width, (j + 1) * width)
@@ -110,25 +150,6 @@
             q, at = divmod(r * across + j, SUB)
             even_ref[count + q, at : at + 1, :] = jnp.where(even, down, up)
             odd_ref[count + q, at : at + 1, :] = jnp.where(even, up, down)
-
-
-def join_edges(first_ref, from_even, from_odd, even_in, odd_in, edge_ref, even_ref, odd_ref):
-    rows = first_ref.shape[0]
-    half = LANE // 2
-    even = lax.axis_index("by") % 2 == 0
-    lane = iota((rows, LANE), 1)
-    a, b = from_even[:rows, :], from_odd[:rows, :]
-    left = jnp.where(even, b, a)
-    right = jnp.where(even, a, b)
-    left = jnp.where(lane < half, left, pltpu.roll(first_ref[...], half, 1))
-    edge_ref[:, :LANE] = left
-    edge_ref[:, LANE:] = right
-    even = lax.axis_index("bx") % 2 == 0
-    upper = iota((SUB, 2 * LANE), 0) < DEEP
-    up = pltpu.roll(edge_ref[:SUB, :], DEEP, 0)
-    down = edge_ref[rows - SUB :, :]
-    even_ref[0] = jnp.where(upper, even_in[0], jnp.where(even, down, up))
-    odd_ref[0] = jnp.where(upper, odd_in[0], jnp.where(even, up, down))
 
 
 def tile_step(get, source, depth, edge, layers):
@@ -255,16 +276,19 @@
     even = lax.axis_index("bx") % 2 == 0
     me = lax.axis_index("by")
     shape = (SUB, f_old.shape[1])
-    upper = iota(shape, 0) < DEEP
+    line = iota(shape, 0)
     planes = []
     base = 6 * layers
-    for q in range(base // 2 + 2):
+    for q in range(base // 4 + 1):
         sent_even, sent_odd, came_even, came_odd = even_out[q], odd_out[q], even_in[q], odd_in[q]
-        ups = [jnp.where(even, came_odd, came_even), jnp.where(even, sent_odd, sent_even)]
-        downs = [jnp.where(even, sent_even, sent_odd), jnp.where(even, came_even, came_odd)]
-        one = [jnp.where(upper, low, pltpu.roll(high, DEEP, 0)) for low, high in (ups, downs)]
-        two = [jnp.where(upper, pltpu.roll(low, DEEP, 0), high) for low, high in (ups, downs)]
-        planes += [jnp.concatenate(one, 0), jnp.concatenate(two, 0)]
+        parts = [jnp.where(even, came_odd, came_even), jnp.where(even, sent_odd, sent_even)]
+        parts += [jnp.where(even, sent_even, sent_odd), jnp.where(even, came_even, came_odd)]
+        for j in range(4):
+            total = None
+            for i, part in enumerate(parts):
+                part = part if i == j else pltpu.roll(part, (2 * (i - j)) % SUB, 0)
+                total = part if i == 0 else jnp.where(line // 2 == i, part, total)
+            planes.append(total)
     warm, salt, forcing = tile_step(
         lambda kind, k: planes[kind * layers + k],
         [planes[base], planes[base + 1]],
@@ -274,17 +298,18 @@
     )
     for fix, fresh in ((t_fix, warm), (s_fix, salt)):
         for k in range(layers):
-            fix[k, :SUB, :] = pltpu.roll(fresh[k][:SUB], DEEP, 0)
-            fix[k, SUB:, :] = pltpu.roll(fresh[k][SUB:], DEEP, 0)
-    top = pltpu.roll(forcing[:SUB], DEEP, 0)
-    bottom = pltpu.roll(forcing[SUB:], DEEP, 0)
-    line = iota(shape, 0)
-    field[:SUB, :] = top
-    field[SUB : SUB + rows, :] = f_old[...]
+            fix[k] = jnp.where(line == 0, pltpu.roll(fresh[k], 6, 0), pltpu.roll(fresh[k], 2, 0))
+    top, bottom = pltpu.roll(forcing, 6, 0), pltpu.roll(forcing, 2, 0)
+    ahead = base // 4 + 1
+    over = pltpu.roll(jnp.where(even, odd_in[ahead], even_in[ahead]), 5, 0)
+    under = pltpu.roll(jnp.where(even, even_in[ahead], odd_in[ahead]), 1, 0)
+    last = SUB - 1
+    field[:SUB, :] = jnp.where(line == last, top, over)
     field[SUB : 2 * SUB, :] = jnp.where(line == 0, top, f_old[:SUB, :])
-    field[rows : rows + SUB, :] = jnp.where(line == SUB - 1, bottom, field[rows : rows + SUB, :])
-    field[SUB + rows : 2 * SUB + rows, :] = bottom
-    extra = even_out.shape[0] - base // 2 - 2
+    field[2 * SUB : rows, :] = f_old[SUB : rows - SUB, :]
+    field[rows : rows + SUB, :] = jnp.where(line == last, bottom, f_old[rows - SUB :, :])
+    field[SUB + rows : 2 * SUB + rows, :] = jnp.where(line == 0, bottom, under)
+    extra = even_out.shape[0] - ahead - 1
     tall = blocks.shape[1] - extra * SUB
     for peer in range(across):
         start = SUB - ITERS + peer * strip
@@ -292,48 +317,20 @@
         blocks[peer, : stop - start, :] = field[start:stop, :]
     use_even = even == (me == 0)
     for q in range(extra):
-        relay = jnp.where(use_even, even_in[base // 2 + 2 + q], odd_in[base // 2 + 2 + q])
+        relay = jnp.where(use_even, even_in[ahead + 1 + q], odd_in[ahead + 1 + q])
         for peer in range(across):
             blocks[peer, tall + q * SUB : tall + (q + 1) * SUB, :] = relay
     for hop in range(across):
         sends[hop][...] = blocks[hop_peer(me, hop, across)]
 
 
-def patch(fix_t, fix_s, t_old, s_old, t_new, s_new):
-    target = jnp.where(pl.program_id(0) == 0, 0, SUB - 1)
-    mine = iota(t_old.shape, 1) == target
-    t_new[...] = jnp.where(mine, fix_t[...], t_old[...])
-    s_new[...] = jnp.where(mine, fix_s[...], s_old[...])
-
-
-def hop_peer(me, hop, count):
-    if count & (count - 1) == 0:
-        return me ^ hop
-    return (me + hop) % count
-
-
-def hop_origin(me, hop, count):
-    if count & (count - 1) == 0:
-        return me ^ hop
-    return (me + count - hop) % count
-
-
-def powers(across, along, *refs):
-    came = refs[:across]
-    from_even, from_odd, main_own = refs[across : across + 3]
-    basis_ref, row_ref, field, main = refs[across + 3 :]
+def main_rows(from_even, from_odd, main_own, out):
     strip, columns = main_own.shape
-    width = columns // across
-    tall = field.shape[0]
-    me = lax.axis_index("by")
-    for hop in range(across):
-        origin = hop_origin(me, hop, across)
-        field[:, pl.ds(pl.multiple_of(origin * width, LANE), width)] = came[hop][:tall, :]
     wide = ITERS - 1
-    main[...] = jnp.zeros(main.shape, jnp.float32)
-    main[ITERS : ITERS + strip, :] = main_own[...]
+    out[...] = jnp.zeros(out.shape, jnp.float32)
+    out[ITERS : ITERS + strip, :] = main_own[...]
     over, under = ITERS - wide, ITERS + strip
-    even = me % 2 == 0
+    even = lax.axis_index("by") % 2 == 0
     parts = columns // LANE
     begin = from_even.shape[0] - wide * parts
     for r in range(wide):
@@ -341,8 +338,41 @@
             here = slice(j * LANE, (j + 1) * LANE)
             at = begin + r * parts + j
             a, b = from_even[at : at + 1, :], from_odd[at : at + 1, :]
-            main[over + r : over + r + 1, here] = jnp.where(even, b, a)
-            main[under + r : under + r + 1, here] = jnp.where(even, a, b)
+            out[over + r : over + r + 1, here] = jnp.where(even, b, a)
+            out[under + r : under + r + 1, here] = jnp.where(even, a, b)
+
+
+def patch(fix_t, fix_s, t_old, s_old, t_new, s_new):
+    target = jnp.where(pl.program_id(0) == 0, 0, SUB - 1)
+    mine = iota(t_old.shape, 1) == target
+    t_new[...] = jnp.where(mine, fix_t[...], t_old[...])
+    s_new[...] = jnp.where(mine, fix_s[...], s_old[...])
+
+
+def hop_peer(me, hop, count):
+    if count & (count - 1) == 0:
+        return me ^ hop
+    return (me + hop) % count
+
+
+def hop_origin(me, hop, count):
+    if count & (count - 1) == 0:
+        return me ^ hop
+    return (me + count - hop) % count
+
+
+def powers(across, along, *refs):
+    came = refs[:across]
+    main_in, basis_ref, row_ref, field, main = refs[across:]
+    tall, columns = main_in.shape
+    strip = basis_ref.shape[1]
+    width = columns // across
+    me = lax.axis_index("by")
+    for hop in range(across):
+        origin = hop_origin(me, hop, across)
+        field[:, pl.ds(pl.multiple_of(origin * width, LANE), width)] = came[hop][:tall, :]
+    wide = ITERS - 1
+    main[...] = main_in[...]
 
     def relayed(start, mine, sender):
         hop = [h for h in range(across) if hop_origin(mine, h, across) == sender][0]
@@ -355,8 +385,8 @@
                     here = slice(j * width, (j + 1) * width)
                     main[start + r : start + r + 1, here] = came[hop][at : at + 1, :]
 
-    relayed(over, 0, across - 1)
-    relayed(under, across - 1, 0)
+    relayed(ITERS - wide, 0, across - 1)
+    relayed(ITERS + strip, across - 1, 0)
     shape = (tall, columns)
     lane = iota(shape, 1)
     line = (lax.axis_index("bx") * across + me) * strip - ITERS + iota(shape, 0)
@@ -455,39 +485,37 @@
             pltpu.VMEM((6, layers, rows, LANE), jnp.float32),
             pltpu.VMEM((2, rows, LANE), jnp.int32),
             pltpu.VMEM(main.shape, jnp.float32),
-            pltpu.SemaphoreType.DMA((9,)),
+            pltpu.SemaphoreType.DMA((15,)),
         ],
     )(*(pltpu.with_memory_space_constraint(a, pltpu.HBM) for a in (t, s, v, y, depth, main)))
     from_even = lax.ppermute(even, "by", pairs(across, 0))
     from_odd = lax.ppermute(odd, "by", pairs(across, 1))
 
     fields = (t, s, u, v, x, y, source)
-    deep = [(f.shape[0], SUB, columns) for f in fields]
     foot = rows // SUB - 1
-    count = (6 * layers + 4) // 2
+    near = shape_of(6 * layers + 2, 2 * SUB, columns)
+    near_depth = jax.ShapeDtypeStruct((2 * SUB, columns), depth.dtype)
+    near, near_depth = call(
+        gather_rows,
+        grid=(1,),
+        in_specs=[hbm] * 8,
+        out_specs=[whole(near), whole(near_depth)],
+        out_shape=[near, near_depth],
+        scratch_shapes=[pltpu.SemaphoreType.DMA((16,))],
+    )(*(pltpu.with_memory_space_constraint(a, pltpu.HBM) for a in (*fields, depth)))
+
     extra = -(-wide * across // SUB)
-    rim = shape_of(count + extra, SUB, columns)
-    even, odd = call(
+    plane = shape_of(rows, columns)
+    sides = shape_of(rows, 2 * LANE)
+    rim = shape_of(6 * layers // 4 + 2 + extra, SUB, columns)
+    args = (first, from_even, from_odd, near, near_depth, main)
+    edge, even, odd = call(
         functools.partial(pack_rows, across),
         grid=(1,),
-        in_specs=[block(d, 0, 0, 0) for d in deep]
-        + [block((SUB, columns), 0, 0)]
-        + [block(d, 0, foot, 0) for d in deep]
-        + [block((SUB, columns), foot, 0), whole(main)],
-        out_specs=[whole(rim)] * 2,
-        out_shape=[rim] * 2,
-    )(*fields, depth, *fields, depth, main)
-
-    plane = shape_of(rows, columns)
-    tail = block((1, SUB, columns), count - 1, 0, 0)
-    edge, even, odd = call(
-        join_edges,
-        grid=(1,),
-        in_specs=[whole(pack), whole(more), whole(more), tail, tail],
-        out_specs=[block((rows, 2 * LANE), 0, 0), tail, tail],
-        out_shape=[shape_of(rows, 2 * LANE), rim, rim],
-        input_output_aliases={3: 1, 4: 2},
-    )(first, from_even, from_odd, even, odd)
+        in_specs=[whole(a) for a in args],
+        out_specs=[whole(sides), whole(rim), whole(rim)],
+        out_shape=[sides, rim, rim],
+    )(*args)
     odd_in = lax.ppermute(odd, "bx", pairs(along, 1))
     even_in = lax.ppermute(even, "bx", pairs(along, 0))
 
@@ -503,7 +531,7 @@
 
     tall = -(-(strip + 2 * ITERS) // SUB) * SUB
     part = shape_of(tall + extra * SUB, columns)
-    fix = shape_of(layers, 2 * SUB, columns)
+    fix = shape_of(layers, SUB, columns)
     fix_t, fix_s, *sends = call(
         functools.partial(rim_rows, across),
         grid=(1,),
@@ -521,12 +549,11 @@
         route = [(i, hop_peer(i, hop, across)) for i in range(across)]
         came.append(lax.ppermute(sends[hop], "by", route))
 
-    rimmed = pl.BlockSpec((layers, SUB, columns), lambda i: (0, i, 0))
     touched = pl.BlockSpec((layers, SUB, columns), lambda i: (0, i * foot, 0))
     warm, salt = call(
         patch,
         grid=(2,),
-        in_specs=[rimmed, rimmed, touched, touched],
+        in_specs=[whole(fix), whole(fix), touched, touched],
         out_specs=[touched, touched],
         out_shape=[cube, cube],
         input_output_aliases={2: 0, 3: 1},
@@ -535,7 +562,16 @@
     basis_shape = shape_of(ITERS, strip, columns * across)
     names = ("bx", "by")
     row_shape = shape_of(across * along, 1, LANE)
-    args = (*came, from_even, from_odd, main)
+    ready = shape_of(tall, columns * across)
+    args = (from_even, from_odd, main)
+    ready = call(
+        main_rows,
+        grid=(1,),
+        in_specs=[whole(a) for a in args],
+        out_specs=whole(ready),
+        out_shape=ready,
+    )(*args)
+    args = (*came, ready)
     basis, row = call(
         functools.partial(powers, across, along),
         grid=(1,),

time: 40.9 us -> 38.3 us (0.936)
  local copies, waits for them, and re-layouts: 3.44 us -> 0.05 us
  Pallas kernels: 9.59 us -> 11.3 us
  starting transfers between devices: 18 us -> 17.2 us
    ppermute x3, starting transfers between devices: 8.26 us -> 4.83 us  [local(): came.append(lax.ppermute(sends[hop], 'by', route))]
    unnamed x24 -> x18, local copies, waits for them, and re-layouts: 3.44 us -> 0.05 us
    pallas_call x3 -> x4, Pallas kernels: 1.79 us -> 4.43 us  [the longest x1 1.63 us: local(): call(patch, grid=(2,), in_specs=[whole(fix), whole(fix), touched, touched...]
    all_to_all x1, starting transfers between devices: 5.38 us -> 8.01 us  [local(): gathered = lax.all_to_all(row, names, 0, 0, tiled=True)]
    pallas_call x1, Pallas kernels: 1.36 us -> 0.53 us  [local(): call(functools.partial(rim_rows, across), grid=(1,), in_specs=[whole(rim)...]
  transfers between devices with their start and end apart: 8 -> 8, of which waited for: 4 -> 3; matrix products, arithmetic and copies ran while one was open for 0% -> 0% of each run, Pallas kernels for 11% -> 16%
where the time goes in v4:
time: 38.3 us; the launch traced here: 38 us
  starting transfers between devices  17.2 us (45%)
  Pallas kernels  11.3 us (30%)
  waiting for transfers between devices  8.52 us (22%)
  between operations  0.84 us (2%)
    all_to_all x1, starting transfers between devices, local(): gathered = lax.all_to_all(row, names, 0, 0, tiled=True)  8.01 us
    all_to_all x1, waiting for transfers between devices, local(): gathered = lax.all_to_all(row, names, 0, 0, tiled=True)  5.45 us
    ppermute x3, starting transfers between devices, local(): came.append(lax.ppermute(sends[hop], 'by', route))  4.83 us
    ppermute x3, waiting for transfers between devices, local(): came.append(lax.ppermute(sends[hop], 'by', route))  3.06 us
    pallas_call x1, Pallas kernels, local(): call(inner_tile, grid=(1,), in_specs=[whole(a) for a in args], out_specs=...  2.88 us
    ppermute x1, starting transfers between devices, local(): even_in = lax.ppermute(even, 'bx', pairs(along, 0))  2.45 us
    pallas_call x1, Pallas kernels, local(): call(patch, grid=(2,), in_specs=[whole(fix), whole(fix), touched, touched...  1.63 us
    pallas_call x1, Pallas kernels, local(): call(pack_edges, grid=(1,), in_specs=[hbm] * 6, out_specs=[whole(pack), w...  1.6 us
  transfers between devices with their start and end apart: 8, of which 3 were waited for; matrix products, arithmetic and copies ran while one was open for 0% of the time, Pallas kernels for 16%

profile of v4, /device:TPU:0, one launch (start us, length us, event | category | flops | bytes accessed | tf_op | source)
XLA Modules:
  0.0 38.0 jit_solution(17262703978233117475)
XLA Ops:
  0.6 1.6 %shard_map.112 = (f32[32,128]{1,0:T(8,128)S(1)}, f32[48,128]{1,0:T(8,128)S(1)}, f32[48,128]{1,0:T(8,128)S(1)}) custom-call(f32[8,32,256]{2,1,0:T(8,128)} %t.5, f32[8,32,256]{2,1,0:T(8,128)} %s.5, f32[8,32,256]{2,1,0:T(8,128)} %v.5, f32[8,32,256]{2,1,0:T(8,128)} %y.5, s32[32,256]{1,0:T(8,128)} %depth.5, f32[8,1024]{1,0:T(8,128)} %main_own.1), custom_call_target="tpu_custom_call" | custom-call | tf_op jit(solution)/shard_map/pallas_call | solution.py:478
  2.2 0.5 %collective-permute-start = (f32[48,128]{1,0:T(8,128)S(1)}, f32[48,128]{1,0:T(8,128)S(1)}, u32[]{:S(2)}, u32[]{:S(2)}) collective-permute-start(f32[48,128]{1,0:T(8,128)S(1)} %get-tuple-element.25), channel_id=1, source_target_pairs={{0,1},{2,3},{1,0},{3,2},{4,5},{6,7},{5,4},{7,6},{8,9},{10,11},{9,8... | collective-permute-start | bytes 73736 | tf_op jit(solution)/shard_map/ppermute | solution.py:491
  2.8 0.0 copy-start.6
  2.8 0.8 %collective-permute-start.1 = (f32[48,128]{1,0:T(8,128)S(1)}, f32[48,128]{1,0:T(8,128)S(1)}, u32[]{:S(2)}, u32[]{:S(2)}) collective-permute-start(f32[48,128]{1,0:T(8,128)S(1)} %get-tuple-element.26), channel_id=1, source_target_pairs={{1,2},{2,1},{5,6},{6,5},{9,10},{10,9},{13,14},{14,13},{17,18},{18,... | collective-permute-start | bytes 73736 | tf_op jit(solution)/shard_map/ppermute | solution.py:492
  3.5 0.0 copy-start.3
  3.6 0.0 copy-start.4
  3.6 0.0 copy-start.5
  3.6 1.4 %shard_map.113 = (f32[50,16,256]{2,1,0:T(8,128)S(1)}, s32[16,256]{1,0:T(8,128)S(1)}) custom-call(f32[8,32,256]{2,1,0:T(8,128)} %t.5, f32[8,32,256]{2,1,0:T(8,128)} %s.5, f32[8,32,256]{2,1,0:T(8,128)} %u.3, f32[8,32,256]{2,1,0:T(8,128)} %v.5, f32[8,32,256]{2,1,0:T(8,128)} %x.3, f32[8,32,256]{2,1,0:T(8,128)} %y.5, f32[2,32,256]{2,1,0:T(8,128)} %source.3, ...), custom_call_target="tpu_custom_call" | custom-call | tf_op jit(solution)/shard_map/pallas_call | solution.py:498
  5.0 0.0 collective-permute-done.from_even
  5.0 0.0 collective-permute-done.1.from_odd
  5.0 0.0 copy-done.6
  5.0 0.0 copy-start
  5.0 0.0 copy-start.1
  5.0 0.0 copy-start.2
  5.0 0.0 copy-start.7
  5.0 0.0 copy-start.8
  5.1 1.4 %shard_map.114 = (f32[32,256]{1,0:T(8,128)S(1)}, f32[15,8,256]{2,1,0:T(8,128)S(1)}, f32[15,8,256]{2,1,0:T(8,128)S(1)}) custom-call(f32[32,128]{1,0:T(8,128)S(1)} %get-tuple-element.24.first_ref, f32[48,128]{1,0:T(8,128)S(1)} %collective-permute-done.from_even, f32[48,128]{1,0:T(8,128)S(1)} %collective-permute-done.1.from_odd, ...), custom_call_target="tpu_custom_call" | custom-call | tf_op jit(solution)/shard_map/pallas_call | solution.py:512
  6.5 2.5 %collective-permute-start.2 = (f32[15,8,256]{2,1,0:T(8,128)S(1)}, f32[15,8,256]{2,1,0:T(8,128)S(1)}, u32[]{:S(2)}, u32[]{:S(2)}) collective-permute-start(f32[15,8,256]{2,1,0:T(8,128)S(1)} %get-tuple-element.29.even_out), channel_id=1, source_target_pairs={{0,4},{8,12},{16,20},{24,28},{4,0},{12,8},{20,16},{28,24},{1,5},{9... | collective-permute-start | bytes 368648 | tf_op jit(solution)/shard_map/ppermute | solution.py:520
  8.9 0.7 %collective-permute-start.3 = (f32[15,8,256]{2,1,0:T(8,128)S(1)}, f32[15,8,256]{2,1,0:T(8,128)S(1)}, u32[]{:S(2)}, u32[]{:S(2)}) collective-permute-start(f32[15,8,256]{2,1,0:T(8,128)S(1)} %get-tuple-element.30.odd_out), channel_id=1, source_target_pairs={{4,8},{12,16},{20,24},{8,4},{16,12},{24,20},{5,9},{13,17},{21,25},... | collective-permute-start | bytes 368648 | tf_op jit(solution)/shard_map/ppermute | solution.py:519
  9.6 0.0 copy-done.3
  9.6 0.0 copy-done.4
  9.6 0.0 copy-done.5
  9.6 0.0 copy-done
  9.6 0.0 copy-done.1
  9.6 0.0 copy-done.2
  9.6 0.0 copy-done.7
  9.7 0.0 copy-done.8
  9.7 2.9 %shard_map.115 = (f32[8,32,256]{2,1,0:T(8,128)}, f32[8,32,256]{2,1,0:T(8,128)}, f32[32,256]{1,0:T(8,128)S(1)}) custom-call(f32[8,32,256]{2,1,0:T(8,128)S(1)} %copy-done, f32[8,32,256]{2,1,0:T(8,128)S(1)} %copy-done.1, f32[8,32,256]{2,1,0:T(8,128)S(1)} %copy-done.4, f32[8,32,256]{2,1,0:T(8,128)S(1)} %copy-done.2, f32[8,32,256]{2,1,0:T(8,128)S(1)} %copy-done.5, ...), custom_call_target="tpu_custom_call" | custom-call | tf_op jit(solution)/shard_map/pallas_call | solution.py:524
  12.5 0.0 collective-permute-done.2.even_in
  12.6 0.0 collective-permute-done.3.odd_in
  12.6 0.5 %shard_map.116 = (f32[8,8,256]{2,1,0:T(8,128)S(1)}, f32[8,8,256]{2,1,0:T(8,128)S(1)}, f32[24,256]{1,0:T(8,128)S(1)}, f32[24,256]{1,0:T(8,128)S(1)}, f32[24,256]{1,0:T(8,128)S(1)}, /*index=5*/f32[24,256]{1,0:T(8,128)S(1)}) custom-call(f32[15,8,256]{2,1,0:T(8,128)S(1)} %get-tuple-element.29.even_out, f32[15,8,256]{2,1,0:T(8,128)S(1)} %get-tuple-element.30.odd_out, ...), custom_call_target="tpu_custom_call" | custom-call | tf_op jit(solution)/shard_map/pallas_call | solution.py:535
  13.1 3.4 %collective-permute-start.4 = (f32[24,256]{1,0:T(8,128)S(1)}, f32[24,256]{1,0:T(8,128)S(1)}, u32[]{:S(2)}, u32[]{:S(2)}) collective-permute-start(f32[24,256]{1,0:T(8,128)S(1)} %get-tuple-element.40), channel_id=1, source_target_pairs={{0,1},{1,0},{2,3},{3,2},{4,5},{5,4},{6,7},{7,6},{8,9},{9,8},{10,11... | collective-permute-start | bytes 73736 | tf_op jit(solution)/shard_map/ppermute | solution.py:550
  16.5 1.3 %collective-permute-start.5 = (f32[24,256]{1,0:T(8,128)S(1)}, f32[24,256]{1,0:T(8,128)S(1)}, u32[]{:S(2)}, u32[]{:S(2)}) collective-permute-start(f32[24,256]{1,0:T(8,128)S(1)} %get-tuple-element.41), channel_id=1, source_target_pairs={{0,2},{1,3},{2,0},{3,1},{4,6},{5,7},{6,4},{7,5},{8,10},{9,11},{10,... | collective-permute-start | bytes 73736 | tf_op jit(solution)/shard_map/ppermute | solution.py:550
  17.8 0.2 collective-permute-start.6
  17.9 0.0 collective-permute-done.4.refs_1_
  17.9 2.4 %collective-permute-done.5.refs_2_ = f32[24,256]{1,0:T(8,128)S(1)} collective-permute-done((f32[24,256]{1,0:T(8,128)S(1)}, f32[24,256]{1,0:T(8,128)S(1)}, u32[]{:S(2)}, u32[]{:S(2)}) %collective-permute-start.5) | collective-permute-done | bytes 24608 | tf_op jit(solution)/shard_map/ppermute | solution.py:550
  20.3 0.7 %collective-permute-done.6.refs_3_ = f32[24,256]{1,0:T(8,128)S(1)} collective-permute-done((f32[24,256]{1,0:T(8,128)S(1)}, f32[24,256]{1,0:T(8,128)S(1)}, u32[]{:S(2)}, u32[]{:S(2)}) %collective-permute-start.6) | collective-permute-done | bytes 24608 | tf_op jit(solution)/shard_map/ppermute | solution.py:550
  21.0 1.0 %shard_map.119 = (f32[3,8,1024]{2,1,0:T(8,128)S(1)}, f32[32,1,128]{2,1,0:T(1,128)}) custom-call(f32[24,256]{1,0:T(8,128)S(1)} %get-tuple-element.39.refs_0_, f32[24,256]{1,0:T(8,128)S(1)} %collective-permute-done.4.refs_1_, f32[24,256]{1,0:T(8,128)S(1)} %collective-permute-done.5.refs_2_, f32[24,256]{1,0:T(8,128)S(1)} %collective-permute-done.6.refs_3_, ...), custom_call_target="tpu_custom_call" | custom-call | tf_op jit(solution)/shard_map/pallas_call | solution.py:575
  22.0 8.0 %all-to-all-start = ((f32[32,1,128]{2,1,0:T(1,128)}), f32[32,1,128]{2,1,0:T(1,128)S(1)}, u32[]{:S(2)}, u32[]{:S(2)}) async-start(f32[32,1,128]{2,1,0:T(1,128)} %get-tuple-element.43), calls=%async_computation | async-start | bytes 32768 | tf_op jit(solution)/shard_map/all_to_all | solution.py:583
  30.1 1.6 %shard_map.117 = (f32[8,32,256]{2,1,0:T(8,128)}, f32[8,32,256]{2,1,0:T(8,128)}) custom-call(f32[8,8,256]{2,1,0:T(8,128)S(1)} %get-tuple-element.33.fix_t, f32[8,8,256]{2,1,0:T(8,128)S(1)} %get-tuple-element.34.fix_s, f32[8,32,256]{2,1,0:T(8,128)} %get-tuple-element.35.t_old, ...), custom_call_target="tpu_custom_call", output_to_operand_aliasing={{0}: (2, {}), {1}: (3, {})} | custom-call | tf_op jit(solution)/shard_map/pallas_call | solution.py:553
  31.7 5.4 %all-to-all-done.rows_ref = f32[32,1,128]{2,1,0:T(1,128)S(1)} async-done(((f32[32,1,128]{2,1,0:T(1,128)}), f32[32,1,128]{2,1,0:T(1,128)S(1)}, u32[]{:S(2)}, u32[]{:S(2)}) %all-to-all-start) | async-done | bytes 16416 | tf_op jit(solution)/shard_map/all_to_all | solution.py:583
  37.1 0.8 %shard_map.120 = f32[8,1024]{1,0:T(8,128)} custom-call(f32[32,1,128]{2,1,0:T(1,128)S(1)} %all-to-all-done.rows_ref, f32[3,8,1024]{2,1,0:T(8,128)S(1)} %get-tuple-element.44.basis_ref), custom_call_target="tpu_custom_call" | custom-call | tf_op jit(solution)/shard_map/pallas_call | solution.py:585
  (1 shorter events, 0.0 us)
Async XLA Ops:
  2.2 2.7 %collective-permute-start = (f32[48,128]{1,0:T(8,128)S(1)}, f32[48,128]{1,0:T(8,128)S(1)}, u32[]{:S(2)}, u32[]{:S(2)}) collective-permute-start(f32[48,128]{1,0:T(8,128)S(1)} %get-tuple-element.25), channel_id=1, source_target_pairs={{0,1},{2,3},{1,0},{3,2},{4,5},{6,7},{5,4},{7,6},{8,9},{10,11},{9,8... | collective-permute-start | bytes 73736 | tf_op jit(solution)/shard_map/ppermute | solution.py:491
  2.8 2.2 %copy-start.6 = (f32[8,1024]{1,0:T(8,128)S(1)}, f32[8,1024]{1,0:T(8,128)}, u32[]{:S(2)}) copy-start(f32[8,1024]{1,0:T(8,128)} %main_own.1) | copy-start | bytes 98308
  2.8 2.2 %collective-permute-start.1 = (f32[48,128]{1,0:T(8,128)S(1)}, f32[48,128]{1,0:T(8,128)S(1)}, u32[]{:S(2)}, u32[]{:S(2)}) collective-permute-start(f32[48,128]{1,0:T(8,128)S(1)} %get-tuple-element.26), channel_id=1, source_target_pairs={{1,2},{2,1},{5,6},{6,5},{9,10},{10,9},{13,14},{14,13},{17,18},{18,... | collective-permute-start | bytes 73736 | tf_op jit(solution)/shard_map/ppermute | solution.py:492
  3.5 6.0 %copy-start.3 = (f32[8,32,256]{2,1,0:T(8,128)S(1)}, f32[8,32,256]{2,1,0:T(8,128)}, u32[]{:S(2)}) copy-start(f32[8,32,256]{2,1,0:T(8,128)} %y.5) | copy-start | bytes 786436
  3.6 6.0 %copy-start.4 = (f32[8,32,256]{2,1,0:T(8,128)S(1)}, f32[8,32,256]{2,1,0:T(8,128)}, u32[]{:S(2)}) copy-start(f32[8,32,256]{2,1,0:T(8,128)} %u.3) | copy-start | bytes 786436
  3.6 6.0 %copy-start.5 = (f32[8,32,256]{2,1,0:T(8,128)S(1)}, f32[8,32,256]{2,1,0:T(8,128)}, u32[]{:S(2)}) copy-start(f32[8,32,256]{2,1,0:T(8,128)} %x.3) | copy-start | bytes 786436
  5.0 4.6 %copy-start = (f32[8,32,256]{2,1,0:T(8,128)S(1)}, f32[8,32,256]{2,1,0:T(8,128)}, u32[]{:S(2)}) copy-start(f32[8,32,256]{2,1,0:T(8,128)} %t.5) | copy-start | bytes 786436
  5.0 4.6 %copy-start.1 = (f32[8,32,256]{2,1,0:T(8,128)S(1)}, f32[8,32,256]{2,1,0:T(8,128)}, u32[]{:S(2)}) copy-start(f32[8,32,256]{2,1,0:T(8,128)} %s.5) | copy-start | bytes 786436
  5.0 4.6 %copy-start.2 = (f32[8,32,256]{2,1,0:T(8,128)S(1)}, f32[8,32,256]{2,1,0:T(8,128)}, u32[]{:S(2)}) copy-start(f32[8,32,256]{2,1,0:T(8,128)} %v.5) | copy-start | bytes 786436
  5.0 4.6 %copy-start.7 = (s32[32,256]{1,0:T(8,128)S(1)}, s32[32,256]{1,0:T(8,128)}, u32[]{:S(2)}) copy-start(s32[32,256]{1,0:T(8,128)} %depth.5) | copy-start | bytes 98308
  5.0 4.6 %copy-start.8 = (f32[2,32,256]{2,1,0:T(8,128)S(1)}, f32[2,32,256]{2,1,0:T(8,128)}, u32[]{:S(2)}) copy-start(f32[2,32,256]{2,1,0:T(8,128)} %source.3) | copy-start | bytes 196612
  6.5 6.1 %collective-permute-start.2 = (f32[15,8,256]{2,1,0:T(8,128)S(1)}, f32[15,8,256]{2,1,0:T(8,128)S(1)}, u32[]{:S(2)}, u32[]{:S(2)}) collective-permute-start(f32[15,8,256]{2,1,0:T(8,128)S(1)} %get-tuple-element.29.even_out), channel_id=1, source_target_pairs={{0,4},{8,12},{16,20},{24,28},{4,0},{12,8},{20,16},{28,24},{1,5},{9... | collective-permute-start | bytes 368648 | tf_op jit(solution)/shard_map/ppermute | solution.py:520
  8.9 3.6 %collective-permute-start.3 = (f32[15,8,256]{2,1,0:T(8,128)S(1)}, f32[15,8,256]{2,1,0:T(8,128)S(1)}, u32[]{:S(2)}, u32[]{:S(2)}) collective-permute-start(f32[15,8,256]{2,1,0:T(8,128)S(1)} %get-tuple-element.30.odd_out), channel_id=1, source_target_pairs={{4,8},{12,16},{20,24},{8,4},{16,12},{24,20},{5,9},{13,17},{21,25},... | collective-permute-start | bytes 368648 | tf_op jit(solution)/shard_map/ppermute | solution.py:519
  13.1 4.9 %collective-permute-start.4 = (f32[24,256]{1,0:T(8,128)S(1)}, f32[24,256]{1,0:T(8,128)S(1)}, u32[]{:S(2)}, u32[]{:S(2)}) collective-permute-start(f32[24,256]{1,0:T(8,128)S(1)} %get-tuple-element.40), channel_id=1, source_target_pairs={{0,1},{1,0},{2,3},{3,2},{4,5},{5,4},{6,7},{7,6},{8,9},{9,8},{10,11... | collective-permute-start | bytes 73736 | tf_op jit(solution)/shard_map/ppermute | solution.py:550
  16.5 3.8 %collective-permute-start.5 = (f32[24,256]{1,0:T(8,128)S(1)}, f32[24,256]{1,0:T(8,128)S(1)}, u32[]{:S(2)}, u32[]{:S(2)}) collective-permute-start(f32[24,256]{1,0:T(8,128)S(1)} %get-tuple-element.41), channel_id=1, source_target_pairs={{0,2},{1,3},{2,0},{3,1},{4,6},{5,7},{6,4},{7,5},{8,10},{9,11},{10,... | collective-permute-start | bytes 73736 | tf_op jit(solution)/shard_map/ppermute | solution.py:550
  17.8 3.3 %collective-permute-start.6 = (f32[24,256]{1,0:T(8,128)S(1)}, f32[24,256]{1,0:T(8,128)S(1)}, u32[]{:S(2)}, u32[]{:S(2)}) collective-permute-start(f32[24,256]{1,0:T(8,128)S(1)} %get-tuple-element.42), channel_id=1, source_target_pairs={{0,3},{1,2},{2,1},{3,0},{4,7},{5,6},{6,5},{7,4},{8,11},{9,10},{10,... | collective-permute-start | bytes 73736 | tf_op jit(solution)/shard_map/ppermute | solution.py:550
  22.0 15.1 %all-to-all-start = ((f32[32,1,128]{2,1,0:T(1,128)}), f32[32,1,128]{2,1,0:T(1,128)S(1)}, u32[]{:S(2)}, u32[]{:S(2)}) async-start(f32[32,1,128]{2,1,0:T(1,128)} %get-tuple-element.43), calls=%async_computation | async-start | bytes 32768 | tf_op jit(solution)/shard_map/all_to_all | solution.py:583

commit v5 on v4

--- a/solution.py
+++ b/solution.py
@@ -81,27 +81,75 @@
             odd_ref[at : at + 1, :] = jnp.where(even, up, down)
 
 
-def gather_rows(t, s, u, v, x, y, source, depth, near, near_depth, sems):
-    rows = t.shape[1]
+def gather_rows(across, *refs):
+    fields, depth, main = refs[:7], refs[7], refs[8]
+    near, even_ref, odd_ref, raw, raw_depth, sems = refs[9:]
+    layers, rows = fields[0].shape[:2]
     copies = []
     at = 0
-    for ref in (t, s, u, v, x, y, source):
+    for ref in fields:
         for i, start in enumerate((0, rows - SUB)):
-            planes = near.at[pl.ds(at, ref.shape[0]), pl.ds(i * SUB, SUB)]
+            planes = raw.at[pl.ds(at, ref.shape[0]), pl.ds(i * SUB, SUB)]
             copies.append((ref.at[:, pl.ds(start, SUB)], planes))
         at += ref.shape[0]
     for i, start in enumerate((0, rows - SUB)):
-        copies.append((depth.at[pl.ds(start, SUB)], near_depth.at[pl.ds(i * SUB, SUB)]))
+        copies.append((depth.at[pl.ds(start, SUB)], raw_depth.at[pl.ds(i * SUB, SUB)]))
     copies = [pltpu.make_async_copy(a, b, sems.at[i]) for i, (a, b) in enumerate(copies)]
     for copy in copies:
         copy.start()
     for copy in copies:
         copy.wait()
-
-
-def pack_rows(across, first_ref, from_even, from_odd, near, near_depth, main, edge_ref, even_ref, odd_ref):
+    base = 6 * layers
+    planes = [(raw[p, :SUB], raw[p, SUB:]) for p in range(base + 2)]
+    levels = raw_depth[...].astype(jnp.float32)
+    planes.append((levels[:SUB], levels[SUB:]))
+    line = iota(planes[0][0].shape, 0)
+    for p, (up, down) in enumerate(planes):
+        near[p] = jnp.where(line < SUB // 2, up, down)
+    even = lax.axis_index("bx") % 2 == 0
+
+    def put(q, parts):
+        out_even, out_odd = None, None
+        for p, at, count in parts:
+            up, down = planes[p]
+            up = pltpu.roll(up, at, 0) if at else up
+            down = pltpu.roll(down, (at + count) % SUB, 0)
+            one, two = jnp.where(even, down, up), jnp.where(even, up, down)
+            out_even = one if at == 0 else jnp.where(line >= at, one, out_even)
+            out_odd = two if at == 0 else jnp.where(line >= at, two, out_odd)
+        even_ref[q] = out_even
+        odd_ref[q] = out_odd
+
+    twice, once = row_planes(layers)
+    for q in range(len(twice) // 4):
+        put(q, [(twice[4 * q + j], 2 * j, 2) for j in range(4)])
+    for q in range(len(once) // SUB):
+        put(len(twice) // 4 + q, [(once[SUB * q + j], j, 1) for j in range(SUB)])
+    count = len(twice) // 4 + len(once) // SUB
+    put(count, [(base, 0, 1), (base + 1, 1, 1), (base + 2, 2, 2)])
+    count += 1
+    wide = ITERS - 1
+    strip = main.shape[0]
+    width = fields[0].shape[2]
+    for r in range(wide):
+        for j in range(across):
+            here = slice(j * width, (j + 1) * width)
+            up = main[r : r + 1, here]
+            down = main[strip - wide + r : strip - wide + r + 1, here]
+            q, at = divmod(r * across + j, SUB)
+            even_ref[count + q, at : at + 1, :] = jnp.where(even, down, up)
+            odd_ref[count + q, at : at + 1, :] = jnp.where(even, up, down)
+
+
+def row_planes(layers):
+    kinds = [[kind * layers + k for k in range(layers)] for kind in range(6)]
+    return kinds[0] + kinds[1] + kinds[2] + kinds[4], kinds[3] + kinds[5]
+
+
+def pack_rows(first_ref, from_even, from_odd, near, even_in, odd_in, edge_ref, even_ref, odd_ref):
     rows, half = first_ref.shape[0], LANE // 2
-    layers = near.shape[0] // 6
+    base = near.shape[0] - 3
+    layers = base // 6
     even = lax.axis_index("by") % 2 == 0
     lane = iota((rows, LANE), 1)
     a, b = from_even[:rows, :], from_odd[:rows, :]
@@ -110,46 +158,20 @@
     left = jnp.where(lane < half, left, pltpu.roll(first_ref[...], half, 1))
     edge_ref[:, :LANE] = left
     edge_ref[:, LANE:] = right
-
-    base = 6 * layers
-    depth = near_depth[...].astype(jnp.float32)
-    edge = jnp.concatenate([edge_ref[:SUB, :], edge_ref[rows - SUB :, :]], 0)
+    head, tail = edge_ref[:SUB, :], edge_ref[rows - SUB :, :]
+    line = iota(head.shape, 0)
     _, _, forcing = tile_step(
-        lambda kind, k: near[kind * layers + k], [near[base], near[base + 1]], depth, edge, layers
+        lambda kind, k: near[kind * layers + k],
+        [near[base], near[base + 1]],
+        near[base + 2],
+        jnp.where(line < SUB // 2, head, tail),
+        layers,
     )
+    up = jnp.where(line < 6, pltpu.roll(head, 4, 0), pltpu.roll(forcing, 5, 0))
+    down = jnp.where(line < 6, pltpu.roll(tail, 6, 0), pltpu.roll(forcing, 1, 0))
     even = lax.axis_index("bx") % 2 == 0
-    group = iota((SUB, edge.shape[1]), 0) // 2
-
-    def put(q, planes):
-        out_even, out_odd = None, None
-        for j, (up, down) in enumerate(planes):
-            one = jnp.where(even, down, up)
-            two = jnp.where(even, up, down)
-            one, two = [z if j == 0 else pltpu.roll(z, 2 * j, 0) for z in (one, two)]
-            out_even = one if j == 0 else jnp.where(group == j, one, out_even)
-            out_odd = two if j == 0 else jnp.where(group == j, two, out_odd)
-        even_ref[q] = out_even
-        odd_ref[q] = out_odd
-
-    def ends(plane):
-        return plane[:SUB], pltpu.roll(plane[SUB:], 2, 0)
-
-    for q in range(base // 4):
-        put(q, [ends(near[4 * q + j]) for j in range(4)])
-    put(base // 4, [ends(near[base]), ends(near[base + 1]), ends(depth), ends(edge)])
-    put(base // 4 + 1, [(pltpu.roll(forcing[:SUB], SUB - 1, 0), pltpu.roll(forcing[SUB:], 3, 0))])
-    count = base // 4 + 2
-    wide = ITERS - 1
-    strip = main.shape[0]
-    width = edge.shape[1]
-    for r in range(wide):
-        for j in range(across):
-            here = slice(j * width, (j + 1) * width)
-            up = main[r : r + 1, here]
-            down = main[strip - wide + r : strip - wide + r + 1, here]
-            q, at = divmod(r * across + j, SUB)
-            even_ref[count + q, at : at + 1, :] = jnp.where(even, down, up)
-            odd_ref[count + q, at : at + 1, :] = jnp.where(even, up, down)
+    even_ref[0] = jnp.where(line < 4, even_in[0], jnp.where(even, down, up))
+    odd_ref[0] = jnp.where(line < 4, odd_in[0], jnp.where(even, up, down))
 
 
 def tile_step(get, source, depth, edge, layers):
@@ -277,18 +299,38 @@
     me = lax.axis_index("by")
     shape = (SUB, f_old.shape[1])
     line = iota(shape, 0)
-    planes = []
     base = 6 * layers
-    for q in range(base // 4 + 1):
+    planes = [None] * (base + 4)
+
+    def parts(q):
         sent_even, sent_odd, came_even, came_odd = even_out[q], odd_out[q], even_in[q], odd_in[q]
-        parts = [jnp.where(even, came_odd, came_even), jnp.where(even, sent_odd, sent_even)]
-        parts += [jnp.where(even, sent_even, sent_odd), jnp.where(even, came_even, came_odd)]
-        for j in range(4):
-            total = None
-            for i, part in enumerate(parts):
-                part = part if i == j else pltpu.roll(part, (2 * (i - j)) % SUB, 0)
-                total = part if i == 0 else jnp.where(line // 2 == i, part, total)
-            planes.append(total)
+        four = [jnp.where(even, came_odd, came_even), jnp.where(even, sent_odd, sent_even)]
+        return four + [jnp.where(even, sent_even, sent_odd), jnp.where(even, came_even, came_odd)]
+
+    def take(four, starts, at):
+        total = None
+        for i, part in enumerate(four):
+            part = part if starts[i] == at else pltpu.roll(part, (starts[i] - at) % SUB, 0)
+            total = part if i == 0 else jnp.where(line >= 2 * i, part, total)
+        return total
+
+    two_rows, one_row = (0, 2, 4, 6), (1, 2, 5, 6)
+    twice, once = row_planes(layers)
+    for i, p in enumerate(twice):
+        if i % 4 == 0:
+            four = parts(i // 4)
+        planes[p] = take(four, two_rows, 2 * (i % 4))
+    for i, p in enumerate(once):
+        if i % SUB == 0:
+            four = parts(len(twice) // 4 + i // SUB)
+        planes[p] = take(four, one_row, i % SUB)
+    ahead = len(twice) // 4 + len(once) // SUB
+    four = parts(ahead)
+    planes[base] = take(four, one_row, 0)
+    planes[base + 1] = take(four, one_row, 1)
+    planes[base + 2] = take(four, two_rows, 2)
+    planes[base + 3] = take(four, two_rows, 4)
+    over, under = pltpu.roll(four[0], 7, 0), pltpu.roll(four[3], 3, 0)
     warm, salt, forcing = tile_step(
         lambda kind, k: planes[kind * layers + k],
         [planes[base], planes[base + 1]],
@@ -300,9 +342,6 @@
         for k in range(layers):
             fix[k] = jnp.where(line == 0, pltpu.roll(fresh[k], 6, 0), pltpu.roll(fresh[k], 2, 0))
     top, bottom = pltpu.roll(forcing, 6, 0), pltpu.roll(forcing, 2, 0)
-    ahead = base // 4 + 1
-    over = pltpu.roll(jnp.where(even, odd_in[ahead], even_in[ahead]), 5, 0)
-    under = pltpu.roll(jnp.where(even, even_in[ahead], odd_in[ahead]), 1, 0)
     last = SUB - 1
     field[:SUB, :] = jnp.where(line == last, top, over)
     field[SUB : 2 * SUB, :] = jnp.where(line == 0, top, f_old[:SUB, :])
@@ -342,11 +381,27 @@
             out[under + r : under + r + 1, here] = jnp.where(even, a, b)
 
 
-def patch(fix_t, fix_s, t_old, s_old, t_new, s_new):
-    target = jnp.where(pl.program_id(0) == 0, 0, SUB - 1)
-    mine = iota(t_old.shape, 1) == target
-    t_new[...] = jnp.where(mine, fix_t[...], t_old[...])
-    s_new[...] = jnp.where(mine, fix_s[...], s_old[...])
+def flush(fix_t, fix_s, t_mid, s_mid, t_out, s_out, ends, sems):
+    layers, rows, columns = t_mid.shape
+    inner = pl.ds(SUB, rows - 2 * SUB)
+    copies = []
+
+    def begin(source, target):
+        copies.append(pltpu.make_async_copy(source, target, sems.at[len(copies)]))
+        copies[-1].start()
+
+    for mid, out in ((t_mid, t_out), (s_mid, s_out)):
+        for low in range(0, layers, 2):
+            some = pl.ds(low, 2)
+            begin(mid.at[some, inner], out.at[some, inner])
+    line = iota((layers, SUB, columns), 1)
+    for i, (mid, fix, out) in enumerate(((t_mid, fix_t, t_out), (s_mid, fix_s, s_out))):
+        for j, (start, at) in enumerate(((0, 0), (rows - SUB, SUB - 1))):
+            old = mid[:, start : start + SUB, :]
+            ends[2 * i + j] = jnp.where(line == at, fix[...], old)
+            begin(ends.at[2 * i + j], out.at[:, pl.ds(start, SUB)])
+    for copy in copies:
+        copy.wait()
 
 
 def hop_peer(me, hop, count):
@@ -492,30 +547,35 @@
     from_odd = lax.ppermute(odd, "by", pairs(across, 1))
 
     fields = (t, s, u, v, x, y, source)
-    foot = rows // SUB - 1
-    near = shape_of(6 * layers + 2, 2 * SUB, columns)
-    near_depth = jax.ShapeDtypeStruct((2 * SUB, columns), depth.dtype)
-    near, near_depth = call(
-        gather_rows,
-        grid=(1,),
-        in_specs=[hbm] * 8,
-        out_specs=[whole(near), whole(near_depth)],
-        out_shape=[near, near_depth],
-        scratch_shapes=[pltpu.SemaphoreType.DMA((16,))],
-    )(*(pltpu.with_memory_space_constraint(a, pltpu.HBM) for a in (*fields, depth)))
-
     extra = -(-wide * across // SUB)
+    sides = shape_of(rows, 2 * LANE)
+    near = shape_of(6 * layers + 3, SUB, columns)
+    shared = layers + 2 * layers // SUB
+    rim = shape_of(shared + 1 + extra, SUB, columns)
+    near, even, odd = call(
+        functools.partial(gather_rows, across),
+        grid=(1,),
+        in_specs=[hbm] * 8 + [whole(main)],
+        out_specs=[whole(near), whole(rim), whole(rim)],
+        out_shape=[near, rim, rim],
+        scratch_shapes=[
+            pltpu.VMEM((6 * layers + 2, 2 * SUB, columns), jnp.float32),
+            pltpu.VMEM((2 * SUB, columns), depth.dtype),
+            pltpu.SemaphoreType.DMA((16,)),
+        ],
+    )(*(pltpu.with_memory_space_constraint(a, pltpu.HBM) for a in (*fields, depth)), main)
+
     plane = shape_of(rows, columns)
-    sides = shape_of(rows, 2 * LANE)
-    rim = shape_of(6 * layers // 4 + 2 + extra, SUB, columns)
-    args = (first, from_even, from_odd, near, near_depth, main)
+    args = (first, from_even, from_odd, near)
+    tile = block((1, SUB, columns), shared, 0, 0)
     edge, even, odd = call(
-        functools.partial(pack_rows, across),
-        grid=(1,),
-        in_specs=[whole(a) for a in args],
-        out_specs=[whole(sides), whole(rim), whole(rim)],
+        pack_rows,
+        grid=(1,),
+        in_specs=[whole(a) for a in args] + [tile] * 2,
+        out_specs=[whole(sides), tile, tile],
         out_shape=[sides, rim, rim],
-    )(*args)
+        input_output_aliases={4: 1, 5: 2},
+    )(*args, even, odd)
     odd_in = lax.ppermute(odd, "bx", pairs(along, 1))
     even_in = lax.ppermute(even, "bx", pairs(along, 0))
 
@@ -549,15 +609,18 @@
         route = [(i, hop_peer(i, hop, across)) for i in range(across)]
         came.append(lax.ppermute(sends[hop], "by", route))
 
-    touched = pl.BlockSpec((layers, SUB, columns), lambda i: (0, i * foot, 0))
+    args = (fix_t, fix_s, warm, salt)
     warm, salt = call(
-        patch,
-        grid=(2,),
-        in_specs=[whole(fix), whole(fix), touched, touched],
-        out_specs=[touched, touched],
-        out_shape=[cube, cube],
-        input_output_aliases={2: 0, 3: 1},
-    )(fix_t, fix_s, warm, salt)
+        flush,
+        grid=(1,),
+        in_specs=[whole(a) for a in args],
+        out_specs=[hbm] * 2,
+        out_shape=[cube] * 2,
+        scratch_shapes=[
+            pltpu.VMEM((4, layers, SUB, columns), jnp.float32),
+            pltpu.SemaphoreType.DMA((layers + 4,)),
+        ],
+    )(*args)
 
     basis_shape = shape_of(ITERS, strip, columns * across)
     names = ("bx", "by")
@@ -571,6 +634,7 @@
         out_specs=whole(ready),
         out_shape=ready,
     )(*args)
+    ready, warm, salt = lax.optimization_barrier((ready, warm, salt))
     args = (*came, ready)
     basis, row = call(
         functools.partial(powers, across, along),

time: 38.3 us -> 36.3 us (0.948)
  blocking collectives: 0 us -> 15.2 us
  starting transfers between devices: 17.2 us -> 9.21 us
  waiting for transfers between devices: 8.52 us -> 2.26 us
  Pallas kernels: 11.3 us -> 8.45 us
    all_to_all x0 -> x1, blocking collectives: none -> 15.2 us  [local(): gathered = lax.all_to_all(row, names, 0, 0, tiled=True)]
    all_to_all x1 -> x0, starting transfers between devices: 8.01 us -> none  [local(): gathered = lax.all_to_all(row, names, 0, 0, tiled=True)]
    all_to_all x1 -> x0, waiting for transfers between devices: 5.45 us -> none  [local(): gathered = lax.all_to_all(row, names, 0, 0, tiled=True)]
    pallas_call x3, Pallas kernels: 4.4 us -> 2.93 us  [the longest x1 1.52 us: local(): call(functools.partial(gather_rows, across), grid=(1,), in_specs=[hbm] *...]
    ppermute x3, waiting for transfers between devices: 3.06 us -> 2.25 us  [local(): came.append(lax.ppermute(sends[hop], 'by', route))]
    pallas_call x1, Pallas kernels: 2.88 us -> 2.1 us  [local(): call(inner_tile, grid=(1,), in_specs=[whole(a) for a in args], out_specs=...]
    pallas_call x1, Pallas kernels: 1.04 us -> 0.43 us  [local(): call(functools.partial(powers, across, along), grid=(1,), in_specs=[whole...]
  transfers between devices with their start and end apart: 8 -> 7, of which waited for: 3 -> 2; matrix products, arithmetic and copies ran while one was open for 0% -> 0% of each run, Pallas kernels for 16% -> 13%
where the time goes in v5:
time: 36.3 us; the launch traced here: 36.1 us
  blocking collectives  15.2 us (42%)
  starting transfers between devices  9.21 us (25%)
  Pallas kernels  8.45 us (23%)
  waiting for transfers between devices  2.26 us (6%)
  between operations  0.87 us (2%)
    all_to_all x1, blocking collectives, local(): gathered = lax.all_to_all(row, names, 0, 0, tiled=True)  15.2 us
    ppermute x3, starting transfers between devices, local(): came.append(lax.ppermute(sends[hop], 'by', route))  4.81 us
    ppermute x1, starting transfers between devices, local(): even_in = lax.ppermute(even, 'bx', pairs(along, 0))  2.58 us
    ppermute x3, waiting for transfers between devices, local(): came.append(lax.ppermute(sends[hop], 'by', route))  2.25 us
    pallas_call x1, Pallas kernels, local(): call(inner_tile, grid=(1,), in_specs=[whole(a) for a in args], out_specs=...  2.1 us
    pallas_call x1, Pallas kernels, local(): call(pack_edges, grid=(1,), in_specs=[hbm] * 6, out_specs=[whole(pack), w...  1.6 us
    pallas_call x1, Pallas kernels, local(): call(functools.partial(gather_rows, across), grid=(1,), in_specs=[hbm] *...  1.52 us
    pallas_call x1, Pallas kernels, local(): call(flush, grid=(1,), in_specs=[whole(a) for a in args], out_specs=[hbm]...  0.89 us
  transfers between devices with their start and end apart: 7, of which 2 were waited for; matrix products, arithmetic and copies ran while one was open for 0% of the time, Pallas kernels for 13%

profile of v5, /device:TPU:0, one launch (start us, length us, event | category | flops | bytes accessed | tf_op | source)
XLA Modules:
  0.0 36.1 jit_solution(1637837176272828443)
XLA Ops:
  0.6 0.0 copy-start.6
  0.6 1.6 %shard_map.112 = (f32[32,128]{1,0:T(8,128)S(1)}, f32[48,128]{1,0:T(8,128)S(1)}, f32[48,128]{1,0:T(8,128)S(1)}) custom-call(f32[8,32,256]{2,1,0:T(8,128)} %t.3, f32[8,32,256]{2,1,0:T(8,128)} %s.3, f32[8,32,256]{2,1,0:T(8,128)} %v.3, f32[8,32,256]{2,1,0:T(8,128)} %y.3, s32[32,256]{1,0:T(8,128)} %depth.3, f32[8,1024]{1,0:T(8,128)} %refs_8_.1), custom_call_target="tpu_custom_call" | custom-call | tf_op jit(solution)/shard_map/pallas_call | solution.py:533
  2.2 0.5 %collective-permute-start = (f32[48,128]{1,0:T(8,128)S(1)}, f32[48,128]{1,0:T(8,128)S(1)}, u32[]{:S(2)}, u32[]{:S(2)}) collective-permute-start(f32[48,128]{1,0:T(8,128)S(1)} %get-tuple-element.28), channel_id=1, source_target_pairs={{0,1},{2,3},{1,0},{3,2},{4,5},{6,7},{5,4},{7,6},{8,9},{10,11},{9,8... | collective-permute-start | bytes 73736 | tf_op jit(solution)/shard_map/ppermute | solution.py:546
  2.8 0.7 %collective-permute-start.1 = (f32[48,128]{1,0:T(8,128)S(1)}, f32[48,128]{1,0:T(8,128)S(1)}, u32[]{:S(2)}, u32[]{:S(2)}) collective-permute-start(f32[48,128]{1,0:T(8,128)S(1)} %get-tuple-element.29), channel_id=1, source_target_pairs={{1,2},{2,1},{5,6},{6,5},{9,10},{10,9},{13,14},{14,13},{17,18},{18,... | collective-permute-start | bytes 73736 | tf_op jit(solution)/shard_map/ppermute | solution.py:547
  3.4 0.0 copy-done.6
  3.4 0.0 copy-start.2
  3.4 0.0 copy-start.3
  3.5 0.0 copy-start.4
  3.5 0.0 copy-start.5
  3.5 1.5 %shard_map.114 = (f32[51,8,256]{2,1,0:T(8,128)S(1)}, f32[12,8,256]{2,1,0:T(8,128)S(1)}, f32[12,8,256]{2,1,0:T(8,128)S(1)}) custom-call(f32[8,32,256]{2,1,0:T(8,128)} %t.3, f32[8,32,256]{2,1,0:T(8,128)} %s.3, f32[8,32,256]{2,1,0:T(8,128)} %u.1, f32[8,32,256]{2,1,0:T(8,128)} %v.3, f32[8,32,256]{2,1,0:T(8,128)} %x.1, f32[8,32,256]{2,1,0:T(8,128)} %y.3, ...), custom_call_target="tpu_custom_call" | custom-call | tf_op jit(solution)/shard_map/pallas_call | solution.py:555
  5.0 0.0 collective-permute-done.from_even
  5.0 0.0 collective-permute-done.1.from_odd
  5.0 0.0 copy-start
  5.0 0.0 copy-start.1
  5.1 0.0 copy-start.7
  5.1 0.0 copy-start.8
  5.1 0.5 %shard_map.115 = (f32[32,256]{1,0:T(8,128)S(1)}, f32[12,8,256]{2,1,0:T(8,128)S(1)}, f32[12,8,256]{2,1,0:T(8,128)S(1)}) custom-call(f32[32,128]{1,0:T(8,128)S(1)} %get-tuple-element.30.first_ref, f32[48,128]{1,0:T(8,128)S(1)} %collective-permute-done.from_even, ...), custom_call_target="tpu_custom_call", output_to_operand_aliasing={{1}: (4, {}), {2}: (5, {})} | custom-call | tf_op jit(solution)/shard_map/pallas_call | solution.py:571
  5.6 2.6 %collective-permute-start.2 = (f32[12,8,256]{2,1,0:T(8,128)S(1)}, f32[12,8,256]{2,1,0:T(8,128)S(1)}, u32[]{:S(2)}, u32[]{:S(2)}) collective-permute-start(f32[12,8,256]{2,1,0:T(8,128)S(1)} %get-tuple-element.34.even_out), channel_id=1, source_target_pairs={{0,4},{8,12},{16,20},{24,28},{4,0},{12,8},{20,16},{28,24},{1,5},{9... | collective-permute-start | bytes 294920 | tf_op jit(solution)/shard_map/ppermute | solution.py:580
  8.2 0.7 %collective-permute-start.3 = (f32[12,8,256]{2,1,0:T(8,128)S(1)}, f32[12,8,256]{2,1,0:T(8,128)S(1)}, u32[]{:S(2)}, u32[]{:S(2)}) collective-permute-start(f32[12,8,256]{2,1,0:T(8,128)S(1)} %get-tuple-element.35.odd_out), channel_id=1, source_target_pairs={{4,8},{12,16},{20,24},{8,4},{16,12},{24,20},{5,9},{13,17},{21,25},... | collective-permute-start | bytes 294920 | tf_op jit(solution)/shard_map/ppermute | solution.py:579
  8.8 0.0 copy-done.2
  8.9 0.0 copy-done.3
  8.9 0.0 copy-done.4
  8.9 0.0 copy-done.5
  8.9 0.0 copy-done
  8.9 0.0 copy-done.1
  8.9 0.0 copy-done.7
  8.9 0.0 copy-done.8
  8.9 2.1 %shard_map.116 = (f32[8,32,256]{2,1,0:T(8,128)S(1)}, f32[8,32,256]{2,1,0:T(8,128)S(1)}, f32[32,256]{1,0:T(8,128)S(1)}) custom-call(f32[8,32,256]{2,1,0:T(8,128)S(1)} %copy-done, f32[8,32,256]{2,1,0:T(8,128)S(1)} %copy-done.1, f32[8,32,256]{2,1,0:T(8,128)S(1)} %copy-done.4, f32[8,32,256]{2,1,0:T(8,128)S(1)} %copy-done.2, f32[8,32,256]{2,1,0:T(8,128)S(1)} %copy-done.5, ...), custom_call_target="tpu_custom_call" | custom-call | tf_op jit(solution)/shard_map/pallas_call | solution.py:584
  11.0 0.0 collective-permute-done.2.even_in
  11.0 0.0 collective-permute-done.3.odd_in
  11.1 0.5 %shard_map.117 = (f32[8,8,256]{2,1,0:T(8,128)S(1)}, f32[8,8,256]{2,1,0:T(8,128)S(1)}, f32[24,256]{1,0:T(8,128)S(1)}, f32[24,256]{1,0:T(8,128)S(1)}, f32[24,256]{1,0:T(8,128)S(1)}, /*index=5*/f32[24,256]{1,0:T(8,128)S(1)}) custom-call(f32[12,8,256]{2,1,0:T(8,128)S(1)} %get-tuple-element.34.even_out, f32[12,8,256]{2,1,0:T(8,128)S(1)} %get-tuple-element.35.odd_out, ...), custom_call_target="tpu_custom_call" | custom-call | tf_op jit(solution)/shard_map/pallas_call | solution.py:595
  11.6 3.1 %collective-permute-start.4 = (f32[24,256]{1,0:T(8,128)S(1)}, f32[24,256]{1,0:T(8,128)S(1)}, u32[]{:S(2)}, u32[]{:S(2)}) collective-permute-start(f32[24,256]{1,0:T(8,128)S(1)} %get-tuple-element.47), channel_id=1, source_target_pairs={{0,1},{1,0},{2,3},{3,2},{4,5},{5,4},{6,7},{7,6},{8,9},{9,8},{10,11... | collective-permute-start | bytes 73736 | tf_op jit(solution)/shard_map/ppermute | solution.py:610
  14.7 1.6 %collective-permute-start.5 = (f32[24,256]{1,0:T(8,128)S(1)}, f32[24,256]{1,0:T(8,128)S(1)}, u32[]{:S(2)}, u32[]{:S(2)}) collective-permute-start(f32[24,256]{1,0:T(8,128)S(1)} %get-tuple-element.48), channel_id=1, source_target_pairs={{0,2},{1,3},{2,0},{3,1},{4,6},{5,7},{6,4},{7,5},{8,10},{9,11},{10,... | collective-permute-start | bytes 73736 | tf_op jit(solution)/shard_map/ppermute | solution.py:610
  16.3 0.1 collective-permute-start.6
  16.4 0.9 %shard_map.118 = (f32[8,32,256]{2,1,0:T(8,128)}, f32[8,32,256]{2,1,0:T(8,128)}) custom-call(f32[8,8,256]{2,1,0:T(8,128)S(1)} %get-tuple-element.38.fix_t, f32[8,8,256]{2,1,0:T(8,128)S(1)} %get-tuple-element.39.fix_s, f32[8,32,256]{2,1,0:T(8,128)S(1)} %get-tuple-element.40.t_mid, f32[8,32,256]{2,1,0:T(8,128)S(1)} %get-tuple-element.41.s_mid), custom_call_target="tpu_custom_call" | custom-call | tf_op jit(solution)/shard_map/pallas_call | solution.py:613
  17.3 0.0 collective-permute-done.4.refs_1_
  17.3 1.2 %collective-permute-done.5.refs_2_ = f32[24,256]{1,0:T(8,128)S(1)} collective-permute-done((f32[24,256]{1,0:T(8,128)S(1)}, f32[24,256]{1,0:T(8,128)S(1)}, u32[]{:S(2)}, u32[]{:S(2)}) %collective-permute-start.5) | collective-permute-done | bytes 24608 | tf_op jit(solution)/shard_map/ppermute | solution.py:610
  18.5 1.1 %collective-permute-done.6.refs_3_ = f32[24,256]{1,0:T(8,128)S(1)} collective-permute-done((f32[24,256]{1,0:T(8,128)S(1)}, f32[24,256]{1,0:T(8,128)S(1)}, u32[]{:S(2)}, u32[]{:S(2)}) %collective-permute-start.6) | collective-permute-done | bytes 24608 | tf_op jit(solution)/shard_map/ppermute | solution.py:610
  19.6 0.4 %shard_map.119 = (f32[3,8,1024]{2,1,0:T(8,128)S(1)}, f32[32,1,128]{2,1,0:T(1,128)S(1)}) custom-call(f32[24,256]{1,0:T(8,128)S(1)} %get-tuple-element.46.refs_0_, f32[24,256]{1,0:T(8,128)S(1)} %collective-permute-done.4.refs_1_, f32[24,256]{1,0:T(8,128)S(1)} %collective-permute-done.5.refs_2_, f32[24,256]{1,0:T(8,128)S(1)} %collective-permute-done.6.refs_3_, ...), custom_call_target="tpu_custom_call" | custom-call | tf_op jit(solution)/shard_map/pallas_call | solution.py:639
  20.0 15.2 %all_to_all.5.rows_ref = f32[32,1,128]{2,1,0:T(1,128)S(1)} all-to-all(f32[32,1,128]{2,1,0:T(1,128)S(1)} %get-tuple-element.51), channel_id=1, replica_groups=mesh['bx'=8,'by'=4] {'bx','by'}, dimensions={0} | all-to-all | bytes 32768 | tf_op jit(solution)/shard_map/all_to_all | solution.py:647
  35.2 0.8 %shard_map.120 = f32[8,1024]{1,0:T(8,128)} custom-call(f32[32,1,128]{2,1,0:T(1,128)S(1)} %all_to_all.5.rows_ref, f32[3,8,1024]{2,1,0:T(8,128)S(1)} %get-tuple-element.52.basis_ref), custom_call_target="tpu_custom_call" | custom-call | tf_op jit(solution)/shard_map/pallas_call | solution.py:649
  (1 shorter events, 0.0 us)
Async XLA Ops:
  0.6 2.8 %copy-start.6 = (f32[8,1024]{1,0:T(8,128)S(1)}, f32[8,1024]{1,0:T(8,128)}, u32[]{:S(2)}) copy-start(f32[8,1024]{1,0:T(8,128)} %refs_8_.1) | copy-start | bytes 98308
  2.2 2.8 %collective-permute-start = (f32[48,128]{1,0:T(8,128)S(1)}, f32[48,128]{1,0:T(8,128)S(1)}, u32[]{:S(2)}, u32[]{:S(2)}) collective-permute-start(f32[48,128]{1,0:T(8,128)S(1)} %get-tuple-element.28), channel_id=1, source_target_pairs={{0,1},{2,3},{1,0},{3,2},{4,5},{6,7},{5,4},{7,6},{8,9},{10,11},{9,8... | collective-permute-start | bytes 73736 | tf_op jit(solution)/shard_map/ppermute | solution.py:546
  2.8 2.3 %collective-permute-start.1 = (f32[48,128]{1,0:T(8,128)S(1)}, f32[48,128]{1,0:T(8,128)S(1)}, u32[]{:S(2)}, u32[]{:S(2)}) collective-permute-start(f32[48,128]{1,0:T(8,128)S(1)} %get-tuple-element.29), channel_id=1, source_target_pairs={{1,2},{2,1},{5,6},{6,5},{9,10},{10,9},{13,14},{14,13},{17,18},{18,... | collective-permute-start | bytes 73736 | tf_op jit(solution)/shard_map/ppermute | solution.py:547
  3.4 5.4 %copy-start.2 = (f32[8,32,256]{2,1,0:T(8,128)S(1)}, f32[8,32,256]{2,1,0:T(8,128)}, u32[]{:S(2)}) copy-start(f32[8,32,256]{2,1,0:T(8,128)} %v.3) | copy-start | bytes 786436
  3.4 5.4 %copy-start.3 = (f32[8,32,256]{2,1,0:T(8,128)S(1)}, f32[8,32,256]{2,1,0:T(8,128)}, u32[]{:S(2)}) copy-start(f32[8,32,256]{2,1,0:T(8,128)} %y.3) | copy-start | bytes 786436
  3.5 5.4 %copy-start.4 = (f32[8,32,256]{2,1,0:T(8,128)S(1)}, f32[8,32,256]{2,1,0:T(8,128)}, u32[]{:S(2)}) copy-start(f32[8,32,256]{2,1,0:T(8,128)} %u.1) | copy-start | bytes 786436
  3.5 5.4 %copy-start.5 = (f32[8,32,256]{2,1,0:T(8,128)S(1)}, f32[8,32,256]{2,1,0:T(8,128)}, u32[]{:S(2)}) copy-start(f32[8,32,256]{2,1,0:T(8,128)} %x.1) | copy-start | bytes 786436
  5.0 3.9 %copy-start = (f32[8,32,256]{2,1,0:T(8,128)S(1)}, f32[8,32,256]{2,1,0:T(8,128)}, u32[]{:S(2)}) copy-start(f32[8,32,256]{2,1,0:T(8,128)} %t.3) | copy-start | bytes 786436
  5.0 3.8 %copy-start.1 = (f32[8,32,256]{2,1,0:T(8,128)S(1)}, f32[8,32,256]{2,1,0:T(8,128)}, u32[]{:S(2)}) copy-start(f32[8,32,256]{2,1,0:T(8,128)} %s.3) | copy-start | bytes 786436
  5.1 3.8 %copy-start.7 = (s32[32,256]{1,0:T(8,128)S(1)}, s32[32,256]{1,0:T(8,128)}, u32[]{:S(2)}) copy-start(s32[32,256]{1,0:T(8,128)} %depth.3) | copy-start | bytes 98308
  5.1 3.8 %copy-start.8 = (f32[2,32,256]{2,1,0:T(8,128)S(1)}, f32[2,32,256]{2,1,0:T(8,128)}, u32[]{:S(2)}) copy-start(f32[2,32,256]{2,1,0:T(8,128)} %source.1) | copy-start | bytes 196612
  5.6 5.4 %collective-permute-start.2 = (f32[12,8,256]{2,1,0:T(8,128)S(1)}, f32[12,8,256]{2,1,0:T(8,128)S(1)}, u32[]{:S(2)}, u32[]{:S(2)}) collective-permute-start(f32[12,8,256]{2,1,0:T(8,128)S(1)} %get-tuple-element.34.even_out), channel_id=1, source_target_pairs={{0,4},{8,12},{16,20},{24,28},{4,0},{12,8},{20,16},{28,24},{1,5},{9... | collective-permute-start | bytes 294920 | tf_op jit(solution)/shard_map/ppermute | solution.py:580
  8.2 2.9 %collective-permute-start.3 = (f32[12,8,256]{2,1,0:T(8,128)S(1)}, f32[12,8,256]{2,1,0:T(8,128)S(1)}, u32[]{:S(2)}, u32[]{:S(2)}) collective-permute-start(f32[12,8,256]{2,1,0:T(8,128)S(1)} %get-tuple-element.35.odd_out), channel_id=1, source_target_pairs={{4,8},{12,16},{20,24},{8,4},{16,12},{24,20},{5,9},{13,17},{21,25},... | collective-permute-start | bytes 294920 | tf_op jit(solution)/shard_map/ppermute | solution.py:579
  11.6 5.7 %collective-permute-start.4 = (f32[24,256]{1,0:T(8,128)S(1)}, f32[24,256]{1,0:T(8,128)S(1)}, u32[]{:S(2)}, u32[]{:S(2)}) collective-permute-start(f32[24,256]{1,0:T(8,128)S(1)} %get-tuple-element.47), channel_id=1, source_target_pairs={{0,1},{1,0},{2,3},{3,2},{4,5},{5,4},{6,7},{7,6},{8,9},{9,8},{10,11... | collective-permute-start | bytes 73736 | tf_op jit(solution)/shard_map/ppermute | solution.py:610
  14.7 3.8 %collective-permute-start.5 = (f32[24,256]{1,0:T(8,128)S(1)}, f32[24,256]{1,0:T(8,128)S(1)}, u32[]{:S(2)}, u32[]{:S(2)}) collective-permute-start(f32[24,256]{1,0:T(8,128)S(1)} %get-tuple-element.48), channel_id=1, source_target_pairs={{0,2},{1,3},{2,0},{3,1},{4,6},{5,7},{6,4},{7,5},{8,10},{9,11},{10,... | collective-permute-start | bytes 73736 | tf_op jit(solution)/shard_map/ppermute | solution.py:610
  16.3 3.3 %collective-permute-start.6 = (f32[24,256]{1,0:T(8,128)S(1)}, f32[24,256]{1,0:T(8,128)S(1)}, u32[]{:S(2)}, u32[]{:S(2)}) collective-permute-start(f32[24,256]{1,0:T(8,128)S(1)} %get-tuple-element.49), channel_id=1, source_target_pairs={{0,3},{1,2},{2,1},{3,0},{4,7},{5,6},{6,5},{7,4},{8,11},{9,10},{10,... | collective-permute-start | bytes 73736 | tf_op jit(solution)/shard_map/ppermute | solution.py:610

commit v6 on v5

--- a/solution.py
+++ b/solution.py
@@ -146,15 +146,17 @@
     return kinds[0] + kinds[1] + kinds[2] + kinds[4], kinds[3] + kinds[5]
 
 
-def pack_rows(first_ref, from_even, from_odd, near, even_in, odd_in, edge_ref, even_ref, odd_ref):
+def pack_rows(first_ref, from_odd, from_even, near, even_in, odd_in, edge_ref, even_ref, odd_ref):
     rows, half = first_ref.shape[0], LANE // 2
     base = near.shape[0] - 3
     layers = base // 6
     even = lax.axis_index("by") % 2 == 0
     lane = iota((rows, LANE), 1)
     a, b = from_even[:rows, :], from_odd[:rows, :]
-    left = jnp.where(even, b, a)
-    right = jnp.where(even, a, b)
+    left, right = jnp.where(even, b, a), jnp.where(even, a, b)
+    me = lax.axis_index("by")
+    left = jnp.where(me == 0, 0.0, left)
+    right = jnp.where(me == lax.axis_size("by") - 1, 0.0, right)
     left = jnp.where(lane < half, left, pltpu.roll(first_ref[...], half, 1))
     edge_ref[:, :LANE] = left
     edge_ref[:, LANE:] = right
@@ -289,7 +291,7 @@
     f_out[...] = forcing
 
 
-def rim_rows(across, even_out, odd_out, even_in, odd_in, f_old, *refs):
+def rim_rows(across, even_out, odd_out, odd_in, even_in, f_old, *refs):
     layers = refs[0].shape[0]
     t_fix, s_fix = refs[:2]
     sends, (field, blocks) = refs[2 : 2 + across], refs[2 + across :]
@@ -326,6 +328,9 @@
         planes[p] = take(four, one_row, i % SUB)
     ahead = len(twice) // 4 + len(once) // SUB
     four = parts(ahead)
+    me_along = lax.axis_index("bx")
+    four[0] = jnp.where(me_along == 0, 0.0, four[0])
+    four[3] = jnp.where(me_along == lax.axis_size("bx") - 1, 0.0, four[3])
     planes[base] = take(four, one_row, 0)
     planes[base + 1] = take(four, one_row, 1)
     planes[base + 2] = take(four, two_rows, 2)
@@ -417,7 +422,7 @@
 
 
 def powers(across, along, *refs):
-    came = refs[:across]
+    came = [refs[0], *refs[1:across][::-1]]
     main_in, basis_ref, row_ref, field, main = refs[across:]
     tall, columns = main_in.shape
     strip = basis_ref.shape[1]
@@ -513,15 +518,29 @@
     return pl.BlockSpec(shape, lambda *_: index)
 
 
-def pairs(count, start):
+def swaps(count, start):
     both = [(i, i + 1) for i in range(start, count - 1, 2)]
-    return both + [(b, a) for a, b in both]
+    both += [(b, a) for a, b in both]
+    return both, sorted(set(range(count)) - {a for a, _ in both})
+
+
+def across_route(across, start):
+    both, alone = swaps(across, start)
+    return both + list(zip(alone, alone[::-1]))
+
+
+def along_route(along, across, start):
+    both, alone = swaps(along, start)
+    route = [(a * across + i, b * across + i) for a, b in both for i in range(across)]
+    side = dict(across_route(across, 0))
+    return route + [(a * across + i, a * across + side[i]) for a in alone for i in range(across)]
 
 
 def local(t, s, u, v, x, y, source, depth, main):
     layers, rows, columns = t.shape
     across, along = lax.axis_size("by"), lax.axis_size("bx")
     strip = rows // across
+    names = ("bx", "by")
     params = pltpu.CompilerParams(vmem_limit_bytes=48 << 20)
 
     call = functools.partial(pl.pallas_call, compiler_params=params)
@@ -543,8 +562,8 @@
             pltpu.SemaphoreType.DMA((15,)),
         ],
     )(*(pltpu.with_memory_space_constraint(a, pltpu.HBM) for a in (t, s, v, y, depth, main)))
-    from_even = lax.ppermute(even, "by", pairs(across, 0))
-    from_odd = lax.ppermute(odd, "by", pairs(across, 1))
+    from_even = lax.ppermute(even, "by", across_route(across, 0))
+    from_odd = lax.ppermute(odd, "by", across_route(across, 1))
 
     fields = (t, s, u, v, x, y, source)
     extra = -(-wide * across // SUB)
@@ -566,7 +585,7 @@
     )(*(pltpu.with_memory_space_constraint(a, pltpu.HBM) for a in (*fields, depth)), main)
 
     plane = shape_of(rows, columns)
-    args = (first, from_even, from_odd, near)
+    args = (first, from_odd, from_even, near)
     tile = block((1, SUB, columns), shared, 0, 0)
     edge, even, odd = call(
         pack_rows,
@@ -576,8 +595,8 @@
         out_shape=[sides, rim, rim],
         input_output_aliases={4: 1, 5: 2},
     )(*args, even, odd)
-    odd_in = lax.ppermute(odd, "bx", pairs(along, 1))
-    even_in = lax.ppermute(even, "bx", pairs(along, 0))
+    odd_in = lax.ppermute(odd, names, along_route(along, across, 1))
+    even_in = lax.ppermute(even, names, along_route(along, across, 0))
 
     cube = shape_of(layers, rows, columns)
     args = (*fields, depth, edge)
@@ -602,7 +621,7 @@
             pltpu.VMEM((rows + 2 * SUB, columns), jnp.float32),
             pltpu.VMEM((across,) + part.shape, jnp.float32),
         ],
-    )(even, odd, even_in, odd_in, forcing)
+    )(even, odd, odd_in, even_in, forcing)
 
     came = [sends[0]]
     for hop in range(1, across):
@@ -623,7 +642,6 @@
     )(*args)
 
     basis_shape = shape_of(ITERS, strip, columns * across)
-    names = ("bx", "by")
     row_shape = shape_of(across * along, 1, LANE)
     ready = shape_of(tall, columns * across)
     args = (from_even, from_odd, main)
@@ -635,7 +653,7 @@
         out_shape=ready,
     )(*args)
     ready, warm, salt = lax.optimization_barrier((ready, warm, salt))
-    args = (*came, ready)
+    args = (came[0], *came[:0:-1], ready)
     basis, row = call(
         functools.partial(powers, across, along),
         grid=(1,),

time: 36.3 us -> 33.8 us (0.931)
  blocking collectives: 15.2 us -> 11.9 us
  waiting for transfers between devices: 2.26 us -> 4.17 us
  starting transfers between devices: 9.21 us -> 8.25 us
    all_to_all x1, blocking collectives: 15.2 us -> 11.9 us  [local(): gathered = lax.all_to_all(row, names, 0, 0, tiled=True)]
    ppermute x3, starting transfers between devices: 4.81 us -> 1.93 us  [local(): came.append(lax.ppermute(sends[hop], 'by', route))]
    ppermute x4, waiting for transfers between devices: 0.01 us -> 1.97 us  [the longest x1 1.96 us: local(): even_in = lax.ppermute(even, names, along_route(along, across, 0))]
    ppermute x4, starting transfers between devices: 4.4 us -> 6.33 us  [the longest x1 3.04 us: local(): even_in = lax.ppermute(even, names, along_route(along, across, 0))]
  transfers between devices with their start and end apart: 7 -> 7, of which waited for: 2 -> 3; matrix products, arithmetic and copies ran while one was open for 0% -> 0% of each run, Pallas kernels for 13% -> 14%
where the time goes in v6:
time: 33.8 us; the launch traced here: 33.6 us
  blocking collectives  11.9 us (35%)
  Pallas kernels  8.44 us (25%)
  starting transfers between devices  8.25 us (24%)
  waiting for transfers between devices  4.17 us (12%)
  between operations  0.79 us (2%)
    all_to_all x1, blocking collectives, local(): gathered = lax.all_to_all(row, names, 0, 0, tiled=True)  11.9 us
    ppermute x1, starting transfers between devices, local(): even_in = lax.ppermute(even, names, along_route(along, across, 0))  3.04 us
    ppermute x1, starting transfers between devices, local(): from_odd = lax.ppermute(odd, 'by', across_route(across, 1))  2.64 us
    ppermute x3, waiting for transfers between devices, local(): came.append(lax.ppermute(sends[hop], 'by', route))  2.2 us
    pallas_call x1, Pallas kernels, local(): call(inner_tile, grid=(1,), in_specs=[whole(a) for a in args], out_specs=...  2.1 us
    ppermute x1, waiting for transfers between devices, local(): even_in = lax.ppermute(even, names, along_route(along, across, 0))  1.96 us
    ppermute x3, starting transfers between devices, local(): came.append(lax.ppermute(sends[hop], 'by', route))  1.93 us
    pallas_call x1, Pallas kernels, local(): call(pack_edges, grid=(1,), in_specs=[hbm] * 6, out_specs=[whole(pack), w...  1.6 us
  transfers between devices with their start and end apart: 7, of which 3 were waited for; matrix products, arithmetic and copies ran while one was open for 0% of the time, Pallas kernels for 14%

profile of v6, /device:TPU:0, one launch (start us, length us, event | category | flops | bytes accessed | tf_op | source)
XLA Modules:
  0.0 33.6 jit_solution(12930585757074791693)
XLA Ops:
  0.6 0.0 copy-start.6
  0.6 1.6 %shard_map.112 = (f32[32,128]{1,0:T(8,128)S(1)}, f32[48,128]{1,0:T(8,128)S(1)}, f32[48,128]{1,0:T(8,128)S(1)}) custom-call(f32[8,32,256]{2,1,0:T(8,128)} %t.3, f32[8,32,256]{2,1,0:T(8,128)} %s.3, f32[8,32,256]{2,1,0:T(8,128)} %v.3, f32[8,32,256]{2,1,0:T(8,128)} %y.3, s32[32,256]{1,0:T(8,128)} %depth.3, f32[8,1024]{1,0:T(8,128)} %refs_8_.1), custom_call_target="tpu_custom_call" | custom-call | tf_op jit(solution)/shard_map/pallas_call | solution.py:552
  2.2 0.5 %collective-permute-start = (f32[48,128]{1,0:T(8,128)S(1)}, f32[48,128]{1,0:T(8,128)S(1)}, u32[]{:S(2)}, u32[]{:S(2)}) collective-permute-start(f32[48,128]{1,0:T(8,128)S(1)} %get-tuple-element.28), channel_id=1, source_target_pairs={{0,1},{2,3},{1,0},{3,2},{4,5},{6,7},{5,4},{7,6},{8,9},{10,11},{9,8... | collective-permute-start | bytes 73736 | tf_op jit(solution)/shard_map/ppermute | solution.py:565
  2.8 2.6 %collective-permute-start.1 = (f32[48,128]{1,0:T(8,128)S(1)}, f32[48,128]{1,0:T(8,128)S(1)}, u32[]{:S(2)}, u32[]{:S(2)}) collective-permute-start(f32[48,128]{1,0:T(8,128)S(1)} %get-tuple-element.29), channel_id=1, source_target_pairs={{1,2},{2,1},{0,3},{3,0},{5,6},{6,5},{4,7},{7,4},{9,10},{10,9},{8,1... | collective-permute-start | bytes 73736 | tf_op jit(solution)/shard_map/ppermute | solution.py:566
  5.4 0.0 copy-done.6
  5.4 0.0 copy-start.2
  5.4 0.0 copy-start.3
  5.4 0.0 copy-start.4
  5.4 0.0 copy-start.5
  5.4 1.5 %shard_map.114 = (f32[51,8,256]{2,1,0:T(8,128)S(1)}, f32[12,8,256]{2,1,0:T(8,128)S(1)}, f32[12,8,256]{2,1,0:T(8,128)S(1)}) custom-call(f32[8,32,256]{2,1,0:T(8,128)} %t.3, f32[8,32,256]{2,1,0:T(8,128)} %s.3, f32[8,32,256]{2,1,0:T(8,128)} %u.1, f32[8,32,256]{2,1,0:T(8,128)} %v.3, f32[8,32,256]{2,1,0:T(8,128)} %x.1, f32[8,32,256]{2,1,0:T(8,128)} %y.3, ...), custom_call_target="tpu_custom_call" | custom-call | tf_op jit(solution)/shard_map/pallas_call | solution.py:574
  7.0 0.0 collective-permute-done.from_even
  7.0 0.0 collective-permute-done.1.from_odd
  7.0 0.0 copy-start
  7.0 0.0 copy-start.1
  7.0 0.0 copy-start.7
  7.0 0.0 copy-start.8
  7.0 0.5 %shard_map.115 = (f32[32,256]{1,0:T(8,128)S(1)}, f32[12,8,256]{2,1,0:T(8,128)S(1)}, f32[12,8,256]{2,1,0:T(8,128)S(1)}) custom-call(f32[32,128]{1,0:T(8,128)S(1)} %get-tuple-element.30.first_ref, f32[48,128]{1,0:T(8,128)S(1)} %collective-permute-done.1.from_odd, ...), custom_call_target="tpu_custom_call", output_to_operand_aliasing={{1}: (4, {}), {2}: (5, {})} | custom-call | tf_op jit(solution)/shard_map/pallas_call | solution.py:590
  7.6 0.1 collective-permute-start.2
  7.7 3.0 %collective-permute-start.3 = (f32[12,8,256]{2,1,0:T(8,128)S(1)}, f32[12,8,256]{2,1,0:T(8,128)S(1)}, u32[]{:S(2)}, u32[]{:S(2)}) collective-permute-start(f32[12,8,256]{2,1,0:T(8,128)S(1)} %get-tuple-element.34.even_out), channel_id=1, source_target_pairs={{0,4},{1,5},{2,6},{3,7},{8,12},{9,13},{10,14},{11,15},{16,20},{17,... | collective-permute-start | bytes 294920 | tf_op jit(solution)/shard_map/ppermute | solution.py:599
  10.7 0.0 copy-done.2
  10.7 0.0 copy-done.3
  10.7 0.0 copy-done.4
  10.7 0.0 copy-done.5
  10.7 0.0 copy-done
  10.8 0.0 copy-done.1
  10.8 0.0 copy-done.7
  10.8 0.0 copy-done.8
  10.8 2.1 %shard_map.116 = (f32[8,32,256]{2,1,0:T(8,128)S(1)}, f32[8,32,256]{2,1,0:T(8,128)S(1)}, f32[32,256]{1,0:T(8,128)S(1)}) custom-call(f32[8,32,256]{2,1,0:T(8,128)S(1)} %copy-done, f32[8,32,256]{2,1,0:T(8,128)S(1)} %copy-done.1, f32[8,32,256]{2,1,0:T(8,128)S(1)} %copy-done.4, f32[8,32,256]{2,1,0:T(8,128)S(1)} %copy-done.2, f32[8,32,256]{2,1,0:T(8,128)S(1)} %copy-done.5, ...), custom_call_target="tpu_custom_call" | custom-call | tf_op jit(solution)/shard_map/pallas_call | solution.py:603
  12.9 0.0 collective-permute-done.2.odd_in
  12.9 2.0 %collective-permute-done.3.even_in = f32[12,8,256]{2,1,0:T(8,128)S(1)} collective-permute-done((f32[12,8,256]{2,1,0:T(8,128)S(1)}, f32[12,8,256]{2,1,0:T(8,128)S(1)}, u32[]{:S(2)}, u32[]{:S(2)}) %collective-permute-start.3) | collective-permute-done | bytes 98336 | tf_op jit(solution)/shard_map/ppermute | solution.py:599
  14.9 0.5 %shard_map.117 = (f32[8,8,256]{2,1,0:T(8,128)S(1)}, f32[8,8,256]{2,1,0:T(8,128)S(1)}, f32[24,256]{1,0:T(8,128)S(1)}, f32[24,256]{1,0:T(8,128)S(1)}, f32[24,256]{1,0:T(8,128)S(1)}, /*index=5*/f32[24,256]{1,0:T(8,128)S(1)}) custom-call(f32[12,8,256]{2,1,0:T(8,128)S(1)} %get-tuple-element.34.even_out, f32[12,8,256]{2,1,0:T(8,128)S(1)} %get-tuple-element.35.odd_out, ...), custom_call_target="tpu_custom_call" | custom-call | tf_op jit(solution)/shard_map/pallas_call | solution.py:614
  15.4 1.2 %collective-permute-start.4 = (f32[24,256]{1,0:T(8,128)S(1)}, f32[24,256]{1,0:T(8,128)S(1)}, u32[]{:S(2)}, u32[]{:S(2)}) collective-permute-start(f32[24,256]{1,0:T(8,128)S(1)} %get-tuple-element.47), channel_id=1, source_target_pairs={{0,3},{1,2},{2,1},{3,0},{4,7},{5,6},{6,5},{7,4},{8,11},{9,10},{10,... | collective-permute-start | bytes 73736 | tf_op jit(solution)/shard_map/ppermute | solution.py:629
  16.6 0.5 %collective-permute-start.5 = (f32[24,256]{1,0:T(8,128)S(1)}, f32[24,256]{1,0:T(8,128)S(1)}, u32[]{:S(2)}, u32[]{:S(2)}) collective-permute-start(f32[24,256]{1,0:T(8,128)S(1)} %get-tuple-element.48), channel_id=1, source_target_pairs={{0,2},{1,3},{2,0},{3,1},{4,6},{5,7},{6,4},{7,5},{8,10},{9,11},{10,... | collective-permute-start | bytes 73736 | tf_op jit(solution)/shard_map/ppermute | solution.py:629
  17.1 0.2 collective-permute-start.6
  17.3 0.9 %shard_map.118 = (f32[8,32,256]{2,1,0:T(8,128)}, f32[8,32,256]{2,1,0:T(8,128)}) custom-call(f32[8,8,256]{2,1,0:T(8,128)S(1)} %get-tuple-element.38.fix_t, f32[8,8,256]{2,1,0:T(8,128)S(1)} %get-tuple-element.39.fix_s, f32[8,32,256]{2,1,0:T(8,128)S(1)} %get-tuple-element.40.t_mid, f32[8,32,256]{2,1,0:T(8,128)S(1)} %get-tuple-element.41.s_mid), custom_call_target="tpu_custom_call" | custom-call | tf_op jit(solution)/shard_map/pallas_call | solution.py:632
  18.2 0.5 %collective-permute-done.4.refs_1_ = f32[24,256]{1,0:T(8,128)S(1)} collective-permute-done((f32[24,256]{1,0:T(8,128)S(1)}, f32[24,256]{1,0:T(8,128)S(1)}, u32[]{:S(2)}, u32[]{:S(2)}) %collective-permute-start.4) | collective-permute-done | bytes 24608 | tf_op jit(solution)/shard_map/ppermute | solution.py:629
  18.8 1.7 %collective-permute-done.5.refs_2_ = f32[24,256]{1,0:T(8,128)S(1)} collective-permute-done((f32[24,256]{1,0:T(8,128)S(1)}, f32[24,256]{1,0:T(8,128)S(1)}, u32[]{:S(2)}, u32[]{:S(2)}) %collective-permute-start.5) | collective-permute-done | bytes 24608 | tf_op jit(solution)/shard_map/ppermute | solution.py:629
  20.4 0.0 collective-permute-done.6.refs_3_
  20.4 0.4 %shard_map.119 = (f32[3,8,1024]{2,1,0:T(8,128)S(1)}, f32[32,1,128]{2,1,0:T(1,128)S(1)}) custom-call(f32[24,256]{1,0:T(8,128)S(1)} %get-tuple-element.46.refs_0_, f32[24,256]{1,0:T(8,128)S(1)} %collective-permute-done.4.refs_1_, f32[24,256]{1,0:T(8,128)S(1)} %collective-permute-done.5.refs_2_, f32[24,256]{1,0:T(8,128)S(1)} %collective-permute-done.6.refs_3_, ...), custom_call_target="tpu_custom_call" | custom-call | tf_op jit(solution)/shard_map/pallas_call | solution.py:657
  20.9 11.9 %all_to_all.5.rows_ref = f32[32,1,128]{2,1,0:T(1,128)S(1)} all-to-all(f32[32,1,128]{2,1,0:T(1,128)S(1)} %get-tuple-element.51), channel_id=1, replica_groups=mesh['bx'=8,'by'=4] {'bx','by'}, dimensions={0} | all-to-all | bytes 32768 | tf_op jit(solution)/shard_map/all_to_all | solution.py:665
  32.8 0.8 %shard_map.120 = f32[8,1024]{1,0:T(8,128)} custom-call(f32[32,1,128]{2,1,0:T(1,128)S(1)} %all_to_all.5.rows_ref, f32[3,8,1024]{2,1,0:T(8,128)S(1)} %get-tuple-element.52.basis_ref), custom_call_target="tpu_custom_call" | custom-call | tf_op jit(solution)/shard_map/pallas_call | solution.py:667
  (1 shorter events, 0.0 us)
Async XLA Ops:
  0.6 4.8 %copy-start.6 = (f32[8,1024]{1,0:T(8,128)S(1)}, f32[8,1024]{1,0:T(8,128)}, u32[]{:S(2)}) copy-start(f32[8,1024]{1,0:T(8,128)} %refs_8_.1) | copy-start | bytes 98308
  2.2 4.7 %collective-permute-start = (f32[48,128]{1,0:T(8,128)S(1)}, f32[48,128]{1,0:T(8,128)S(1)}, u32[]{:S(2)}, u32[]{:S(2)}) collective-permute-start(f32[48,128]{1,0:T(8,128)S(1)} %get-tuple-element.28), channel_id=1, source_target_pairs={{0,1},{2,3},{1,0},{3,2},{4,5},{6,7},{5,4},{7,6},{8,9},{10,11},{9,8... | collective-permute-start | bytes 73736 | tf_op jit(solution)/shard_map/ppermute | solution.py:565
  2.8 4.2 %collective-permute-start.1 = (f32[48,128]{1,0:T(8,128)S(1)}, f32[48,128]{1,0:T(8,128)S(1)}, u32[]{:S(2)}, u32[]{:S(2)}) collective-permute-start(f32[48,128]{1,0:T(8,128)S(1)} %get-tuple-element.29), channel_id=1, source_target_pairs={{1,2},{2,1},{0,3},{3,0},{5,6},{6,5},{4,7},{7,4},{9,10},{10,9},{8,1... | collective-permute-start | bytes 73736 | tf_op jit(solution)/shard_map/ppermute | solution.py:566
  5.4 5.3 %copy-start.2 = (f32[8,32,256]{2,1,0:T(8,128)S(1)}, f32[8,32,256]{2,1,0:T(8,128)}, u32[]{:S(2)}) copy-start(f32[8,32,256]{2,1,0:T(8,128)} %v.3) | copy-start | bytes 786436
  5.4 5.3 %copy-start.3 = (f32[8,32,256]{2,1,0:T(8,128)S(1)}, f32[8,32,256]{2,1,0:T(8,128)}, u32[]{:S(2)}) copy-start(f32[8,32,256]{2,1,0:T(8,128)} %y.3) | copy-start | bytes 786436
  5.4 5.3 %copy-start.4 = (f32[8,32,256]{2,1,0:T(8,128)S(1)}, f32[8,32,256]{2,1,0:T(8,128)}, u32[]{:S(2)}) copy-start(f32[8,32,256]{2,1,0:T(8,128)} %u.1) | copy-start | bytes 786436
  5.4 5.3 %copy-start.5 = (f32[8,32,256]{2,1,0:T(8,128)S(1)}, f32[8,32,256]{2,1,0:T(8,128)}, u32[]{:S(2)}) copy-start(f32[8,32,256]{2,1,0:T(8,128)} %x.1) | copy-start | bytes 786436
  7.0 3.8 %copy-start = (f32[8,32,256]{2,1,0:T(8,128)S(1)}, f32[8,32,256]{2,1,0:T(8,128)}, u32[]{:S(2)}) copy-start(f32[8,32,256]{2,1,0:T(8,128)} %t.3) | copy-start | bytes 786436
  7.0 3.7 %copy-start.1 = (f32[8,32,256]{2,1,0:T(8,128)S(1)}, f32[8,32,256]{2,1,0:T(8,128)}, u32[]{:S(2)}) copy-start(f32[8,32,256]{2,1,0:T(8,128)} %s.3) | copy-start | bytes 786436
  7.0 3.7 %copy-start.7 = (s32[32,256]{1,0:T(8,128)S(1)}, s32[32,256]{1,0:T(8,128)}, u32[]{:S(2)}) copy-start(s32[32,256]{1,0:T(8,128)} %depth.3) | copy-start | bytes 98308
  7.0 3.7 %copy-start.8 = (f32[2,32,256]{2,1,0:T(8,128)S(1)}, f32[2,32,256]{2,1,0:T(8,128)}, u32[]{:S(2)}) copy-start(f32[2,32,256]{2,1,0:T(8,128)} %source.1) | copy-start | bytes 196612
  7.6 5.3 %collective-permute-start.2 = (f32[12,8,256]{2,1,0:T(8,128)S(1)}, f32[12,8,256]{2,1,0:T(8,128)S(1)}, u32[]{:S(2)}, u32[]{:S(2)}) collective-permute-start(f32[12,8,256]{2,1,0:T(8,128)S(1)} %get-tuple-element.35.odd_out), channel_id=1, source_target_pairs={{4,8},{5,9},{6,10},{7,11},{12,16},{13,17},{14,18},{15,19},{20,24},... | collective-permute-start | bytes 294920 | tf_op jit(solution)/shard_map/ppermute | solution.py:598
  7.7 7.2 %collective-permute-start.3 = (f32[12,8,256]{2,1,0:T(8,128)S(1)}, f32[12,8,256]{2,1,0:T(8,128)S(1)}, u32[]{:S(2)}, u32[]{:S(2)}) collective-permute-start(f32[12,8,256]{2,1,0:T(8,128)S(1)} %get-tuple-element.34.even_out), channel_id=1, source_target_pairs={{0,4},{1,5},{2,6},{3,7},{8,12},{9,13},{10,14},{11,15},{16,20},{17,... | collective-permute-start | bytes 294920 | tf_op jit(solution)/shard_map/ppermute | solution.py:599
  15.4 3.4 %collective-permute-start.4 = (f32[24,256]{1,0:T(8,128)S(1)}, f32[24,256]{1,0:T(8,128)S(1)}, u32[]{:S(2)}, u32[]{:S(2)}) collective-permute-start(f32[24,256]{1,0:T(8,128)S(1)} %get-tuple-element.47), channel_id=1, source_target_pairs={{0,3},{1,2},{2,1},{3,0},{4,7},{5,6},{6,5},{7,4},{8,11},{9,10},{10,... | collective-permute-start | bytes 73736 | tf_op jit(solution)/shard_map/ppermute | solution.py:629
  16.6 3.8 %collective-permute-start.5 = (f32[24,256]{1,0:T(8,128)S(1)}, f32[24,256]{1,0:T(8,128)S(1)}, u32[]{:S(2)}, u32[]{:S(2)}) collective-permute-start(f32[24,256]{1,0:T(8,128)S(1)} %get-tuple-element.48), channel_id=1, source_target_pairs={{0,2},{1,3},{2,0},{3,1},{4,6},{5,7},{6,4},{7,5},{8,10},{9,11},{10,... | collective-permute-start | bytes 73736 | tf_op jit(solution)/shard_map/ppermute | solution.py:629
  17.1 3.3 %collective-permute-start.6 = (f32[24,256]{1,0:T(8,128)S(1)}, f32[24,256]{1,0:T(8,128)S(1)}, u32[]{:S(2)}, u32[]{:S(2)}) collective-permute-start(f32[24,256]{1,0:T(8,128)S(1)} %get-tuple-element.49), channel_id=1, source_target_pairs={{0,1},{1,0},{2,3},{3,2},{4,5},{5,4},{6,7},{7,6},{8,9},{9,8},{10,11... | collective-permute-start | bytes 73736 | tf_op jit(solution)/shard_map/ppermute | solution.py:629

commit v7 on v6

--- a/solution.py
+++ b/solution.py
@@ -108,26 +108,11 @@
         near[p] = jnp.where(line < SUB // 2, up, down)
     even = lax.axis_index("bx") % 2 == 0
 
-    def put(q, parts):
-        out_even, out_odd = None, None
-        for p, at, count in parts:
-            up, down = planes[p]
-            up = pltpu.roll(up, at, 0) if at else up
-            down = pltpu.roll(down, (at + count) % SUB, 0)
-            one, two = jnp.where(even, down, up), jnp.where(even, up, down)
-            out_even = one if at == 0 else jnp.where(line >= at, one, out_even)
-            out_odd = two if at == 0 else jnp.where(line >= at, two, out_odd)
-        even_ref[q] = out_even
-        odd_ref[q] = out_odd
-
-    twice, once = row_planes(layers)
-    for q in range(len(twice) // 4):
-        put(q, [(twice[4 * q + j], 2 * j, 2) for j in range(4)])
-    for q in range(len(once) // SUB):
-        put(len(twice) // 4 + q, [(once[SUB * q + j], j, 1) for j in range(SUB)])
-    count = len(twice) // 4 + len(once) // SUB
-    put(count, [(base, 0, 1), (base + 1, 1, 1), (base + 2, 2, 2)])
-    count += 1
+    mine = row_planes(layers)
+    begin = 2 * layers // SUB + 1
+    for q in range(len(mine) // SUB):
+        put_rows(even_ref, odd_ref, begin + q, [planes[p] for p in mine[q * SUB : (q + 1) * SUB]], even)
+    count = begin + len(mine) // SUB
     wide = ITERS - 1
     strip = main.shape[0]
     width = fields[0].shape[2]
@@ -141,9 +126,21 @@
             odd_ref[count + q, at : at + 1, :] = jnp.where(even, up, down)
 
 
+def put_rows(even_ref, odd_ref, q, planes, even):
+    line = iota(planes[0][0].shape, 0)
+    out_even, out_odd = None, None
+    for j, (up, down) in enumerate(planes):
+        up = pltpu.roll(up, j, 0) if j else up
+        down = pltpu.roll(down, (j + 1) % SUB, 0) if (j + 1) % SUB else down
+        one, two = jnp.where(even, down, up), jnp.where(even, up, down)
+        out_even = one if j == 0 else jnp.where(line >= j, one, out_even)
+        out_odd = two if j == 0 else jnp.where(line >= j, two, out_odd)
+    even_ref[q] = out_even
+    odd_ref[q] = out_odd
+
+
 def row_planes(layers):
-    kinds = [[kind * layers + k for k in range(layers)] for kind in range(6)]
-    return kinds[0] + kinds[1] + kinds[2] + kinds[4], kinds[3] + kinds[5]
+    return [kind * layers + k for kind in (0, 1, 5, 2, 4) for k in range(layers)]
 
 
 def pack_rows(first_ref, from_odd, from_even, near, even_in, odd_in, edge_ref, even_ref, odd_ref):
@@ -162,32 +159,31 @@
     edge_ref[:, LANE:] = right
     head, tail = edge_ref[:SUB, :], edge_ref[rows - SUB :, :]
     line = iota(head.shape, 0)
-    _, _, forcing = tile_step(
+    depth = near[base + 2]
+    stars = stars_of(
         lambda kind, k: near[kind * layers + k],
         [near[base], near[base + 1]],
-        near[base + 2],
+        depth,
         jnp.where(line < SUB // 2, head, tail),
         layers,
+        True,
     )
-    up = jnp.where(line < 6, pltpu.roll(head, 4, 0), pltpu.roll(forcing, 5, 0))
-    down = jnp.where(line < 6, pltpu.roll(tail, 6, 0), pltpu.roll(forcing, 1, 0))
+    _, _, forcing = solve_columns(stars, depth, layers)
     even = lax.axis_index("bx") % 2 == 0
-    even_ref[0] = jnp.where(line < 4, even_in[0], jnp.where(even, down, up))
-    odd_ref[0] = jnp.where(line < 4, odd_in[0], jnp.where(even, up, down))
-
-
-def tile_step(get, source, depth, edge, layers):
-    rows, columns = depth.shape
+    both = stars[0] + stars[1]
+    for q in range(len(both) // SUB):
+        put_rows(even_ref, odd_ref, q, [(p, p) for p in both[q * SUB : (q + 1) * SUB]], even)
+    up = jnp.where(line < 1, depth, jnp.where(line < 2, pltpu.roll(head, 1, 0), pltpu.roll(forcing, 1, 0)))
+    down = jnp.where(line < 2, pltpu.roll(tail, 2, 0), pltpu.roll(forcing, 5, 0))
+    down = jnp.where(line < 1, pltpu.roll(depth, 1, 0), down)
+    q = len(both) // SUB
+    even_ref[q] = jnp.where(even, down, up)
+    odd_ref[q] = jnp.where(even, up, down)
+
+
+def edge_cells(edge, layers):
+    rows = edge.shape[0]
     cells = 2 * layers
-    lane = iota((rows, columns), 1)
-    first, last = lane == 0, lane == columns - 1
-
-    def after(x, fill):
-        return jnp.where(last, fill, left_by(x, 1))
-
-    def before(x, fill):
-        return jnp.where(first, fill, pltpu.roll(x, 1, 1))
-
     level = (iota((rows, LANE), 1) % layers).astype(jnp.float32)
     left, right = edge[:, :LANE], edge[:, LANE:]
     wet_left = level < left_by(left, 3 * cells)
@@ -196,16 +192,45 @@
     cell_left = jnp.where(wet_left, left, 0.0)
     cell_own = jnp.where(wet_own, left_by(left, LANE // 2), 0.0)
     cell_right = jnp.where(wet_right, right, 0.0)
-    slope_left = below(cell_left) - above(cell_left)
-    slope_own = below(cell_own) - above(cell_own)
-    slope_right = below(cell_right) - above(cell_right)
+    return cell_left, cell_own, cell_right, wet_left & wet_own
+
+
+def column_shifts(shape):
+    lane = iota(shape, 1)
+    first, last = lane == 0, lane == shape[1] - 1
+
+    def after(x, fill):
+        return jnp.where(last, fill, left_by(x, 1))
+
+    def before(x, fill):
+        return jnp.where(first, fill, pltpu.roll(x, 1, 1))
+
+    return after, before
+
+
+def stars_of(get, source, depth, edge, layers, open_ends):
+    cells = 2 * layers
+    after, before = column_shifts(depth.shape)
+
+    def under(x):
+        y = below(x)
+        return jnp.where(iota(x.shape, 0) == x.shape[0] - 1, 0.0, y) if open_ends else y
+
+    def over(x):
+        y = above(x)
+        return jnp.where(iota(x.shape, 0) == 0, 0.0, y) if open_ends else y
+
+    left, right = edge[:, :LANE], edge[:, LANE:]
+    cell_left, cell_own, cell_right, wet_both = edge_cells(edge, layers)
+    slope_left = under(cell_left) - over(cell_left)
+    slope_own = under(cell_own) - over(cell_own)
+    slope_right = under(cell_right) - over(cell_right)
     flux_left = left_by(left, cells) * 0.5 * (cell_left + cell_own) - 0.15 * (
         cell_own - cell_left + left_by(left, 2 * cells) * 0.25 * (slope_left + slope_own)
     )
-    flux_left = jnp.where(wet_left & wet_own, flux_left, 0.0)
-
+    flux_left = jnp.where(wet_both, flux_left, 0.0)
     depth_right = right[:, 3 * cells : 3 * cells + 1]
-    depth_east = jnp.minimum(depth, below(depth))
+    depth_east = jnp.minimum(depth, under(depth))
     depth_north = jnp.minimum(depth, after(depth, depth_right))
     stars = ([], [])
     for k in range(layers):
@@ -223,7 +248,7 @@
         for t in range(2):
             one = slice(t * layers + k, t * layers + k + 1)
             cell = jnp.where(wet, get(t, k), 0.0)
-            east, west = below(cell), above(cell)
+            east, west = under(cell), over(cell)
             north = after(cell, cell_right[:, one])
             south = before(cell, cell_left[:, one])
             cross = north - south
@@ -236,6 +261,50 @@
             if k == 0:
                 star = star + source[t]
             stars[t].append(jnp.where(wet, star, 0.0))
+    return stars
+
+
+def joined_stars(part, cells_of, east_speed, east_slope, north_slope, depth, edge, upper, layers):
+    cells = 2 * layers
+    after, before = column_shifts(depth.shape)
+    is_upper = upper(depth.shape)
+    pack_upper = upper((depth.shape[0], LANE))
+
+    def other(x, mine):
+        return jnp.where(mine, below(x), above(x))
+
+    left, right = edge[:, :LANE], edge[:, LANE:]
+    cell_left, cell_own, cell_right, wet_both = edge_cells(edge, layers)
+    cross_left = 0.0375 * left_by(left, 2 * cells)
+    cross_left = cross_left * (other(cell_left, pack_upper) + other(cell_own, pack_upper))
+    cross_left = jnp.where(wet_both, cross_left, 0.0)
+    other_right = other(cell_right, pack_upper)
+    depth_east = jnp.minimum(depth, below(depth))
+    depth_north = jnp.minimum(depth, after(depth, right[:, 3 * cells : 3 * cells + 1]))
+    stars = ([], [])
+    for k in range(layers):
+        wet = depth > k
+        mask = depth_east > k
+        half = 0.5 * east_speed[k]
+        e_here = jnp.where(mask, half + 0.15, 0.0)
+        e_next = jnp.where(mask, half - 0.15, 0.0)
+        e_cross = jnp.where(mask, 0.0375 * east_slope[k], 0.0)
+        n_cross = jnp.where(depth_north > k, 0.0375 * north_slope[k], 0.0)
+        for t in range(2):
+            one = slice(t * layers + k, t * layers + k + 1)
+            cell = jnp.where(wet, cells_of[t][k], 0.0)
+            east = below(cell)
+            cross = after(cell, cell_right[:, one]) - before(cell, cell_left[:, one])
+            flux = e_here * cell + e_next * east - e_cross * (cross + below(cross))
+            beyond = jnp.where(is_upper, east, above(cell))
+            cross = n_cross * (beyond + after(beyond, other_right[:, one]))
+            cross = cross - before(cross, cross_left[:, one])
+            gain = jnp.where(is_upper, cross - flux, above(flux) - cross)
+            stars[t].append(jnp.where(wet, part[t][k] + gain, 0.0))
+    return stars
+
+
+def solve_columns(stars, depth, layers):
     primes, rights = [], ([], [])
     upper = None
     density = 0.8 * stars[1][0] - 0.2 * stars[0][0]
@@ -278,13 +347,11 @@
 def inner_tile(t, s, u, v, x, y, source, depth, edge, t_out, s_out, f_out):
     layers = t.shape[0]
     refs = (t, s, u, v, x, y)
-    warm, salt, forcing = tile_step(
-        lambda kind, k: refs[kind][k],
-        [source[0], source[1]],
-        depth[...].astype(jnp.float32),
-        edge[...],
-        layers,
+    levels = depth[...].astype(jnp.float32)
+    stars = stars_of(
+        lambda kind, k: refs[kind][k], [source[0], source[1]], levels, edge[...], layers, False
     )
+    warm, salt, forcing = solve_columns(stars, levels, layers)
     for k in range(layers):
         t_out[k] = warm[k]
         s_out[k] = salt[k]
@@ -301,48 +368,54 @@
     me = lax.axis_index("by")
     shape = (SUB, f_old.shape[1])
     line = iota(shape, 0)
-    base = 6 * layers
-    planes = [None] * (base + 4)
 
     def parts(q):
         sent_even, sent_odd, came_even, came_odd = even_out[q], odd_out[q], even_in[q], odd_in[q]
         four = [jnp.where(even, came_odd, came_even), jnp.where(even, sent_odd, sent_even)]
         return four + [jnp.where(even, sent_even, sent_odd), jnp.where(even, came_even, came_odd)]
 
-    def take(four, starts, at):
+    def take(four, at):
         total = None
-        for i, part in enumerate(four):
-            part = part if starts[i] == at else pltpu.roll(part, (starts[i] - at) % SUB, 0)
+        for i, (part, place) in enumerate(zip(four, (1, 2, 5, 6))):
+            part = part if place == at else pltpu.roll(part, (place - at) % SUB, 0)
             total = part if i == 0 else jnp.where(line >= 2 * i, part, total)
         return total
 
-    two_rows, one_row = (0, 2, 4, 6), (1, 2, 5, 6)
-    twice, once = row_planes(layers)
-    for i, p in enumerate(twice):
-        if i % 4 == 0:
-            four = parts(i // 4)
-        planes[p] = take(four, two_rows, 2 * (i % 4))
-    for i, p in enumerate(once):
-        if i % SUB == 0:
-            four = parts(len(twice) // 4 + i // SUB)
-        planes[p] = take(four, one_row, i % SUB)
-    ahead = len(twice) // 4 + len(once) // SUB
+    def rows_from(q, count):
+        out = []
+        for i in range(count):
+            if i % SUB == 0:
+                four = parts(q + i // SUB)
+            out.append(take(four, i % SUB))
+        return out
+
+    ahead = 2 * layers // SUB
+    part = rows_from(0, 2 * layers)
+    planes = rows_from(ahead + 1, 5 * layers)
     four = parts(ahead)
     me_along = lax.axis_index("bx")
     four[0] = jnp.where(me_along == 0, 0.0, four[0])
     four[3] = jnp.where(me_along == lax.axis_size("bx") - 1, 0.0, four[3])
-    planes[base] = take(four, one_row, 0)
-    planes[base + 1] = take(four, one_row, 1)
-    planes[base + 2] = take(four, two_rows, 2)
-    planes[base + 3] = take(four, two_rows, 4)
-    over, under = pltpu.roll(four[0], 7, 0), pltpu.roll(four[3], 3, 0)
-    warm, salt, forcing = tile_step(
-        lambda kind, k: planes[kind * layers + k],
-        [planes[base], planes[base + 1]],
-        planes[base + 2],
-        planes[base + 3],
+    depth, edge = take(four, 0), take(four, 1)
+    over, under = pltpu.roll(four[0], 3, 0), pltpu.roll(four[3], 7, 0)
+    kinds = [planes[i * layers : (i + 1) * layers] for i in range(5)]
+
+    def upper(shape):
+        row = iota(shape, 0)
+        return (row == 1) | (row == 5)
+
+    stars = joined_stars(
+        (part[:layers], part[layers:]),
+        (kinds[0], kinds[1]),
+        kinds[3],
+        kinds[4],
+        kinds[2],
+        depth,
+        edge,
+        upper,
         layers,
     )
+    warm, salt, forcing = solve_columns(stars, depth, layers)
     for fix, fresh in ((t_fix, warm), (s_fix, salt)):
         for k in range(layers):
             fix[k] = jnp.where(line == 0, pltpu.roll(fresh[k], 6, 0), pltpu.roll(fresh[k], 2, 0))
@@ -353,7 +426,8 @@
     field[2 * SUB : rows, :] = f_old[SUB : rows - SUB, :]
     field[rows : rows + SUB, :] = jnp.where(line == last, bottom, f_old[rows - SUB :, :])
     field[SUB + rows : 2 * SUB + rows, :] = jnp.where(line == 0, bottom, under)
-    extra = even_out.shape[0] - ahead - 1
+    later = ahead + 1 + 5 * layers // SUB
+    extra = even_out.shape[0] - later
     tall = blocks.shape[1] - extra * SUB
     for peer in range(across):
         start = SUB - ITERS + peer * strip
@@ -361,7 +435,7 @@
         blocks[peer, : stop - start, :] = field[start:stop, :]
     use_even = even == (me == 0)
     for q in range(extra):
-        relay = jnp.where(use_even, even_in[ahead + 1 + q], odd_in[ahead + 1 + q])
+        relay = jnp.where(use_even, even_in[later + q], odd_in[later + q])
         for peer in range(across):
             blocks[peer, tall + q * SUB : tall + (q + 1) * SUB, :] = relay
     for hop in range(across):
@@ -569,8 +643,8 @@
     extra = -(-wide * across // SUB)
     sides = shape_of(rows, 2 * LANE)
     near = shape_of(6 * layers + 3, SUB, columns)
-    shared = layers + 2 * layers // SUB
-    rim = shape_of(shared + 1 + extra, SUB, columns)
+    shared = 2 * layers // SUB + 1
+    rim = shape_of(shared + 5 * layers // SUB + extra, SUB, columns)
     near, even, odd = call(
         functools.partial(gather_rows, across),
         grid=(1,),
@@ -586,7 +660,7 @@
 
     plane = shape_of(rows, columns)
     args = (first, from_odd, from_even, near)
-    tile = block((1, SUB, columns), shared, 0, 0)
+    tile = block((shared, SUB, columns), 0, 0, 0)
     edge, even, odd = call(
         pack_rows,
         grid=(1,),

time: 33.8 us -> 32.8 us (0.970)
  waiting for transfers between devices: 4.17 us -> 3.12 us
    ppermute x1, waiting for transfers between devices: 1.96 us -> 0.91 us  [local(): even_in = lax.ppermute(even, names, along_route(along, across, 0))]
where the time goes in v7:
time: 32.8 us; the launch traced here: 32.6 us
  blocking collectives  11.9 us (36%)
  Pallas kernels  8.4 us (26%)
  starting transfers between devices  8.28 us (25%)
  waiting for transfers between devices  3.12 us (10%)
  between operations  0.79 us (2%)
    all_to_all x1, blocking collectives, local(): gathered = lax.all_to_all(row, names, 0, 0, tiled=True)  11.9 us
    ppermute x1, starting transfers between devices, local(): even_in = lax.ppermute(even, names, along_route(along, across, 0))  3.06 us
    ppermute x1, starting transfers between devices, local(): from_odd = lax.ppermute(odd, 'by', across_route(across, 1))  2.64 us
    ppermute x3, waiting for transfers between devices, local(): came.append(lax.ppermute(sends[hop], 'by', route))  2.2 us
    pallas_call x1, Pallas kernels, local(): call(inner_tile, grid=(1,), in_specs=[whole(a) for a in args], out_specs=...  2.1 us
    ppermute x3, starting transfers between devices, local(): came.append(lax.ppermute(sends[hop], 'by', route))  1.93 us
    pallas_call x1, Pallas kernels, local(): call(pack_edges, grid=(1,), in_specs=[hbm] * 6, out_specs=[whole(pack), w...  1.6 us
    pallas_call x1, Pallas kernels, local(): call(functools.partial(gather_rows, across), grid=(1,), in_specs=[hbm] *...  1.5 us
  transfers between devices with their start and end apart: 7, of which 3 were waited for; matrix products, arithmetic and copies ran while one was open for 0% of the time, Pallas kernels for 14%

profile of v7, /device:TPU:0, one launch (start us, length us, event | category | flops | bytes accessed | tf_op | source)
XLA Modules:
  0.0 32.6 jit_solution(8594638476483896392)
XLA Ops:
  0.6 0.0 copy-start.6
  0.6 1.6 %shard_map.112 = (f32[32,128]{1,0:T(8,128)S(1)}, f32[48,128]{1,0:T(8,128)S(1)}, f32[48,128]{1,0:T(8,128)S(1)}) custom-call(f32[8,32,256]{2,1,0:T(8,128)} %t.3, f32[8,32,256]{2,1,0:T(8,128)} %s.3, f32[8,32,256]{2,1,0:T(8,128)} %v.3, f32[8,32,256]{2,1,0:T(8,128)} %y.3, s32[32,256]{1,0:T(8,128)} %depth.3, f32[8,1024]{1,0:T(8,128)} %refs_8_.1), custom_call_target="tpu_custom_call" | custom-call | tf_op jit(solution)/shard_map/pallas_call | solution.py:626
  2.2 0.5 %collective-permute-start = (f32[48,128]{1,0:T(8,128)S(1)}, f32[48,128]{1,0:T(8,128)S(1)}, u32[]{:S(2)}, u32[]{:S(2)}) collective-permute-start(f32[48,128]{1,0:T(8,128)S(1)} %get-tuple-element.28), channel_id=1, source_target_pairs={{0,1},{2,3},{1,0},{3,2},{4,5},{6,7},{5,4},{7,6},{8,9},{10,11},{9,8... | collective-permute-start | bytes 73736 | tf_op jit(solution)/shard_map/ppermute | solution.py:639
  2.8 2.6 %collective-permute-start.1 = (f32[48,128]{1,0:T(8,128)S(1)}, f32[48,128]{1,0:T(8,128)S(1)}, u32[]{:S(2)}, u32[]{:S(2)}) collective-permute-start(f32[48,128]{1,0:T(8,128)S(1)} %get-tuple-element.29), channel_id=1, source_target_pairs={{1,2},{2,1},{0,3},{3,0},{5,6},{6,5},{4,7},{7,4},{9,10},{10,9},{8,1... | collective-permute-start | bytes 73736 | tf_op jit(solution)/shard_map/ppermute | solution.py:640
  5.4 0.0 copy-done.6
  5.4 0.0 copy-start.2
  5.4 0.0 copy-start.3
  5.4 0.0 copy-start.4
  5.4 0.0 copy-start.5
  5.4 1.5 %shard_map.114 = (f32[51,8,256]{2,1,0:T(8,128)S(1)}, f32[9,8,256]{2,1,0:T(8,128)S(1)}, f32[9,8,256]{2,1,0:T(8,128)S(1)}) custom-call(f32[8,32,256]{2,1,0:T(8,128)} %t.3, f32[8,32,256]{2,1,0:T(8,128)} %s.3, f32[8,32,256]{2,1,0:T(8,128)} %u.1, f32[8,32,256]{2,1,0:T(8,128)} %v.3, f32[8,32,256]{2,1,0:T(8,128)} %x.1, f32[8,32,256]{2,1,0:T(8,128)} %y.3, ...), custom_call_target="tpu_custom_call" | custom-call | tf_op jit(solution)/shard_map/pallas_call | solution.py:648
  6.9 0.0 collective-permute-done.from_even
  7.0 0.0 collective-permute-done.1.from_odd
  7.0 0.0 copy-start
  7.0 0.0 copy-start.1
  7.0 0.0 copy-start.7
  7.0 0.0 copy-start.8
  7.0 0.5 %shard_map.115 = (f32[32,256]{1,0:T(8,128)S(1)}, f32[9,8,256]{2,1,0:T(8,128)S(1)}, f32[9,8,256]{2,1,0:T(8,128)S(1)}) custom-call(f32[32,128]{1,0:T(8,128)S(1)} %get-tuple-element.30.first_ref, f32[48,128]{1,0:T(8,128)S(1)} %collective-permute-done.1.from_odd, ...), custom_call_target="tpu_custom_call", output_to_operand_aliasing={{1}: (4, {}), {2}: (5, {})} | custom-call | tf_op jit(solution)/shard_map/pallas_call | solution.py:664
  7.5 0.1 collective-permute-start.2
  7.7 3.1 %collective-permute-start.3 = (f32[9,8,256]{2,1,0:T(8,128)S(1)}, f32[9,8,256]{2,1,0:T(8,128)S(1)}, u32[]{:S(2)}, u32[]{:S(2)}) collective-permute-start(f32[9,8,256]{2,1,0:T(8,128)S(1)} %get-tuple-element.34.even_out), channel_id=1, source_target_pairs={{0,4},{1,5},{2,6},{3,7},{8,12},{9,13},{10,14},{11,15},{16,20},{17,... | collective-permute-start | bytes 221192 | tf_op jit(solution)/shard_map/ppermute | solution.py:673
  10.7 0.0 copy-done.2
  10.7 0.0 copy-done.3
  10.7 0.0 copy-done.4
  10.7 0.0 copy-done.5
  10.7 0.0 copy-done
  10.8 0.0 copy-done.1
  10.8 0.0 copy-done.7
  10.8 0.0 copy-done.8
  10.8 2.1 %shard_map.116 = (f32[8,32,256]{2,1,0:T(8,128)S(1)}, f32[8,32,256]{2,1,0:T(8,128)S(1)}, f32[32,256]{1,0:T(8,128)S(1)}) custom-call(f32[8,32,256]{2,1,0:T(8,128)S(1)} %copy-done, f32[8,32,256]{2,1,0:T(8,128)S(1)} %copy-done.1, f32[8,32,256]{2,1,0:T(8,128)S(1)} %copy-done.4, f32[8,32,256]{2,1,0:T(8,128)S(1)} %copy-done.2, f32[8,32,256]{2,1,0:T(8,128)S(1)} %copy-done.5, ...), custom_call_target="tpu_custom_call" | custom-call | tf_op jit(solution)/shard_map/pallas_call | solution.py:677
  12.9 0.0 collective-permute-done.2.odd_in
  12.9 0.9 %collective-permute-done.3.even_in = f32[9,8,256]{2,1,0:T(8,128)S(1)} collective-permute-done((f32[9,8,256]{2,1,0:T(8,128)S(1)}, f32[9,8,256]{2,1,0:T(8,128)S(1)}, u32[]{:S(2)}, u32[]{:S(2)}) %collective-permute-start.3) | collective-permute-done | bytes 73760 | tf_op jit(solution)/shard_map/ppermute | solution.py:673
  13.8 0.5 %shard_map.117 = (f32[8,8,256]{2,1,0:T(8,128)S(1)}, f32[8,8,256]{2,1,0:T(8,128)S(1)}, f32[24,256]{1,0:T(8,128)S(1)}, f32[24,256]{1,0:T(8,128)S(1)}, f32[24,256]{1,0:T(8,128)S(1)}, /*index=5*/f32[24,256]{1,0:T(8,128)S(1)}) custom-call(f32[9,8,256]{2,1,0:T(8,128)S(1)} %get-tuple-element.34.even_out, f32[9,8,256]{2,1,0:T(8,128)S(1)} %get-tuple-element.35.odd_out, ...), custom_call_target="tpu_custom_call" | custom-call | tf_op jit(solution)/shard_map/pallas_call | solution.py:688
  14.3 1.2 %collective-permute-start.4 = (f32[24,256]{1,0:T(8,128)S(1)}, f32[24,256]{1,0:T(8,128)S(1)}, u32[]{:S(2)}, u32[]{:S(2)}) collective-permute-start(f32[24,256]{1,0:T(8,128)S(1)} %get-tuple-element.47), channel_id=1, source_target_pairs={{0,3},{1,2},{2,1},{3,0},{4,7},{5,6},{6,5},{7,4},{8,11},{9,10},{10,... | collective-permute-start | bytes 73736 | tf_op jit(solution)/shard_map/ppermute | solution.py:703
  15.5 0.5 %collective-permute-start.5 = (f32[24,256]{1,0:T(8,128)S(1)}, f32[24,256]{1,0:T(8,128)S(1)}, u32[]{:S(2)}, u32[]{:S(2)}) collective-permute-start(f32[24,256]{1,0:T(8,128)S(1)} %get-tuple-element.48), channel_id=1, source_target_pairs={{0,2},{1,3},{2,0},{3,1},{4,6},{5,7},{6,4},{7,5},{8,10},{9,11},{10,... | collective-permute-start | bytes 73736 | tf_op jit(solution)/shard_map/ppermute | solution.py:703
  16.0 0.2 collective-permute-start.6
  16.3 0.9 %shard_map.118 = (f32[8,32,256]{2,1,0:T(8,128)}, f32[8,32,256]{2,1,0:T(8,128)}) custom-call(f32[8,8,256]{2,1,0:T(8,128)S(1)} %get-tuple-element.38.fix_t, f32[8,8,256]{2,1,0:T(8,128)S(1)} %get-tuple-element.39.fix_s, f32[8,32,256]{2,1,0:T(8,128)S(1)} %get-tuple-element.40.t_mid, f32[8,32,256]{2,1,0:T(8,128)S(1)} %get-tuple-element.41.s_mid), custom_call_target="tpu_custom_call" | custom-call | tf_op jit(solution)/shard_map/pallas_call | solution.py:706
  17.2 0.5 %collective-permute-done.4.refs_1_ = f32[24,256]{1,0:T(8,128)S(1)} collective-permute-done((f32[24,256]{1,0:T(8,128)S(1)}, f32[24,256]{1,0:T(8,128)S(1)}, u32[]{:S(2)}, u32[]{:S(2)}) %collective-permute-start.4) | collective-permute-done | bytes 24608 | tf_op jit(solution)/shard_map/ppermute | solution.py:703
  17.7 1.7 %collective-permute-done.5.refs_2_ = f32[24,256]{1,0:T(8,128)S(1)} collective-permute-done((f32[24,256]{1,0:T(8,128)S(1)}, f32[24,256]{1,0:T(8,128)S(1)}, u32[]{:S(2)}, u32[]{:S(2)}) %collective-permute-start.5) | collective-permute-done | bytes 24608 | tf_op jit(solution)/shard_map/ppermute | solution.py:703
  19.4 0.0 collective-permute-done.6.refs_3_
  19.4 0.4 %shard_map.119 = (f32[3,8,1024]{2,1,0:T(8,128)S(1)}, f32[32,1,128]{2,1,0:T(1,128)S(1)}) custom-call(f32[24,256]{1,0:T(8,128)S(1)} %get-tuple-element.46.refs_0_, f32[24,256]{1,0:T(8,128)S(1)} %collective-permute-done.4.refs_1_, f32[24,256]{1,0:T(8,128)S(1)} %collective-permute-done.5.refs_2_, f32[24,256]{1,0:T(8,128)S(1)} %collective-permute-done.6.refs_3_, ...), custom_call_target="tpu_custom_call" | custom-call | tf_op jit(solution)/shard_map/pallas_call | solution.py:731
  19.8 11.9 %all_to_all.5.rows_ref = f32[32,1,128]{2,1,0:T(1,128)S(1)} all-to-all(f32[32,1,128]{2,1,0:T(1,128)S(1)} %get-tuple-element.51), channel_id=1, replica_groups=mesh['bx'=8,'by'=4] {'bx','by'}, dimensions={0} | all-to-all | bytes 32768 | tf_op jit(solution)/shard_map/all_to_all | solution.py:739
  31.7 0.8 %shard_map.120 = f32[8,1024]{1,0:T(8,128)} custom-call(f32[32,1,128]{2,1,0:T(1,128)S(1)} %all_to_all.5.rows_ref, f32[3,8,1024]{2,1,0:T(8,128)S(1)} %get-tuple-element.52.basis_ref), custom_call_target="tpu_custom_call" | custom-call | tf_op jit(solution)/shard_map/pallas_call | solution.py:741
  (1 shorter events, 0.0 us)
Async XLA Ops:
  0.6 4.8 %copy-start.6 = (f32[8,1024]{1,0:T(8,128)S(1)}, f32[8,1024]{1,0:T(8,128)}, u32[]{:S(2)}) copy-start(f32[8,1024]{1,0:T(8,128)} %refs_8_.1) | copy-start | bytes 98308
  2.2 4.7 %collective-permute-start = (f32[48,128]{1,0:T(8,128)S(1)}, f32[48,128]{1,0:T(8,128)S(1)}, u32[]{:S(2)}, u32[]{:S(2)}) collective-permute-start(f32[48,128]{1,0:T(8,128)S(1)} %get-tuple-element.28), channel_id=1, source_target_pairs={{0,1},{2,3},{1,0},{3,2},{4,5},{6,7},{5,4},{7,6},{8,9},{10,11},{9,8... | collective-permute-start | bytes 73736 | tf_op jit(solution)/shard_map/ppermute | solution.py:639
  2.8 4.2 %collective-permute-start.1 = (f32[48,128]{1,0:T(8,128)S(1)}, f32[48,128]{1,0:T(8,128)S(1)}, u32[]{:S(2)}, u32[]{:S(2)}) collective-permute-start(f32[48,128]{1,0:T(8,128)S(1)} %get-tuple-element.29), channel_id=1, source_target_pairs={{1,2},{2,1},{0,3},{3,0},{5,6},{6,5},{4,7},{7,4},{9,10},{10,9},{8,1... | collective-permute-start | bytes 73736 | tf_op jit(solution)/shard_map/ppermute | solution.py:640
  5.4 5.3 %copy-start.2 = (f32[8,32,256]{2,1,0:T(8,128)S(1)}, f32[8,32,256]{2,1,0:T(8,128)}, u32[]{:S(2)}) copy-start(f32[8,32,256]{2,1,0:T(8,128)} %v.3) | copy-start | bytes 786436
  5.4 5.3 %copy-start.3 = (f32[8,32,256]{2,1,0:T(8,128)S(1)}, f32[8,32,256]{2,1,0:T(8,128)}, u32[]{:S(2)}) copy-start(f32[8,32,256]{2,1,0:T(8,128)} %y.3) | copy-start | bytes 786436
  5.4 5.3 %copy-start.4 = (f32[8,32,256]{2,1,0:T(8,128)S(1)}, f32[8,32,256]{2,1,0:T(8,128)}, u32[]{:S(2)}) copy-start(f32[8,32,256]{2,1,0:T(8,128)} %u.1) | copy-start | bytes 786436
  5.4 5.3 %copy-start.5 = (f32[8,32,256]{2,1,0:T(8,128)S(1)}, f32[8,32,256]{2,1,0:T(8,128)}, u32[]{:S(2)}) copy-start(f32[8,32,256]{2,1,0:T(8,128)} %x.1) | copy-start | bytes 786436
  7.0 3.8 %copy-start = (f32[8,32,256]{2,1,0:T(8,128)S(1)}, f32[8,32,256]{2,1,0:T(8,128)}, u32[]{:S(2)}) copy-start(f32[8,32,256]{2,1,0:T(8,128)} %t.3) | copy-start | bytes 786436
  7.0 3.8 %copy-start.1 = (f32[8,32,256]{2,1,0:T(8,128)S(1)}, f32[8,32,256]{2,1,0:T(8,128)}, u32[]{:S(2)}) copy-start(f32[8,32,256]{2,1,0:T(8,128)} %s.3) | copy-start | bytes 786436
  7.0 3.8 %copy-start.7 = (s32[32,256]{1,0:T(8,128)S(1)}, s32[32,256]{1,0:T(8,128)}, u32[]{:S(2)}) copy-start(s32[32,256]{1,0:T(8,128)} %depth.3) | copy-start | bytes 98308
  7.0 3.8 %copy-start.8 = (f32[2,32,256]{2,1,0:T(8,128)S(1)}, f32[2,32,256]{2,1,0:T(8,128)}, u32[]{:S(2)}) copy-start(f32[2,32,256]{2,1,0:T(8,128)} %source.1) | copy-start | bytes 196612
  7.5 5.4 %collective-permute-start.2 = (f32[9,8,256]{2,1,0:T(8,128)S(1)}, f32[9,8,256]{2,1,0:T(8,128)S(1)}, u32[]{:S(2)}, u32[]{:S(2)}) collective-permute-start(f32[9,8,256]{2,1,0:T(8,128)S(1)} %get-tuple-element.35.odd_out), channel_id=1, source_target_pairs={{4,8},{5,9},{6,10},{7,11},{12,16},{13,17},{14,18},{15,19},{20,24},... | collective-permute-start | bytes 221192 | tf_op jit(solution)/shard_map/ppermute | solution.py:672
  7.7 6.1 %collective-permute-start.3 = (f32[9,8,256]{2,1,0:T(8,128)S(1)}, f32[9,8,256]{2,1,0:T(8,128)S(1)}, u32[]{:S(2)}, u32[]{:S(2)}) collective-permute-start(f32[9,8,256]{2,1,0:T(8,128)S(1)} %get-tuple-element.34.even_out), channel_id=1, source_target_pairs={{0,4},{1,5},{2,6},{3,7},{8,12},{9,13},{10,14},{11,15},{16,20},{17,... | collective-permute-start | bytes 221192 | tf_op jit(solution)/shard_map/ppermute | solution.py:673
  14.3 3.4 %collective-permute-start.4 = (f32[24,256]{1,0:T(8,128)S(1)}, f32[24,256]{1,0:T(8,128)S(1)}, u32[]{:S(2)}, u32[]{:S(2)}) collective-permute-start(f32[24,256]{1,0:T(8,128)S(1)} %get-tuple-element.47), channel_id=1, source_target_pairs={{0,3},{1,2},{2,1},{3,0},{4,7},{5,6},{6,5},{7,4},{8,11},{9,10},{10,... | collective-permute-start | bytes 73736 | tf_op jit(solution)/shard_map/ppermute | solution.py:703
  15.5 3.8 %collective-permute-start.5 = (f32[24,256]{1,0:T(8,128)S(1)}, f32[24,256]{1,0:T(8,128)S(1)}, u32[]{:S(2)}, u32[]{:S(2)}) collective-permute-start(f32[24,256]{1,0:T(8,128)S(1)} %get-tuple-element.48), channel_id=1, source_target_pairs={{0,2},{1,3},{2,0},{3,1},{4,6},{5,7},{6,4},{7,5},{8,10},{9,11},{10,... | collective-permute-start | bytes 73736 | tf_op jit(solution)/shard_map/ppermute | solution.py:703
  16.0 3.3 %collective-permute-start.6 = (f32[24,256]{1,0:T(8,128)S(1)}, f32[24,256]{1,0:T(8,128)S(1)}, u32[]{:S(2)}, u32[]{:S(2)}) collective-permute-start(f32[24,256]{1,0:T(8,128)S(1)} %get-tuple-element.49), channel_id=1, source_target_pairs={{0,1},{1,0},{2,3},{3,2},{4,5},{5,4},{6,7},{7,6},{8,9},{9,8},{10,11... | collective-permute-start | bytes 73736 | tf_op jit(solution)/shard_map/ppermute | solution.py:703

commit v8 on v7

--- a/solution.py
+++ b/solution.py
@@ -71,14 +71,12 @@
     odd_ref[:rows, :] = jnp.where(even, first, last)
     strip = lines.shape[0]
     parts = lines.shape[1] // LANE
-    for r in range(wide):
-        for j in range(parts):
-            here = slice(j * LANE, (j + 1) * LANE)
-            up = lines[r : r + 1, here]
-            down = lines[strip - wide + r : strip - wide + r + 1, here]
-            at = rows + r * parts + j
-            even_ref[at : at + 1, :] = jnp.where(even, down, up)
-            odd_ref[at : at + 1, :] = jnp.where(even, up, down)
+    for j in range(parts):
+        here = slice(j * LANE, (j + 1) * LANE)
+        up, down = lines[:wide, here], lines[strip - wide :, here]
+        at = rows + j * wide
+        even_ref[at : at + wide, :] = jnp.where(even, down, up)
+        odd_ref[at : at + wide, :] = jnp.where(even, up, down)
 
 
 def gather_rows(across, *refs):
@@ -116,14 +114,12 @@
     wide = ITERS - 1
     strip = main.shape[0]
     width = fields[0].shape[2]
-    for r in range(wide):
-        for j in range(across):
-            here = slice(j * width, (j + 1) * width)
-            up = main[r : r + 1, here]
-            down = main[strip - wide + r : strip - wide + r + 1, here]
-            q, at = divmod(r * across + j, SUB)
-            even_ref[count + q, at : at + 1, :] = jnp.where(even, down, up)
-            odd_ref[count + q, at : at + 1, :] = jnp.where(even, up, down)
+    for j in range(across):
+        here = slice(j * width, (j + 1) * width)
+        up, down = main[:wide, here], main[strip - wide :, here]
+        q, at = divmod(j * wide, SUB)
+        even_ref[count + q, at : at + wide, :] = jnp.where(even, down, up)
+        odd_ref[count + q, at : at + wide, :] = jnp.where(even, up, down)
 
 
 def put_rows(even_ref, odd_ref, q, planes, even):
@@ -358,7 +354,7 @@
     f_out[...] = forcing
 
 
-def rim_rows(across, even_out, odd_out, odd_in, even_in, f_old, *refs):
+def rim_rows(across, even_out, odd_out, even_in, odd_in, f_old, *refs):
     layers = refs[0].shape[0]
     t_fix, s_fix = refs[:2]
     sends, (field, blocks) = refs[2 : 2 + across], refs[2 + across :]
@@ -428,18 +424,18 @@
     field[SUB + rows : 2 * SUB + rows, :] = jnp.where(line == 0, bottom, under)
     later = ahead + 1 + 5 * layers // SUB
     extra = even_out.shape[0] - later
-    tall = blocks.shape[1] - extra * SUB
+    tall = blocks.shape[1]
     for peer in range(across):
         start = SUB - ITERS + peer * strip
         stop = min(start + tall, field.shape[0])
         blocks[peer, : stop - start, :] = field[start:stop, :]
+    for hop in range(across):
+        sends[hop][:tall, :] = blocks[hop_peer(me, hop, across)]
     use_even = even == (me == 0)
     for q in range(extra):
         relay = jnp.where(use_even, even_in[later + q], odd_in[later + q])
-        for peer in range(across):
-            blocks[peer, tall + q * SUB : tall + (q + 1) * SUB, :] = relay
-    for hop in range(across):
-        sends[hop][...] = blocks[hop_peer(me, hop, across)]
+        for hop in relaying(across):
+            sends[hop][tall + q * SUB : tall + (q + 1) * SUB, :] = relay
 
 
 def main_rows(from_even, from_odd, main_own, out):
@@ -451,13 +447,12 @@
     even = lax.axis_index("by") % 2 == 0
     parts = columns // LANE
     begin = from_even.shape[0] - wide * parts
-    for r in range(wide):
-        for j in range(parts):
-            here = slice(j * LANE, (j + 1) * LANE)
-            at = begin + r * parts + j
-            a, b = from_even[at : at + 1, :], from_odd[at : at + 1, :]
-            out[over + r : over + r + 1, here] = jnp.where(even, b, a)
-            out[under + r : under + r + 1, here] = jnp.where(even, a, b)
+    for j in range(parts):
+        here = slice(j * LANE, (j + 1) * LANE)
+        at = begin + j * wide
+        a, b = from_even[at : at + wide, :], from_odd[at : at + wide, :]
+        out[over : over + wide, here] = jnp.where(even, b, a)
+        out[under : under + wide, here] = jnp.where(even, a, b)
 
 
 def flush(fix_t, fix_s, t_mid, s_mid, t_out, s_out, ends, sems):
@@ -489,6 +484,10 @@
     return (me + hop) % count
 
 
+def relaying(count):
+    return [h for h in range(count) if hop_peer(0, h, count) == count - 1 or hop_peer(count - 1, h, count) == 0]
+
+
 def hop_origin(me, hop, count):
     if count & (count - 1) == 0:
         return me ^ hop
@@ -513,11 +512,10 @@
 
         @pl.when(me == mine)
         def _():
-            for r in range(wide):
-                for j in range(across):
-                    at = tall + r * across + j
-                    here = slice(j * width, (j + 1) * width)
-                    main[start + r : start + r + 1, here] = came[hop][at : at + 1, :]
+            for j in range(across):
+                at = tall + j * wide
+                here = slice(j * width, (j + 1) * width)
+                main[start : start + wide, here] = came[hop][at : at + wide, :]
 
     relayed(ITERS - wide, 0, across - 1)
     relayed(ITERS + strip, across - 1, 0)
@@ -548,28 +546,46 @@
     row_ref[...] = jnp.broadcast_to(row[None], row_ref.shape)
 
 
+def times(x, y):
+    for a, b in ((x, y), (y, x)):
+        if isinstance(a, float) and a in (0.0, 1.0):
+            return b if a else 0.0
+    return x * y
+
+
+def plus(x, y):
+    for a, b in ((x, y), (y, x)):
+        if isinstance(a, float) and a == 0.0:
+            return b
+    return x + y
+
+
 def coefficients(moments):
     def inner(a, b):
-        return sum(x * y * moments[i + j] for i, x in enumerate(a) for j, y in enumerate(b))
-
-    zero = jnp.zeros_like(moments[0])
-    resid = [zero + 1.0]
-    direction = [zero + 1.0]
-    total = [zero] * ITERS
+        total = 0.0
+        for k in range(len(a) + len(b) - 1):
+            part = 0.0
+            for i in range(len(a)):
+                if 0 <= k - i < len(b):
+                    part = plus(part, times(a[i], b[k - i]))
+            total = plus(total, times(part, moments[k]))
+        return total
+
+    resid, direction, total = [1.0], [1.0], [0.0] * ITERS
     norm_now = inner(resid, resid)
     for step in range(ITERS):
-        image = [zero] * (len(direction) + 1)
+        image = [0.0] * (len(direction) + 1)
         for i, x in enumerate(direction):
-            image[i] = image[i] + CENTRE * x
-            image[i + 1] = image[i + 1] + SCALE * x
+            image[i] = plus(image[i], times(CENTRE, x))
+            image[i + 1] = times(SCALE, x)
         alpha = norm_now / inner(direction, image)
         for i, x in enumerate(direction):
-            total[i] = total[i] + alpha * x
+            total[i] = plus(total[i], times(alpha, x))
         if step + 1 < ITERS:
-            resid = [r - alpha * q for r, q in zip(resid + [zero], image)]
+            resid = [plus(r, times(-alpha, q)) for r, q in zip(resid + [0.0], image)]
             norm_next = inner(resid, resid)
             beta = norm_next / norm_now
-            direction = [r + beta * p for r, p in zip(resid, direction + [zero])]
+            direction = [plus(r, times(beta, p)) for r, p in zip(resid, direction + [0.0])]
             norm_now = norm_next
     return total
 
@@ -683,19 +699,19 @@
     )(*args)
 
     tall = -(-(strip + 2 * ITERS) // SUB) * SUB
-    part = shape_of(tall + extra * SUB, columns)
+    parts = [shape_of(tall + extra * SUB * (hop in relaying(across)), columns) for hop in range(across)]
     fix = shape_of(layers, SUB, columns)
     fix_t, fix_s, *sends = call(
         functools.partial(rim_rows, across),
         grid=(1,),
         in_specs=[whole(rim)] * 4 + [whole(plane)],
-        out_specs=[whole(fix)] * 2 + [whole(part)] * across,
-        out_shape=[fix] * 2 + [part] * across,
+        out_specs=[whole(fix)] * 2 + [whole(part) for part in parts],
+        out_shape=[fix] * 2 + parts,
         scratch_shapes=[
             pltpu.VMEM((rows + 2 * SUB, columns), jnp.float32),
-            pltpu.VMEM((across,) + part.shape, jnp.float32),
+            pltpu.VMEM((across, tall, columns), jnp.float32),
         ],
-    )(even, odd, odd_in, even_in, forcing)
+    )(even, odd, even_in, odd_in, forcing)
 
     came = [sends[0]]
     for hop in range(1, across):

time: 32.8 us -> 32.2 us (0.982)
  blocking collectives: 11.9 us -> 13.3 us
  starting transfers between devices: 8.28 us -> 6.9 us
  waiting for transfers between devices: 3.12 us -> 2.56 us
    ppermute x1, starting transfers between devices: 3.06 us -> 1.64 us  [local(): even_in = lax.ppermute(even, names, along_route(along, across, 0))]
    all_to_all x1, blocking collectives: 11.9 us -> 13.3 us  [local(): gathered = lax.all_to_all(row, names, 0, 0, tiled=True)]
    ppermute x3, waiting for transfers between devices: 2.2 us -> 1.13 us  [local(): came.append(lax.ppermute(sends[hop], 'by', route))]
    ppermute x1, waiting for transfers between devices: 0.91 us -> 1.43 us  [local(): even_in = lax.ppermute(even, names, along_route(along, across, 0))]
  transfers between devices with their start and end apart: 7 -> 7, of which waited for: 3 -> 2; matrix products, arithmetic and copies ran while one was open for 0% -> 0% of each run, Pallas kernels for 14% -> 14%
where the time goes in v8:
time: 32.2 us; the launch traced here: 32 us
  blocking collectives  13.3 us (41%)
  Pallas kernels  8.39 us (26%)
  starting transfers between devices  6.9 us (21%)
  waiting for transfers between devices  2.56 us (8%)
  between operations  0.78 us (2%)
    all_to_all x1, blocking collectives, local(): gathered = lax.all_to_all(row, names, 0, 0, tiled=True)  13.3 us
    ppermute x1, starting transfers between devices, local(): from_odd = lax.ppermute(odd, 'by', across_route(across, 1))  2.64 us
    pallas_call x1, Pallas kernels, local(): call(inner_tile, grid=(1,), in_specs=[whole(a) for a in args], out_specs=...  2.1 us
    ppermute x3, starting transfers between devices, local(): came.append(lax.ppermute(sends[hop], 'by', route))  1.93 us
    ppermute x1, starting transfers between devices, local(): even_in = lax.ppermute(even, names, along_route(along, across, 0))  1.64 us
    pallas_call x1, Pallas kernels, local(): call(pack_edges, grid=(1,), in_specs=[hbm] * 6, out_specs=[whole(pack), w...  1.6 us
    pallas_call x1, Pallas kernels, local(): call(functools.partial(gather_rows, across), grid=(1,), in_specs=[hbm] *...  1.51 us
    ppermute x1, waiting for transfers between devices, local(): even_in = lax.ppermute(even, names, along_route(along, across, 0))  1.43 us
  transfers between devices with their start and end apart: 7, of which 2 were waited for; matrix products, arithmetic and copies ran while one was open for 0% of the time, Pallas kernels for 14%

profile of v8, /device:TPU:0, one launch (start us, length us, event | category | flops | bytes accessed | tf_op | source)
XLA Modules:
  0.0 32.0 jit_solution(120017155236640679)
XLA Ops:
  0.6 0.0 copy-start.6
  0.6 1.6 %shard_map.112 = (f32[32,128]{1,0:T(8,128)S(1)}, f32[48,128]{1,0:T(8,128)S(1)}, f32[48,128]{1,0:T(8,128)S(1)}) custom-call(f32[8,32,256]{2,1,0:T(8,128)} %t.3, f32[8,32,256]{2,1,0:T(8,128)} %s.3, f32[8,32,256]{2,1,0:T(8,128)} %v.3, f32[8,32,256]{2,1,0:T(8,128)} %y.3, s32[32,256]{1,0:T(8,128)} %depth.3, f32[8,1024]{1,0:T(8,128)} %refs_8_.1), custom_call_target="tpu_custom_call" | custom-call | tf_op jit(solution)/shard_map/pallas_call | solution.py:642
  2.2 0.5 %collective-permute-start = (f32[48,128]{1,0:T(8,128)S(1)}, f32[48,128]{1,0:T(8,128)S(1)}, u32[]{:S(2)}, u32[]{:S(2)}) collective-permute-start(f32[48,128]{1,0:T(8,128)S(1)} %get-tuple-element.28), channel_id=1, source_target_pairs={{0,1},{2,3},{1,0},{3,2},{4,5},{6,7},{5,4},{7,6},{8,9},{10,11},{9,8... | collective-permute-start | bytes 73736 | tf_op jit(solution)/shard_map/ppermute | solution.py:655
  2.8 2.6 %collective-permute-start.1 = (f32[48,128]{1,0:T(8,128)S(1)}, f32[48,128]{1,0:T(8,128)S(1)}, u32[]{:S(2)}, u32[]{:S(2)}) collective-permute-start(f32[48,128]{1,0:T(8,128)S(1)} %get-tuple-element.29), channel_id=1, source_target_pairs={{1,2},{2,1},{0,3},{3,0},{5,6},{6,5},{4,7},{7,4},{9,10},{10,9},{8,1... | collective-permute-start | bytes 73736 | tf_op jit(solution)/shard_map/ppermute | solution.py:656
  5.4 0.0 copy-done.6
  5.4 0.0 copy-start.2
  5.4 0.0 copy-start.3
  5.4 0.0 copy-start.4
  5.4 0.0 copy-start.5
  5.4 1.5 %shard_map.114 = (f32[51,8,256]{2,1,0:T(8,128)S(1)}, f32[9,8,256]{2,1,0:T(8,128)S(1)}, f32[9,8,256]{2,1,0:T(8,128)S(1)}) custom-call(f32[8,32,256]{2,1,0:T(8,128)} %t.3, f32[8,32,256]{2,1,0:T(8,128)} %s.3, f32[8,32,256]{2,1,0:T(8,128)} %u.1, f32[8,32,256]{2,1,0:T(8,128)} %v.3, f32[8,32,256]{2,1,0:T(8,128)} %x.1, f32[8,32,256]{2,1,0:T(8,128)} %y.3, ...), custom_call_target="tpu_custom_call" | custom-call | tf_op jit(solution)/shard_map/pallas_call | solution.py:664
  6.9 0.0 collective-permute-done.from_even
  7.0 0.0 collective-permute-done.1.from_odd
  7.0 0.0 copy-start
  7.0 0.0 copy-start.1
  7.0 0.0 copy-start.7
  7.0 0.0 copy-start.8
  7.0 0.5 %shard_map.115 = (f32[32,256]{1,0:T(8,128)S(1)}, f32[9,8,256]{2,1,0:T(8,128)S(1)}, f32[9,8,256]{2,1,0:T(8,128)S(1)}) custom-call(f32[32,128]{1,0:T(8,128)S(1)} %get-tuple-element.30.first_ref, f32[48,128]{1,0:T(8,128)S(1)} %collective-permute-done.1.from_odd, ...), custom_call_target="tpu_custom_call", output_to_operand_aliasing={{1}: (4, {}), {2}: (5, {})} | custom-call | tf_op jit(solution)/shard_map/pallas_call | solution.py:680
  7.5 1.6 %collective-permute-start.2 = (f32[9,8,256]{2,1,0:T(8,128)S(1)}, f32[9,8,256]{2,1,0:T(8,128)S(1)}, u32[]{:S(2)}, u32[]{:S(2)}) collective-permute-start(f32[9,8,256]{2,1,0:T(8,128)S(1)} %get-tuple-element.34.even_out), channel_id=1, source_target_pairs={{0,4},{1,5},{2,6},{3,7},{8,12},{9,13},{10,14},{11,15},{16,20},{17,... | collective-permute-start | bytes 221192 | tf_op jit(solution)/shard_map/ppermute | solution.py:689
  9.2 0.2 collective-permute-start.3
  9.4 0.0 copy-done.2
  9.4 0.0 copy-done.3
  9.4 0.0 copy-done.4
  9.4 0.0 copy-done.5
  9.4 0.0 copy-done
  9.4 0.0 copy-done.1
  9.4 0.0 copy-done.7
  9.4 0.0 copy-done.8
  9.4 2.1 %shard_map.116 = (f32[8,32,256]{2,1,0:T(8,128)S(1)}, f32[8,32,256]{2,1,0:T(8,128)S(1)}, f32[32,256]{1,0:T(8,128)S(1)}) custom-call(f32[8,32,256]{2,1,0:T(8,128)S(1)} %copy-done, f32[8,32,256]{2,1,0:T(8,128)S(1)} %copy-done.1, f32[8,32,256]{2,1,0:T(8,128)S(1)} %copy-done.4, f32[8,32,256]{2,1,0:T(8,128)S(1)} %copy-done.2, f32[8,32,256]{2,1,0:T(8,128)S(1)} %copy-done.5, ...), custom_call_target="tpu_custom_call" | custom-call | tf_op jit(solution)/shard_map/pallas_call | solution.py:693
  11.5 1.4 %collective-permute-done.2.even_in = f32[9,8,256]{2,1,0:T(8,128)S(1)} collective-permute-done((f32[9,8,256]{2,1,0:T(8,128)S(1)}, f32[9,8,256]{2,1,0:T(8,128)S(1)}, u32[]{:S(2)}, u32[]{:S(2)}) %collective-permute-start.2) | collective-permute-done | bytes 73760 | tf_op jit(solution)/shard_map/ppermute | solution.py:689
  12.9 0.0 collective-permute-done.3.odd_in
  12.9 0.5 %shard_map.117 = (f32[8,8,256]{2,1,0:T(8,128)S(1)}, f32[8,8,256]{2,1,0:T(8,128)S(1)}, f32[16,256]{1,0:T(8,128)S(1)}, f32[16,256]{1,0:T(8,128)S(1)}, f32[16,256]{1,0:T(8,128)S(1)}, /*index=5*/f32[24,256]{1,0:T(8,128)S(1)}) custom-call(f32[9,8,256]{2,1,0:T(8,128)S(1)} %get-tuple-element.34.even_out, f32[9,8,256]{2,1,0:T(8,128)S(1)} %get-tuple-element.35.odd_out, ...), custom_call_target="tpu_custom_call" | custom-call | tf_op jit(solution)/shard_map/pallas_call | solution.py:704
  13.4 0.2 collective-permute-start.4
  13.7 1.4 %collective-permute-start.5 = (f32[16,256]{1,0:T(8,128)S(1)}, f32[16,256]{1,0:T(8,128)S(1)}, u32[]{:S(2)}, u32[]{:S(2)}) collective-permute-start(f32[16,256]{1,0:T(8,128)S(1)} %get-tuple-element.48), channel_id=1, source_target_pairs={{0,2},{1,3},{2,0},{3,1},{4,6},{5,7},{6,4},{7,5},{8,10},{9,11},{10,... | collective-permute-start | bytes 49160 | tf_op jit(solution)/shard_map/ppermute | solution.py:719
  15.1 0.3 collective-permute-start.6
  15.4 0.9 %shard_map.118 = (f32[8,32,256]{2,1,0:T(8,128)}, f32[8,32,256]{2,1,0:T(8,128)}) custom-call(f32[8,8,256]{2,1,0:T(8,128)S(1)} %get-tuple-element.38.fix_t, f32[8,8,256]{2,1,0:T(8,128)S(1)} %get-tuple-element.39.fix_s, f32[8,32,256]{2,1,0:T(8,128)S(1)} %get-tuple-element.40.t_mid, f32[8,32,256]{2,1,0:T(8,128)S(1)} %get-tuple-element.41.s_mid), custom_call_target="tpu_custom_call" | custom-call | tf_op jit(solution)/shard_map/pallas_call | solution.py:722
  16.3 1.1 %collective-permute-done.5.refs_2_ = f32[16,256]{1,0:T(8,128)S(1)} collective-permute-done((f32[16,256]{1,0:T(8,128)S(1)}, f32[16,256]{1,0:T(8,128)S(1)}, u32[]{:S(2)}, u32[]{:S(2)}) %collective-permute-start.5) | collective-permute-done | bytes 16416 | tf_op jit(solution)/shard_map/ppermute | solution.py:719
  17.4 0.0 collective-permute-done.6.refs_3_
  17.4 0.0 collective-permute-done.4.refs_1_
  17.4 0.4 %shard_map.119 = (f32[3,8,1024]{2,1,0:T(8,128)S(1)}, f32[32,1,128]{2,1,0:T(1,128)S(1)}) custom-call(f32[16,256]{1,0:T(8,128)S(1)} %get-tuple-element.46.refs_0_, f32[24,256]{1,0:T(8,128)S(1)} %collective-permute-done.4.refs_1_, f32[16,256]{1,0:T(8,128)S(1)} %collective-permute-done.5.refs_2_, f32[16,256]{1,0:T(8,128)S(1)} %collective-permute-done.6.refs_3_, ...), custom_call_target="tpu_custom_call" | custom-call | tf_op jit(solution)/shard_map/pallas_call | solution.py:747
  17.8 13.3 %all_to_all.5.rows_ref = f32[32,1,128]{2,1,0:T(1,128)S(1)} all-to-all(f32[32,1,128]{2,1,0:T(1,128)S(1)} %get-tuple-element.51), channel_id=1, replica_groups=mesh['bx'=8,'by'=4] {'bx','by'}, dimensions={0} | all-to-all | bytes 32768 | tf_op jit(solution)/shard_map/all_to_all | solution.py:755
  31.1 0.8 %shard_map.120 = f32[8,1024]{1,0:T(8,128)} custom-call(f32[32,1,128]{2,1,0:T(1,128)S(1)} %all_to_all.5.rows_ref, f32[3,8,1024]{2,1,0:T(8,128)S(1)} %get-tuple-element.52.basis_ref), custom_call_target="tpu_custom_call" | custom-call | tf_op jit(solution)/shard_map/pallas_call | solution.py:757
  (1 shorter events, 0.0 us)
Async XLA Ops:
  0.6 4.8 %copy-start.6 = (f32[8,1024]{1,0:T(8,128)S(1)}, f32[8,1024]{1,0:T(8,128)}, u32[]{:S(2)}) copy-start(f32[8,1024]{1,0:T(8,128)} %refs_8_.1) | copy-start | bytes 98308
  2.2 4.7 %collective-permute-start = (f32[48,128]{1,0:T(8,128)S(1)}, f32[48,128]{1,0:T(8,128)S(1)}, u32[]{:S(2)}, u32[]{:S(2)}) collective-permute-start(f32[48,128]{1,0:T(8,128)S(1)} %get-tuple-element.28), channel_id=1, source_target_pairs={{0,1},{2,3},{1,0},{3,2},{4,5},{6,7},{5,4},{7,6},{8,9},{10,11},{9,8... | collective-permute-start | bytes 73736 | tf_op jit(solution)/shard_map/ppermute | solution.py:655
  2.8 4.2 %collective-permute-start.1 = (f32[48,128]{1,0:T(8,128)S(1)}, f32[48,128]{1,0:T(8,128)S(1)}, u32[]{:S(2)}, u32[]{:S(2)}) collective-permute-start(f32[48,128]{1,0:T(8,128)S(1)} %get-tuple-element.29), channel_id=1, source_target_pairs={{1,2},{2,1},{0,3},{3,0},{5,6},{6,5},{4,7},{7,4},{9,10},{10,9},{8,1... | collective-permute-start | bytes 73736 | tf_op jit(solution)/shard_map/ppermute | solution.py:656
  5.4 3.9 %copy-start.2 = (f32[8,32,256]{2,1,0:T(8,128)S(1)}, f32[8,32,256]{2,1,0:T(8,128)}, u32[]{:S(2)}) copy-start(f32[8,32,256]{2,1,0:T(8,128)} %v.3) | copy-start | bytes 786436
  5.4 3.9 %copy-start.3 = (f32[8,32,256]{2,1,0:T(8,128)S(1)}, f32[8,32,256]{2,1,0:T(8,128)}, u32[]{:S(2)}) copy-start(f32[8,32,256]{2,1,0:T(8,128)} %y.3) | copy-start | bytes 786436
  5.4 3.9 %copy-start.4 = (f32[8,32,256]{2,1,0:T(8,128)S(1)}, f32[8,32,256]{2,1,0:T(8,128)}, u32[]{:S(2)}) copy-start(f32[8,32,256]{2,1,0:T(8,128)} %u.1) | copy-start | bytes 786436
  5.4 3.9 %copy-start.5 = (f32[8,32,256]{2,1,0:T(8,128)S(1)}, f32[8,32,256]{2,1,0:T(8,128)}, u32[]{:S(2)}) copy-start(f32[8,32,256]{2,1,0:T(8,128)} %x.1) | copy-start | bytes 786436
  7.0 2.4 %copy-start = (f32[8,32,256]{2,1,0:T(8,128)S(1)}, f32[8,32,256]{2,1,0:T(8,128)}, u32[]{:S(2)}) copy-start(f32[8,32,256]{2,1,0:T(8,128)} %t.3) | copy-start | bytes 786436
  7.0 2.4 %copy-start.1 = (f32[8,32,256]{2,1,0:T(8,128)S(1)}, f32[8,32,256]{2,1,0:T(8,128)}, u32[]{:S(2)}) copy-start(f32[8,32,256]{2,1,0:T(8,128)} %s.3) | copy-start | bytes 786436
  7.0 2.4 %copy-start.7 = (s32[32,256]{1,0:T(8,128)S(1)}, s32[32,256]{1,0:T(8,128)}, u32[]{:S(2)}) copy-start(s32[32,256]{1,0:T(8,128)} %depth.3) | copy-start | bytes 98308
  7.0 2.4 %copy-start.8 = (f32[2,32,256]{2,1,0:T(8,128)S(1)}, f32[2,32,256]{2,1,0:T(8,128)}, u32[]{:S(2)}) copy-start(f32[2,32,256]{2,1,0:T(8,128)} %source.1) | copy-start | bytes 196612
  7.5 5.4 %collective-permute-start.2 = (f32[9,8,256]{2,1,0:T(8,128)S(1)}, f32[9,8,256]{2,1,0:T(8,128)S(1)}, u32[]{:S(2)}, u32[]{:S(2)}) collective-permute-start(f32[9,8,256]{2,1,0:T(8,128)S(1)} %get-tuple-element.34.even_out), channel_id=1, source_target_pairs={{0,4},{1,5},{2,6},{3,7},{8,12},{9,13},{10,14},{11,15},{16,20},{17,... | collective-permute-start | bytes 221192 | tf_op jit(solution)/shard_map/ppermute | solution.py:689
  9.2 3.8 %collective-permute-start.3 = (f32[9,8,256]{2,1,0:T(8,128)S(1)}, f32[9,8,256]{2,1,0:T(8,128)S(1)}, u32[]{:S(2)}, u32[]{:S(2)}) collective-permute-start(f32[9,8,256]{2,1,0:T(8,128)S(1)} %get-tuple-element.35.odd_out), channel_id=1, source_target_pairs={{4,8},{5,9},{6,10},{7,11},{12,16},{13,17},{14,18},{15,19},{20,24},... | collective-permute-start | bytes 221192 | tf_op jit(solution)/shard_map/ppermute | solution.py:688
  13.4 4.0 %collective-permute-start.4 = (f32[24,256]{1,0:T(8,128)S(1)}, f32[24,256]{1,0:T(8,128)S(1)}, u32[]{:S(2)}, u32[]{:S(2)}) collective-permute-start(f32[24,256]{1,0:T(8,128)S(1)} %get-tuple-element.47), channel_id=1, source_target_pairs={{0,3},{1,2},{2,1},{3,0},{4,7},{5,6},{6,5},{7,4},{8,11},{9,10},{10,... | collective-permute-start | bytes 73736 | tf_op jit(solution)/shard_map/ppermute | solution.py:719
  13.7 3.7 %collective-permute-start.5 = (f32[16,256]{1,0:T(8,128)S(1)}, f32[16,256]{1,0:T(8,128)S(1)}, u32[]{:S(2)}, u32[]{:S(2)}) collective-permute-start(f32[16,256]{1,0:T(8,128)S(1)} %get-tuple-element.48), channel_id=1, source_target_pairs={{0,2},{1,3},{2,0},{3,1},{4,6},{5,7},{6,4},{7,5},{8,10},{9,11},{10,... | collective-permute-start | bytes 49160 | tf_op jit(solution)/shard_map/ppermute | solution.py:719
  15.1 2.3 %collective-permute-start.6 = (f32[16,256]{1,0:T(8,128)S(1)}, f32[16,256]{1,0:T(8,128)S(1)}, u32[]{:S(2)}, u32[]{:S(2)}) collective-permute-start(f32[16,256]{1,0:T(8,128)S(1)} %get-tuple-element.49), channel_id=1, source_target_pairs={{0,1},{1,0},{2,3},{3,2},{4,5},{5,4},{6,7},{7,6},{8,9},{9,8},{10,11... | collective-permute-start | bytes 49160 | tf_op jit(solution)/shard_map/ppermute | solution.py:719

commit v9 on v8

--- a/solution.py
+++ b/solution.py
@@ -10,7 +10,9 @@
 
 ITERS = 3
 CENTRE = 4.5
-SCALE = 4.5
+SCALE = 4.0
+LEAST = 0.0499
+TINY = 1e-30
 DEEP = ITERS + 1
 SUB = 8
 LANE = 128
@@ -578,13 +580,14 @@
         for i, x in enumerate(direction):
             image[i] = plus(image[i], times(CENTRE, x))
             image[i + 1] = times(SCALE, x)
-        alpha = norm_now / inner(direction, image)
+        bound = jnp.maximum(LEAST * norm_now, TINY)
+        alpha = norm_now / jnp.maximum(inner(direction, image), bound)
         for i, x in enumerate(direction):
             total[i] = plus(total[i], times(alpha, x))
         if step + 1 < ITERS:
             resid = [plus(r, times(-alpha, q)) for r, q in zip(resid + [0.0], image)]
-            norm_next = inner(resid, resid)
-            beta = norm_next / norm_now
+            norm_next = jnp.maximum(inner(resid, resid), 0.0)
+            beta = norm_next / jnp.maximum(norm_now, TINY)
             direction = [plus(r, times(beta, p)) for r, p in zip(resid, direction + [0.0])]
             norm_now = norm_next
     return total

time: 32.2 us -> 32.2 us (level)
  no operation moved by 1% of the time
where the time goes in v9:
time: 32.2 us; the launch traced here: 32 us
  blocking collectives  13.3 us (41%)
  Pallas kernels  8.39 us (26%)
  starting transfers between devices  6.9 us (21%)
  waiting for transfers between devices  2.56 us (8%)
  between operations  0.78 us (2%)
    all_to_all x1, blocking collectives, local(): gathered = lax.all_to_all(row, names, 0, 0, tiled=True)  13.3 us
    ppermute x1, starting transfers between devices, local(): from_odd = lax.ppermute(odd, 'by', across_route(across, 1))  2.64 us
    pallas_call x1, Pallas kernels, local(): call(inner_tile, grid=(1,), in_specs=[whole(a) for a in args], out_specs=...  2.1 us
    ppermute x3, starting transfers between devices, local(): came.append(lax.ppermute(sends[hop], 'by', route))  1.93 us
    ppermute x1, starting transfers between devices, local(): even_in = lax.ppermute(even, names, along_route(along, across, 0))  1.64 us
    pallas_call x1, Pallas kernels, local(): call(pack_edges, grid=(1,), in_specs=[hbm] * 6, out_specs=[whole(pack), w...  1.6 us
    pallas_call x1, Pallas kernels, local(): call(functools.partial(gather_rows, across), grid=(1,), in_specs=[hbm] *...  1.51 us
    ppermute x1, waiting for transfers between devices, local(): even_in = lax.ppermute(even, names, along_route(along, across, 0))  1.43 us
  transfers between devices with their start and end apart: 7, of which 2 were waited for; matrix products, arithmetic and copies ran while one was open for 0% of the time, Pallas kernels for 14%

profile of v9, /device:TPU:0, one launch (start us, length us, event | category | flops | bytes accessed | tf_op | source)
XLA Modules:
  0.0 32.0 jit_solution(5600583146196049985)
XLA Ops:
  0.6 0.0 copy-start.6
  0.6 1.6 %shard_map.112 = (f32[32,128]{1,0:T(8,128)S(1)}, f32[48,128]{1,0:T(8,128)S(1)}, f32[48,128]{1,0:T(8,128)S(1)}) custom-call(f32[8,32,256]{2,1,0:T(8,128)} %t.3, f32[8,32,256]{2,1,0:T(8,128)} %s.3, f32[8,32,256]{2,1,0:T(8,128)} %v.3, f32[8,32,256]{2,1,0:T(8,128)} %y.3, s32[32,256]{1,0:T(8,128)} %depth.3, f32[8,1024]{1,0:T(8,128)} %refs_8_.1), custom_call_target="tpu_custom_call" | custom-call | tf_op jit(solution)/shard_map/pallas_call | solution.py:645
  2.2 0.5 %collective-permute-start = (f32[48,128]{1,0:T(8,128)S(1)}, f32[48,128]{1,0:T(8,128)S(1)}, u32[]{:S(2)}, u32[]{:S(2)}) collective-permute-start(f32[48,128]{1,0:T(8,128)S(1)} %get-tuple-element.28), channel_id=1, source_target_pairs={{0,1},{2,3},{1,0},{3,2},{4,5},{6,7},{5,4},{7,6},{8,9},{10,11},{9,8... | collective-permute-start | bytes 73736 | tf_op jit(solution)/shard_map/ppermute | solution.py:658
  2.8 2.6 %collective-permute-start.1 = (f32[48,128]{1,0:T(8,128)S(1)}, f32[48,128]{1,0:T(8,128)S(1)}, u32[]{:S(2)}, u32[]{:S(2)}) collective-permute-start(f32[48,128]{1,0:T(8,128)S(1)} %get-tuple-element.29), channel_id=1, source_target_pairs={{1,2},{2,1},{0,3},{3,0},{5,6},{6,5},{4,7},{7,4},{9,10},{10,9},{8,1... | collective-permute-start | bytes 73736 | tf_op jit(solution)/shard_map/ppermute | solution.py:659
  5.4 0.0 copy-done.6
  5.4 0.0 copy-start.2
  5.4 0.0 copy-start.3
  5.4 0.0 copy-start.4
  5.4 0.0 copy-start.5
  5.4 1.5 %shard_map.114 = (f32[51,8,256]{2,1,0:T(8,128)S(1)}, f32[9,8,256]{2,1,0:T(8,128)S(1)}, f32[9,8,256]{2,1,0:T(8,128)S(1)}) custom-call(f32[8,32,256]{2,1,0:T(8,128)} %t.3, f32[8,32,256]{2,1,0:T(8,128)} %s.3, f32[8,32,256]{2,1,0:T(8,128)} %u.1, f32[8,32,256]{2,1,0:T(8,128)} %v.3, f32[8,32,256]{2,1,0:T(8,128)} %x.1, f32[8,32,256]{2,1,0:T(8,128)} %y.3, ...), custom_call_target="tpu_custom_call" | custom-call | tf_op jit(solution)/shard_map/pallas_call | solution.py:667
  6.9 0.0 collective-permute-done.from_even
  7.0 0.0 collective-permute-done.1.from_odd
  7.0 0.0 copy-start
  7.0 0.0 copy-start.1
  7.0 0.0 copy-start.7
  7.0 0.0 copy-start.8
  7.0 0.5 %shard_map.115 = (f32[32,256]{1,0:T(8,128)S(1)}, f32[9,8,256]{2,1,0:T(8,128)S(1)}, f32[9,8,256]{2,1,0:T(8,128)S(1)}) custom-call(f32[32,128]{1,0:T(8,128)S(1)} %get-tuple-element.30.first_ref, f32[48,128]{1,0:T(8,128)S(1)} %collective-permute-done.1.from_odd, ...), custom_call_target="tpu_custom_call", output_to_operand_aliasing={{1}: (4, {}), {2}: (5, {})} | custom-call | tf_op jit(solution)/shard_map/pallas_call | solution.py:683
  7.5 1.6 %collective-permute-start.2 = (f32[9,8,256]{2,1,0:T(8,128)S(1)}, f32[9,8,256]{2,1,0:T(8,128)S(1)}, u32[]{:S(2)}, u32[]{:S(2)}) collective-permute-start(f32[9,8,256]{2,1,0:T(8,128)S(1)} %get-tuple-element.34.even_out), channel_id=1, source_target_pairs={{0,4},{1,5},{2,6},{3,7},{8,12},{9,13},{10,14},{11,15},{16,20},{17,... | collective-permute-start | bytes 221192 | tf_op jit(solution)/shard_map/ppermute | solution.py:692
  9.2 0.2 collective-permute-start.3
  9.4 0.0 copy-done.2
  9.4 0.0 copy-done.3
  9.4 0.0 copy-done.4
  9.4 0.0 copy-done.5
  9.4 0.0 copy-done
  9.4 0.0 copy-done.1
  9.4 0.0 copy-done.7
  9.4 0.0 copy-done.8
  9.4 2.1 %shard_map.116 = (f32[8,32,256]{2,1,0:T(8,128)S(1)}, f32[8,32,256]{2,1,0:T(8,128)S(1)}, f32[32,256]{1,0:T(8,128)S(1)}) custom-call(f32[8,32,256]{2,1,0:T(8,128)S(1)} %copy-done, f32[8,32,256]{2,1,0:T(8,128)S(1)} %copy-done.1, f32[8,32,256]{2,1,0:T(8,128)S(1)} %copy-done.4, f32[8,32,256]{2,1,0:T(8,128)S(1)} %copy-done.2, f32[8,32,256]{2,1,0:T(8,128)S(1)} %copy-done.5, ...), custom_call_target="tpu_custom_call" | custom-call | tf_op jit(solution)/shard_map/pallas_call | solution.py:696
  11.5 1.4 %collective-permute-done.2.even_in = f32[9,8,256]{2,1,0:T(8,128)S(1)} collective-permute-done((f32[9,8,256]{2,1,0:T(8,128)S(1)}, f32[9,8,256]{2,1,0:T(8,128)S(1)}, u32[]{:S(2)}, u32[]{:S(2)}) %collective-permute-start.2) | collective-permute-done | bytes 73760 | tf_op jit(solution)/shard_map/ppermute | solution.py:692
  12.9 0.0 collective-permute-done.3.odd_in
  12.9 0.5 %shard_map.117 = (f32[8,8,256]{2,1,0:T(8,128)S(1)}, f32[8,8,256]{2,1,0:T(8,128)S(1)}, f32[16,256]{1,0:T(8,128)S(1)}, f32[16,256]{1,0:T(8,128)S(1)}, f32[16,256]{1,0:T(8,128)S(1)}, /*index=5*/f32[24,256]{1,0:T(8,128)S(1)}) custom-call(f32[9,8,256]{2,1,0:T(8,128)S(1)} %get-tuple-element.34.even_out, f32[9,8,256]{2,1,0:T(8,128)S(1)} %get-tuple-element.35.odd_out, ...), custom_call_target="tpu_custom_call" | custom-call | tf_op jit(solution)/shard_map/pallas_call | solution.py:707
  13.4 0.2 collective-permute-start.4
  13.7 1.4 %collective-permute-start.5 = (f32[16,256]{1,0:T(8,128)S(1)}, f32[16,256]{1,0:T(8,128)S(1)}, u32[]{:S(2)}, u32[]{:S(2)}) collective-permute-start(f32[16,256]{1,0:T(8,128)S(1)} %get-tuple-element.48), channel_id=1, source_target_pairs={{0,2},{1,3},{2,0},{3,1},{4,6},{5,7},{6,4},{7,5},{8,10},{9,11},{10,... | collective-permute-start | bytes 49160 | tf_op jit(solution)/shard_map/ppermute | solution.py:722
  15.1 0.3 collective-permute-start.6
  15.4 0.9 %shard_map.118 = (f32[8,32,256]{2,1,0:T(8,128)}, f32[8,32,256]{2,1,0:T(8,128)}) custom-call(f32[8,8,256]{2,1,0:T(8,128)S(1)} %get-tuple-element.38.fix_t, f32[8,8,256]{2,1,0:T(8,128)S(1)} %get-tuple-element.39.fix_s, f32[8,32,256]{2,1,0:T(8,128)S(1)} %get-tuple-element.40.t_mid, f32[8,32,256]{2,1,0:T(8,128)S(1)} %get-tuple-element.41.s_mid), custom_call_target="tpu_custom_call" | custom-call | tf_op jit(solution)/shard_map/pallas_call | solution.py:725
  16.3 1.1 %collective-permute-done.5.refs_2_ = f32[16,256]{1,0:T(8,128)S(1)} collective-permute-done((f32[16,256]{1,0:T(8,128)S(1)}, f32[16,256]{1,0:T(8,128)S(1)}, u32[]{:S(2)}, u32[]{:S(2)}) %collective-permute-start.5) | collective-permute-done | bytes 16416 | tf_op jit(solution)/shard_map/ppermute | solution.py:722
  17.4 0.0 collective-permute-done.6.refs_3_
  17.4 0.0 collective-permute-done.4.refs_1_
  17.4 0.4 %shard_map.119 = (f32[3,8,1024]{2,1,0:T(8,128)S(1)}, f32[32,1,128]{2,1,0:T(1,128)S(1)}) custom-call(f32[16,256]{1,0:T(8,128)S(1)} %get-tuple-element.46.refs_0_, f32[24,256]{1,0:T(8,128)S(1)} %collective-permute-done.4.refs_1_, f32[16,256]{1,0:T(8,128)S(1)} %collective-permute-done.5.refs_2_, f32[16,256]{1,0:T(8,128)S(1)} %collective-permute-done.6.refs_3_, ...), custom_call_target="tpu_custom_call" | custom-call | tf_op jit(solution)/shard_map/pallas_call | solution.py:750
  17.8 13.3 %all_to_all.5.rows_ref = f32[32,1,128]{2,1,0:T(1,128)S(1)} all-to-all(f32[32,1,128]{2,1,0:T(1,128)S(1)} %get-tuple-element.51), channel_id=1, replica_groups=mesh['bx'=8,'by'=4] {'bx','by'}, dimensions={0} | all-to-all | bytes 32768 | tf_op jit(solution)/shard_map/all_to_all | solution.py:758
  31.1 0.8 %shard_map.120 = f32[8,1024]{1,0:T(8,128)} custom-call(f32[32,1,128]{2,1,0:T(1,128)S(1)} %all_to_all.5.rows_ref, f32[3,8,1024]{2,1,0:T(8,128)S(1)} %get-tuple-element.52.basis_ref), custom_call_target="tpu_custom_call" | custom-call | tf_op jit(solution)/shard_map/pallas_call | solution.py:760
  (1 shorter events, 0.0 us)
Async XLA Ops:
  0.6 4.8 %copy-start.6 = (f32[8,1024]{1,0:T(8,128)S(1)}, f32[8,1024]{1,0:T(8,128)}, u32[]{:S(2)}) copy-start(f32[8,1024]{1,0:T(8,128)} %refs_8_.1) | copy-start | bytes 98308
  2.2 4.7 %collective-permute-start = (f32[48,128]{1,0:T(8,128)S(1)}, f32[48,128]{1,0:T(8,128)S(1)}, u32[]{:S(2)}, u32[]{:S(2)}) collective-permute-start(f32[48,128]{1,0:T(8,128)S(1)} %get-tuple-element.28), channel_id=1, source_target_pairs={{0,1},{2,3},{1,0},{3,2},{4,5},{6,7},{5,4},{7,6},{8,9},{10,11},{9,8... | collective-permute-start | bytes 73736 | tf_op jit(solution)/shard_map/ppermute | solution.py:658
  2.8 4.2 %collective-permute-start.1 = (f32[48,128]{1,0:T(8,128)S(1)}, f32[48,128]{1,0:T(8,128)S(1)}, u32[]{:S(2)}, u32[]{:S(2)}) collective-permute-start(f32[48,128]{1,0:T(8,128)S(1)} %get-tuple-element.29), channel_id=1, source_target_pairs={{1,2},{2,1},{0,3},{3,0},{5,6},{6,5},{4,7},{7,4},{9,10},{10,9},{8,1... | collective-permute-start | bytes 73736 | tf_op jit(solution)/shard_map/ppermute | solution.py:659
  5.4 3.9 %copy-start.2 = (f32[8,32,256]{2,1,0:T(8,128)S(1)}, f32[8,32,256]{2,1,0:T(8,128)}, u32[]{:S(2)}) copy-start(f32[8,32,256]{2,1,0:T(8,128)} %v.3) | copy-start | bytes 786436
  5.4 3.9 %copy-start.3 = (f32[8,32,256]{2,1,0:T(8,128)S(1)}, f32[8,32,256]{2,1,0:T(8,128)}, u32[]{:S(2)}) copy-start(f32[8,32,256]{2,1,0:T(8,128)} %y.3) | copy-start | bytes 786436
  5.4 3.9 %copy-start.4 = (f32[8,32,256]{2,1,0:T(8,128)S(1)}, f32[8,32,256]{2,1,0:T(8,128)}, u32[]{:S(2)}) copy-start(f32[8,32,256]{2,1,0:T(8,128)} %u.1) | copy-start | bytes 786436
  5.4 3.9 %copy-start.5 = (f32[8,32,256]{2,1,0:T(8,128)S(1)}, f32[8,32,256]{2,1,0:T(8,128)}, u32[]{:S(2)}) copy-start(f32[8,32,256]{2,1,0:T(8,128)} %x.1) | copy-start | bytes 786436
  7.0 2.4 %copy-start = (f32[8,32,256]{2,1,0:T(8,128)S(1)}, f32[8,32,256]{2,1,0:T(8,128)}, u32[]{:S(2)}) copy-start(f32[8,32,256]{2,1,0:T(8,128)} %t.3) | copy-start | bytes 786436
  7.0 2.4 %copy-start.1 = (f32[8,32,256]{2,1,0:T(8,128)S(1)}, f32[8,32,256]{2,1,0:T(8,128)}, u32[]{:S(2)}) copy-start(f32[8,32,256]{2,1,0:T(8,128)} %s.3) | copy-start | bytes 786436
  7.0 2.4 %copy-start.7 = (s32[32,256]{1,0:T(8,128)S(1)}, s32[32,256]{1,0:T(8,128)}, u32[]{:S(2)}) copy-start(s32[32,256]{1,0:T(8,128)} %depth.3) | copy-start | bytes 98308
  7.0 2.4 %copy-start.8 = (f32[2,32,256]{2,1,0:T(8,128)S(1)}, f32[2,32,256]{2,1,0:T(8,128)}, u32[]{:S(2)}) copy-start(f32[2,32,256]{2,1,0:T(8,128)} %source.1) | copy-start | bytes 196612
  7.5 5.4 %collective-permute-start.2 = (f32[9,8,256]{2,1,0:T(8,128)S(1)}, f32[9,8,256]{2,1,0:T(8,128)S(1)}, u32[]{:S(2)}, u32[]{:S(2)}) collective-permute-start(f32[9,8,256]{2,1,0:T(8,128)S(1)} %get-tuple-element.34.even_out), channel_id=1, source_target_pairs={{0,4},{1,5},{2,6},{3,7},{8,12},{9,13},{10,14},{11,15},{16,20},{17,... | collective-permute-start | bytes 221192 | tf_op jit(solution)/shard_map/ppermute | solution.py:692
  9.2 3.8 %collective-permute-start.3 = (f32[9,8,256]{2,1,0:T(8,128)S(1)}, f32[9,8,256]{2,1,0:T(8,128)S(1)}, u32[]{:S(2)}, u32[]{:S(2)}) collective-permute-start(f32[9,8,256]{2,1,0:T(8,128)S(1)} %get-tuple-element.35.odd_out), channel_id=1, source_target_pairs={{4,8},{5,9},{6,10},{7,11},{12,16},{13,17},{14,18},{15,19},{20,24},... | collective-permute-start | bytes 221192 | tf_op jit(solution)/shard_map/ppermute | solution.py:691
  13.4 4.0 %collective-permute-start.4 = (f32[24,256]{1,0:T(8,128)S(1)}, f32[24,256]{1,0:T(8,128)S(1)}, u32[]{:S(2)}, u32[]{:S(2)}) collective-permute-start(f32[24,256]{1,0:T(8,128)S(1)} %get-tuple-element.47), channel_id=1, source_target_pairs={{0,3},{1,2},{2,1},{3,0},{4,7},{5,6},{6,5},{7,4},{8,11},{9,10},{10,... | collective-permute-start | bytes 73736 | tf_op jit(solution)/shard_map/ppermute | solution.py:722
  13.7 3.7 %collective-permute-start.5 = (f32[16,256]{1,0:T(8,128)S(1)}, f32[16,256]{1,0:T(8,128)S(1)}, u32[]{:S(2)}, u32[]{:S(2)}) collective-permute-start(f32[16,256]{1,0:T(8,128)S(1)} %get-tuple-element.48), channel_id=1, source_target_pairs={{0,2},{1,3},{2,0},{3,1},{4,6},{5,7},{6,4},{7,5},{8,10},{9,11},{10,... | collective-permute-start | bytes 49160 | tf_op jit(solution)/shard_map/ppermute | solution.py:722
  15.1 2.3 %collective-permute-start.6 = (f32[16,256]{1,0:T(8,128)S(1)}, f32[16,256]{1,0:T(8,128)S(1)}, u32[]{:S(2)}, u32[]{:S(2)}) collective-permute-start(f32[16,256]{1,0:T(8,128)S(1)} %get-tuple-element.49), channel_id=1, source_target_pairs={{0,1},{1,0},{2,3},{3,2},{4,5},{5,4},{6,7},{7,6},{8,9},{9,8},{10,11... | collective-permute-start | bytes 49160 | tf_op jit(solution)/shard_map/ppermute | solution.py:722

commit v10 on v9

--- a/solution.py
+++ b/solution.py
@@ -543,8 +543,10 @@
     place = iota((1, LANE), 1)
     row = jnp.zeros((1, LANE), jnp.float32)
     for k, (i, j) in enumerate(PAIRS):
-        part = jnp.sum(own[i] * own[j], axis=0, keepdims=True)
-        row = jnp.where(place == k, jnp.sum(part, axis=1, keepdims=True), row)
+        part = own[i] * own[j]
+        part = sum(part[:, c : c + LANE] for c in range(0, columns, LANE))
+        part = jnp.sum(jnp.sum(part, axis=1, keepdims=True), axis=0, keepdims=True)
+        row = jnp.where(place == k, part, row)
     row_ref[...] = jnp.broadcast_to(row[None], row_ref.shape)
 
 

time: 32.2 us -> 32.2 us (level)
  no operation moved by 1% of the time
where the time goes in v10:
time: 32.2 us; the launch traced here: 32 us
  blocking collectives  13.3 us (41%)
  Pallas kernels  8.39 us (26%)
  starting transfers between devices  6.9 us (21%)
  waiting for transfers between devices  2.56 us (8%)
  between operations  0.79 us (2%)
    all_to_all x1, blocking collectives, local(): gathered = lax.all_to_all(row, names, 0, 0, tiled=True)  13.3 us
    ppermute x1, starting transfers between devices, local(): from_odd = lax.ppermute(odd, 'by', across_route(across, 1))  2.64 us
    pallas_call x1, Pallas kernels, local(): call(inner_tile, grid=(1,), in_specs=[whole(a) for a in args], out_specs=...  2.1 us
    ppermute x3, starting transfers between devices, local(): came.append(lax.ppermute(sends[hop], 'by', route))  1.93 us
    ppermute x1, starting transfers between devices, local(): even_in = lax.ppermute(even, names, along_route(along, across, 0))  1.64 us
    pallas_call x1, Pallas kernels, local(): call(pack_edges, grid=(1,), in_specs=[hbm] * 6, out_specs=[whole(pack), w...  1.6 us
    pallas_call x1, Pallas kernels, local(): call(functools.partial(gather_rows, across), grid=(1,), in_specs=[hbm] *...  1.51 us
    ppermute x1, waiting for transfers between devices, local(): even_in = lax.ppermute(even, names, along_route(along, across, 0))  1.43 us
  transfers between devices with their start and end apart: 7, of which 2 were waited for; matrix products, arithmetic and copies ran while one was open for 0% of the time, Pallas kernels for 14%

profile of v10, /device:TPU:0, one launch (start us, length us, event | category | flops | bytes accessed | tf_op | source)
XLA Modules:
  0.0 32.0 jit_solution(794311686078114212)
XLA Ops:
  0.6 0.0 copy-start.6
  0.6 1.6 %shard_map.112 = (f32[32,128]{1,0:T(8,128)S(1)}, f32[48,128]{1,0:T(8,128)S(1)}, f32[48,128]{1,0:T(8,128)S(1)}) custom-call(f32[8,32,256]{2,1,0:T(8,128)} %t.3, f32[8,32,256]{2,1,0:T(8,128)} %s.3, f32[8,32,256]{2,1,0:T(8,128)} %v.3, f32[8,32,256]{2,1,0:T(8,128)} %y.3, s32[32,256]{1,0:T(8,128)} %depth.3, f32[8,1024]{1,0:T(8,128)} %refs_8_.1), custom_call_target="tpu_custom_call" | custom-call | tf_op jit(solution)/shard_map/pallas_call | solution.py:647
  2.2 0.5 %collective-permute-start = (f32[48,128]{1,0:T(8,128)S(1)}, f32[48,128]{1,0:T(8,128)S(1)}, u32[]{:S(2)}, u32[]{:S(2)}) collective-permute-start(f32[48,128]{1,0:T(8,128)S(1)} %get-tuple-element.28), channel_id=1, source_target_pairs={{0,1},{2,3},{1,0},{3,2},{4,5},{6,7},{5,4},{7,6},{8,9},{10,11},{9,8... | collective-permute-start | bytes 73736 | tf_op jit(solution)/shard_map/ppermute | solution.py:660
  2.8 2.6 %collective-permute-start.1 = (f32[48,128]{1,0:T(8,128)S(1)}, f32[48,128]{1,0:T(8,128)S(1)}, u32[]{:S(2)}, u32[]{:S(2)}) collective-permute-start(f32[48,128]{1,0:T(8,128)S(1)} %get-tuple-element.29), channel_id=1, source_target_pairs={{1,2},{2,1},{0,3},{3,0},{5,6},{6,5},{4,7},{7,4},{9,10},{10,9},{8,1... | collective-permute-start | bytes 73736 | tf_op jit(solution)/shard_map/ppermute | solution.py:661
  5.4 0.0 copy-done.6
  5.4 0.0 copy-start.2
  5.4 0.0 copy-start.3
  5.4 0.0 copy-start.4
  5.4 0.0 copy-start.5
  5.4 1.5 %shard_map.114 = (f32[51,8,256]{2,1,0:T(8,128)S(1)}, f32[9,8,256]{2,1,0:T(8,128)S(1)}, f32[9,8,256]{2,1,0:T(8,128)S(1)}) custom-call(f32[8,32,256]{2,1,0:T(8,128)} %t.3, f32[8,32,256]{2,1,0:T(8,128)} %s.3, f32[8,32,256]{2,1,0:T(8,128)} %u.1, f32[8,32,256]{2,1,0:T(8,128)} %v.3, f32[8,32,256]{2,1,0:T(8,128)} %x.1, f32[8,32,256]{2,1,0:T(8,128)} %y.3, ...), custom_call_target="tpu_custom_call" | custom-call | tf_op jit(solution)/shard_map/pallas_call | solution.py:669
  6.9 0.0 collective-permute-done.from_even
  7.0 0.0 collective-permute-done.1.from_odd
  7.0 0.0 copy-start
  7.0 0.0 copy-start.1
  7.0 0.0 copy-start.7
  7.0 0.0 copy-start.8
  7.0 0.5 %shard_map.115 = (f32[32,256]{1,0:T(8,128)S(1)}, f32[9,8,256]{2,1,0:T(8,128)S(1)}, f32[9,8,256]{2,1,0:T(8,128)S(1)}) custom-call(f32[32,128]{1,0:T(8,128)S(1)} %get-tuple-element.30.first_ref, f32[48,128]{1,0:T(8,128)S(1)} %collective-permute-done.1.from_odd, ...), custom_call_target="tpu_custom_call", output_to_operand_aliasing={{1}: (4, {}), {2}: (5, {})} | custom-call | tf_op jit(solution)/shard_map/pallas_call | solution.py:685
  7.5 1.6 %collective-permute-start.2 = (f32[9,8,256]{2,1,0:T(8,128)S(1)}, f32[9,8,256]{2,1,0:T(8,128)S(1)}, u32[]{:S(2)}, u32[]{:S(2)}) collective-permute-start(f32[9,8,256]{2,1,0:T(8,128)S(1)} %get-tuple-element.34.even_out), channel_id=1, source_target_pairs={{0,4},{1,5},{2,6},{3,7},{8,12},{9,13},{10,14},{11,15},{16,20},{17,... | collective-permute-start | bytes 221192 | tf_op jit(solution)/shard_map/ppermute | solution.py:694
  9.2 0.2 collective-permute-start.3
  9.4 0.0 copy-done.2
  9.4 0.0 copy-done.3
  9.4 0.0 copy-done.4
  9.4 0.0 copy-done.5
  9.4 0.0 copy-done
  9.4 0.0 copy-done.1
  9.4 0.0 copy-done.7
  9.4 0.0 copy-done.8
  9.4 2.1 %shard_map.116 = (f32[8,32,256]{2,1,0:T(8,128)S(1)}, f32[8,32,256]{2,1,0:T(8,128)S(1)}, f32[32,256]{1,0:T(8,128)S(1)}) custom-call(f32[8,32,256]{2,1,0:T(8,128)S(1)} %copy-done, f32[8,32,256]{2,1,0:T(8,128)S(1)} %copy-done.1, f32[8,32,256]{2,1,0:T(8,128)S(1)} %copy-done.4, f32[8,32,256]{2,1,0:T(8,128)S(1)} %copy-done.2, f32[8,32,256]{2,1,0:T(8,128)S(1)} %copy-done.5, ...), custom_call_target="tpu_custom_call" | custom-call | tf_op jit(solution)/shard_map/pallas_call | solution.py:698
  11.5 1.4 %collective-permute-done.2.even_in = f32[9,8,256]{2,1,0:T(8,128)S(1)} collective-permute-done((f32[9,8,256]{2,1,0:T(8,128)S(1)}, f32[9,8,256]{2,1,0:T(8,128)S(1)}, u32[]{:S(2)}, u32[]{:S(2)}) %collective-permute-start.2) | collective-permute-done | bytes 73760 | tf_op jit(solution)/shard_map/ppermute | solution.py:694
  12.9 0.0 collective-permute-done.3.odd_in
  12.9 0.5 %shard_map.117 = (f32[8,8,256]{2,1,0:T(8,128)S(1)}, f32[8,8,256]{2,1,0:T(8,128)S(1)}, f32[16,256]{1,0:T(8,128)S(1)}, f32[16,256]{1,0:T(8,128)S(1)}, f32[16,256]{1,0:T(8,128)S(1)}, /*index=5*/f32[24,256]{1,0:T(8,128)S(1)}) custom-call(f32[9,8,256]{2,1,0:T(8,128)S(1)} %get-tuple-element.34.even_out, f32[9,8,256]{2,1,0:T(8,128)S(1)} %get-tuple-element.35.odd_out, ...), custom_call_target="tpu_custom_call" | custom-call | tf_op jit(solution)/shard_map/pallas_call | solution.py:709
  13.4 0.2 collective-permute-start.4
  13.7 1.4 %collective-permute-start.5 = (f32[16,256]{1,0:T(8,128)S(1)}, f32[16,256]{1,0:T(8,128)S(1)}, u32[]{:S(2)}, u32[]{:S(2)}) collective-permute-start(f32[16,256]{1,0:T(8,128)S(1)} %get-tuple-element.48), channel_id=1, source_target_pairs={{0,2},{1,3},{2,0},{3,1},{4,6},{5,7},{6,4},{7,5},{8,10},{9,11},{10,... | collective-permute-start | bytes 49160 | tf_op jit(solution)/shard_map/ppermute | solution.py:724
  15.1 0.3 collective-permute-start.6
  15.4 0.9 %shard_map.118 = (f32[8,32,256]{2,1,0:T(8,128)}, f32[8,32,256]{2,1,0:T(8,128)}) custom-call(f32[8,8,256]{2,1,0:T(8,128)S(1)} %get-tuple-element.38.fix_t, f32[8,8,256]{2,1,0:T(8,128)S(1)} %get-tuple-element.39.fix_s, f32[8,32,256]{2,1,0:T(8,128)S(1)} %get-tuple-element.40.t_mid, f32[8,32,256]{2,1,0:T(8,128)S(1)} %get-tuple-element.41.s_mid), custom_call_target="tpu_custom_call" | custom-call | tf_op jit(solution)/shard_map/pallas_call | solution.py:727
  16.3 1.1 %collective-permute-done.5.refs_2_ = f32[16,256]{1,0:T(8,128)S(1)} collective-permute-done((f32[16,256]{1,0:T(8,128)S(1)}, f32[16,256]{1,0:T(8,128)S(1)}, u32[]{:S(2)}, u32[]{:S(2)}) %collective-permute-start.5) | collective-permute-done | bytes 16416 | tf_op jit(solution)/shard_map/ppermute | solution.py:724
  17.4 0.0 collective-permute-done.6.refs_3_
  17.4 0.0 collective-permute-done.4.refs_1_
  17.4 0.4 %shard_map.119 = (f32[3,8,1024]{2,1,0:T(8,128)S(1)}, f32[32,1,128]{2,1,0:T(1,128)S(1)}) custom-call(f32[16,256]{1,0:T(8,128)S(1)} %get-tuple-element.46.refs_0_, f32[24,256]{1,0:T(8,128)S(1)} %collective-permute-done.4.refs_1_, f32[16,256]{1,0:T(8,128)S(1)} %collective-permute-done.5.refs_2_, f32[16,256]{1,0:T(8,128)S(1)} %collective-permute-done.6.refs_3_, ...), custom_call_target="tpu_custom_call" | custom-call | tf_op jit(solution)/shard_map/pallas_call | solution.py:752
  17.9 13.3 %all_to_all.5.rows_ref = f32[32,1,128]{2,1,0:T(1,128)S(1)} all-to-all(f32[32,1,128]{2,1,0:T(1,128)S(1)} %get-tuple-element.51), channel_id=1, replica_groups=mesh['bx'=8,'by'=4] {'bx','by'}, dimensions={0} | all-to-all | bytes 32768 | tf_op jit(solution)/shard_map/all_to_all | solution.py:760
  31.1 0.8 %shard_map.120 = f32[8,1024]{1,0:T(8,128)} custom-call(f32[32,1,128]{2,1,0:T(1,128)S(1)} %all_to_all.5.rows_ref, f32[3,8,1024]{2,1,0:T(8,128)S(1)} %get-tuple-element.52.basis_ref), custom_call_target="tpu_custom_call" | custom-call | tf_op jit(solution)/shard_map/pallas_call | solution.py:762
  (1 shorter events, 0.0 us)
Async XLA Ops:
  0.6 4.8 %copy-start.6 = (f32[8,1024]{1,0:T(8,128)S(1)}, f32[8,1024]{1,0:T(8,128)}, u32[]{:S(2)}) copy-start(f32[8,1024]{1,0:T(8,128)} %refs_8_.1) | copy-start | bytes 98308
  2.2 4.7 %collective-permute-start = (f32[48,128]{1,0:T(8,128)S(1)}, f32[48,128]{1,0:T(8,128)S(1)}, u32[]{:S(2)}, u32[]{:S(2)}) collective-permute-start(f32[48,128]{1,0:T(8,128)S(1)} %get-tuple-element.28), channel_id=1, source_target_pairs={{0,1},{2,3},{1,0},{3,2},{4,5},{6,7},{5,4},{7,6},{8,9},{10,11},{9,8... | collective-permute-start | bytes 73736 | tf_op jit(solution)/shard_map/ppermute | solution.py:660
  2.8 4.2 %collective-permute-start.1 = (f32[48,128]{1,0:T(8,128)S(1)}, f32[48,128]{1,0:T(8,128)S(1)}, u32[]{:S(2)}, u32[]{:S(2)}) collective-permute-start(f32[48,128]{1,0:T(8,128)S(1)} %get-tuple-element.29), channel_id=1, source_target_pairs={{1,2},{2,1},{0,3},{3,0},{5,6},{6,5},{4,7},{7,4},{9,10},{10,9},{8,1... | collective-permute-start | bytes 73736 | tf_op jit(solution)/shard_map/ppermute | solution.py:661
  5.4 3.9 %copy-start.2 = (f32[8,32,256]{2,1,0:T(8,128)S(1)}, f32[8,32,256]{2,1,0:T(8,128)}, u32[]{:S(2)}) copy-start(f32[8,32,256]{2,1,0:T(8,128)} %v.3) | copy-start | bytes 786436
  5.4 3.9 %copy-start.3 = (f32[8,32,256]{2,1,0:T(8,128)S(1)}, f32[8,32,256]{2,1,0:T(8,128)}, u32[]{:S(2)}) copy-start(f32[8,32,256]{2,1,0:T(8,128)} %y.3) | copy-start | bytes 786436
  5.4 3.9 %copy-start.4 = (f32[8,32,256]{2,1,0:T(8,128)S(1)}, f32[8,32,256]{2,1,0:T(8,128)}, u32[]{:S(2)}) copy-start(f32[8,32,256]{2,1,0:T(8,128)} %u.1) | copy-start | bytes 786436
  5.4 3.9 %copy-start.5 = (f32[8,32,256]{2,1,0:T(8,128)S(1)}, f32[8,32,256]{2,1,0:T(8,128)}, u32[]{:S(2)}) copy-start(f32[8,32,256]{2,1,0:T(8,128)} %x.1) | copy-start | bytes 786436
  7.0 2.4 %copy-start = (f32[8,32,256]{2,1,0:T(8,128)S(1)}, f32[8,32,256]{2,1,0:T(8,128)}, u32[]{:S(2)}) copy-start(f32[8,32,256]{2,1,0:T(8,128)} %t.3) | copy-start | bytes 786436
  7.0 2.4 %copy-start.1 = (f32[8,32,256]{2,1,0:T(8,128)S(1)}, f32[8,32,256]{2,1,0:T(8,128)}, u32[]{:S(2)}) copy-start(f32[8,32,256]{2,1,0:T(8,128)} %s.3) | copy-start | bytes 786436
  7.0 2.4 %copy-start.7 = (s32[32,256]{1,0:T(8,128)S(1)}, s32[32,256]{1,0:T(8,128)}, u32[]{:S(2)}) copy-start(s32[32,256]{1,0:T(8,128)} %depth.3) | copy-start | bytes 98308
  7.0 2.4 %copy-start.8 = (f32[2,32,256]{2,1,0:T(8,128)S(1)}, f32[2,32,256]{2,1,0:T(8,128)}, u32[]{:S(2)}) copy-start(f32[2,32,256]{2,1,0:T(8,128)} %source.1) | copy-start | bytes 196612
  7.5 5.4 %collective-permute-start.2 = (f32[9,8,256]{2,1,0:T(8,128)S(1)}, f32[9,8,256]{2,1,0:T(8,128)S(1)}, u32[]{:S(2)}, u32[]{:S(2)}) collective-permute-start(f32[9,8,256]{2,1,0:T(8,128)S(1)} %get-tuple-element.34.even_out), channel_id=1, source_target_pairs={{0,4},{1,5},{2,6},{3,7},{8,12},{9,13},{10,14},{11,15},{16,20},{17,... | collective-permute-start | bytes 221192 | tf_op jit(solution)/shard_map/ppermute | solution.py:694
  9.2 3.8 %collective-permute-start.3 = (f32[9,8,256]{2,1,0:T(8,128)S(1)}, f32[9,8,256]{2,1,0:T(8,128)S(1)}, u32[]{:S(2)}, u32[]{:S(2)}) collective-permute-start(f32[9,8,256]{2,1,0:T(8,128)S(1)} %get-tuple-element.35.odd_out), channel_id=1, source_target_pairs={{4,8},{5,9},{6,10},{7,11},{12,16},{13,17},{14,18},{15,19},{20,24},... | collective-permute-start | bytes 221192 | tf_op jit(solution)/shard_map/ppermute | solution.py:693
  13.4 4.0 %collective-permute-start.4 = (f32[24,256]{1,0:T(8,128)S(1)}, f32[24,256]{1,0:T(8,128)S(1)}, u32[]{:S(2)}, u32[]{:S(2)}) collective-permute-start(f32[24,256]{1,0:T(8,128)S(1)} %get-tuple-element.47), channel_id=1, source_target_pairs={{0,3},{1,2},{2,1},{3,0},{4,7},{5,6},{6,5},{7,4},{8,11},{9,10},{10,... | collective-permute-start | bytes 73736 | tf_op jit(solution)/shard_map/ppermute | solution.py:724
  13.7 3.7 %collective-permute-start.5 = (f32[16,256]{1,0:T(8,128)S(1)}, f32[16,256]{1,0:T(8,128)S(1)}, u32[]{:S(2)}, u32[]{:S(2)}) collective-permute-start(f32[16,256]{1,0:T(8,128)S(1)} %get-tuple-element.48), channel_id=1, source_target_pairs={{0,2},{1,3},{2,0},{3,1},{4,6},{5,7},{6,4},{7,5},{8,10},{9,11},{10,... | collective-permute-start | bytes 49160 | tf_op jit(solution)/shard_map/ppermute | solution.py:724
  15.1 2.3 %collective-permute-start.6 = (f32[16,256]{1,0:T(8,128)S(1)}, f32[16,256]{1,0:T(8,128)S(1)}, u32[]{:S(2)}, u32[]{:S(2)}) collective-permute-start(f32[16,256]{1,0:T(8,128)S(1)} %get-tuple-element.49), channel_id=1, source_target_pairs={{0,1},{1,0},{2,3},{3,2},{4,5},{5,4},{6,7},{7,6},{8,9},{9,8},{10,11... | collective-permute-start | bytes 49160 | tf_op jit(solution)/shard_map/ppermute | solution.py:724
